TPU v7x, 128 devices: a whole 4x4x4 slice. The times are simulated.
128 devices in a mesh: ctx: 32 (over z, x, core), tp: 4 (over y).
Axes of the slice: x: 4, y: 4, z: 4, core: 2. Of those that a mesh axis runs over, the one named last changes fastest.
Arguments:
- queries: bfloat16 [32768, 4096], P(('ctx', 'tp')), may hold values from -40 to 40
- keys_in: bfloat16 [32768, 1024], P(('ctx', 'tp')), may hold values from -4 to 4
- values_in: bfloat16 [32768, 1024], P(('ctx', 'tp')), may hold values from -6 to 6
- grad_output: bfloat16 [32768, 4096], P(('ctx', 'tp')), may hold values from -6 to 6
- beacon_keys: bfloat16 [4096, 1024], P('ctx', 'tp'), may hold values from -6 to 6
- beacon_values: bfloat16 [4096, 1024], P('ctx', 'tp'), may hold values from -6 to 6
- read_blocks: int32 [32, 4], P('ctx'), may hold values from 0 to 30, as said below
- read_counts: int32 [32], P('ctx'), may hold values from 0 to 4, as said below
Outputs:
- attn_out: bfloat16 [32768, 4096], P(('ctx', 'tp'))
- grad_queries: bfloat16 [32768, 4096], P(('ctx', 'tp'))
- grad_keys: bfloat16 [32768, 1024], P(('ctx', 'tp'))
- grad_values: bfloat16 [32768, 1024], P(('ctx', 'tp'))
- grad_beacon_keys: bfloat16 [4096, 1024], P('ctx', 'tp')
- grad_beacon_values: bfloat16 [4096, 1024], P('ctx', 'tp')
Inputs may be any that keep to these rules, and one draw needn't show every extreme that they name: `read_blocks`: row s lists distinct blocks of earlier segments in its first read_counts[s] slots, block s - 1 first; unused slots hold 0. The last segment reads block 15 in its second slot. read_counts[s] is at most min(s, 4); segment 0 reads nothing and the last segment uses all 4 slots.
All inputs are finite; a program needn't handle non-finite values.
Results may differ from a plain program's by a relative error of at most 0.01.
Values may be sent and summed in bfloat16 or wider, within the bound.
No kernel may reach another device: no remote copies, remote signals or barrier semaphores. Data moves between devices by JAX's collectives and lax.ppermute only.
A program may use at most 128 MiB of HBM per device.

v0:
```python
import jax
import jax.numpy as jnp
from jax import lax
from jax.sharding import PartitionSpec as P

HD = 128


def head_grads(query_rows, key_rows, value_rows, grad_rows, allowed, score_scale):
    scores = jnp.dot(query_rows, key_rows.T, preferred_element_type=jnp.float32) * score_scale
    scores = jnp.where(allowed, scores, -1e30)
    row_max = jnp.max(scores, axis=1, keepdims=True)
    weights = jnp.exp(scores - row_max)
    prob_full = weights / jnp.sum(weights, axis=1, keepdims=True)
    prob_half = prob_full.astype(jnp.bfloat16)
    output = jnp.dot(prob_half, value_rows, preferred_element_type=jnp.float32).astype(jnp.bfloat16)
    grad_prob = jnp.dot(grad_rows, value_rows.T, preferred_element_type=jnp.float32)
    row_delta = jnp.sum(
        grad_rows.astype(jnp.float32) * output.astype(jnp.float32), axis=1, keepdims=True
    )
    dscores = (prob_full * (grad_prob - row_delta) * score_scale).astype(jnp.bfloat16)
    grad_query = jnp.dot(dscores, key_rows, preferred_element_type=jnp.float32).astype(jnp.bfloat16)
    grad_key = jnp.dot(dscores.T, query_rows, preferred_element_type=jnp.float32)
    grad_value = jnp.dot(prob_half.T, grad_rows, preferred_element_type=jnp.float32)
    return (output, grad_query, grad_key, grad_value)


def shards(
    queries, keys_in, values_in, grad_output, beacon_keys, beacon_values, read_blocks, read_counts
):
    seg_q, seg_k, seg_v, seg_g = (
        lax.all_to_all(queries, "tp", split_axis=1, concat_axis=0, tiled=True),
        lax.all_to_all(keys_in, "tp", split_axis=1, concat_axis=0, tiled=True),
        lax.all_to_all(values_in, "tp", split_axis=1, concat_axis=0, tiled=True),
        lax.all_to_all(grad_output, "tp", split_axis=1, concat_axis=0, tiled=True),
    )
    all_k, all_v = (
        lax.all_gather(beacon_keys, "ctx", axis=0, tiled=True),
        lax.all_gather(beacon_values, "ctx", axis=0, tiled=True),
    )
    seg_len = seg_q.shape[0]
    head_count = seg_q.shape[1] // HD
    kv_heads = seg_k.shape[1] // HD
    group_size = head_count // kv_heads
    col_width = seg_k.shape[1]
    block_rows = beacon_keys.shape[0]
    owners = lax.axis_size("ctx")
    read_row = read_blocks[0]
    read_count = read_counts[0]
    read_slots = read_row.shape[0]
    beacon_rows = read_slots * block_rows
    score_scale = HD ** (-0.5)
    positions = jnp.arange(seg_len, dtype=jnp.int32)
    causal = positions[None, :] <= positions[:, None]
    slot_ok = jnp.arange(read_slots, dtype=jnp.int32) < read_count
    valid_keys = jnp.repeat(slot_ok, block_rows)
    allowed = jnp.concatenate(
        [causal, jnp.broadcast_to(valid_keys[None, :], (seg_len, beacon_rows))], axis=1
    )
    chosen_k = jnp.take(all_k.reshape(owners, block_rows, col_width), read_row, axis=0).reshape(
        beacon_rows, col_width
    )
    chosen_v = jnp.take(all_v.reshape(owners, block_rows, col_width), read_row, axis=0).reshape(
        beacon_rows, col_width
    )
    query_heads = seg_q.reshape(seg_len, head_count, HD).transpose(1, 0, 2)
    grad_heads = seg_g.reshape(seg_len, head_count, HD).transpose(1, 0, 2)
    key_heads = (
        jnp.concatenate([seg_k, chosen_k], axis=0)
        .reshape(seg_len + beacon_rows, kv_heads, HD)
        .transpose(1, 0, 2)
    )
    value_heads = (
        jnp.concatenate([seg_v, chosen_v], axis=0)
        .reshape(seg_len + beacon_rows, kv_heads, HD)
        .transpose(1, 0, 2)
    )

    def per_head(head_index):
        shared = head_index // group_size
        return head_grads(
            query_heads[head_index],
            key_heads[shared],
            value_heads[shared],
            grad_heads[head_index],
            allowed,
            score_scale,
        )

    outputs, grad_query, grad_key, grad_value = lax.map(
        per_head, jnp.arange(head_count, dtype=jnp.int32)
    )
    grad_key = jnp.sum(grad_key.reshape(kv_heads, group_size, seg_len + beacon_rows, HD), axis=1)
    grad_value = jnp.sum(
        grad_value.reshape(kv_heads, group_size, seg_len + beacon_rows, HD), axis=1
    )
    local_k = (
        grad_key[:, :seg_len].transpose(1, 0, 2).reshape(seg_len, col_width).astype(jnp.bfloat16)
    )
    local_v = (
        grad_value[:, :seg_len].transpose(1, 0, 2).reshape(seg_len, col_width).astype(jnp.bfloat16)
    )
    part_k = grad_key[:, seg_len:].transpose(1, 0, 2).reshape(read_slots, block_rows, col_width)
    part_v = grad_value[:, seg_len:].transpose(1, 0, 2).reshape(read_slots, block_rows, col_width)
    owner_ids = jnp.arange(owners, dtype=jnp.int32)
    onehot = ((read_row[None, :] == owner_ids[:, None]) & slot_ok[None, :]).astype(jnp.float32)
    dense_k = jnp.einsum("bj,jrc->brc", onehot, part_k, precision=lax.Precision.HIGHEST)
    dense_v = jnp.einsum("bj,jrc->brc", onehot, part_v, precision=lax.Precision.HIGHEST)
    summed_k, summed_v = (
        lax.psum_scatter(
            dense_k.astype(jnp.bfloat16), "ctx", scatter_dimension=0, tiled=True
        ).astype(jnp.float32),
        lax.psum_scatter(
            dense_v.astype(jnp.bfloat16), "ctx", scatter_dimension=0, tiled=True
        ).astype(jnp.float32),
    )
    own_k = summed_k[0]
    own_v = summed_v[0]
    seg_out = outputs.transpose(1, 0, 2).reshape(seg_len, head_count * HD)
    seg_gq = grad_query.transpose(1, 0, 2).reshape(seg_len, head_count * HD)
    tok_out, tok_gq, tok_gk, tok_gv = (
        lax.all_to_all(seg_out, "tp", split_axis=0, concat_axis=1, tiled=True),
        lax.all_to_all(seg_gq, "tp", split_axis=0, concat_axis=1, tiled=True),
        lax.all_to_all(local_k, "tp", split_axis=0, concat_axis=1, tiled=True),
        lax.all_to_all(local_v, "tp", split_axis=0, concat_axis=1, tiled=True),
    )
    return (tok_out, tok_gq, tok_gk, tok_gv, own_k.astype(jnp.bfloat16), own_v.astype(jnp.bfloat16))


def solution(mesh):
    in_specs = (
        P(("ctx", "tp"), None),
        P(("ctx", "tp"), None),
        P(("ctx", "tp"), None),
        P(("ctx", "tp"), None),
        P("ctx", "tp"),
        P("ctx", "tp"),
        P("ctx", None),
        P("ctx"),
    )
    out_specs = (
        P(("ctx", "tp"), None),
        P(("ctx", "tp"), None),
        P(("ctx", "tp"), None),
        P(("ctx", "tp"), None),
        P("ctx", "tp"),
        P("ctx", "tp"),
    )
    return jax.shard_map(shards, mesh=mesh, in_specs=in_specs, out_specs=out_specs, check_vma=False)
```

profile of v0, /device:TPU:0, one launch (start us, length us, event | category | flops | bytes accessed | tf_op | source)
XLA Modules:
  0.0 490.3 jit_solution(4537114664854206258)
XLA Ops:
  10.7 4.6 all-to-all-start.1
  16.1 8.6 %all-to-all-done.1 = bf16[256,4,256]{2,0,1:T(8,128)(2,1)S(1)} async-done(((bf16[256,4,256]{2,0,1:T(8,128)(2,1)}), bf16[256,4,256]{2,0,1:T(8,128)(2,1)S(1)}, u32[]{:S(2)}, u32[]{:S(2)}) %all-to-all-start.1) | async-done | bytes 524320 | tf_op jit(solution)/shard_map/all_to_all | solution.py:33
  29.8 6.8 %all-to-all-done.2 = bf16[256,4,256]{2,0,1:T(8,128)(2,1)S(1)} async-done(((bf16[256,4,256]{2,0,1:T(8,128)(2,1)}), bf16[256,4,256]{2,0,1:T(8,128)(2,1)S(1)}, u32[]{:S(2)}, u32[]{:S(2)}) %all-to-all-start.2) | async-done | bytes 524320 | tf_op jit(solution)/shard_map/all_to_all | solution.py:34
  36.5 4.6 all-to-all-start
  44.3 20.9 %all-to-all-done = bf16[256,4,1024]{2,0,1:T(8,128)(2,1)} async-done(((bf16[256,4,1024]{2,0,1:T(8,128)(2,1)}), bf16[256,4,1024]{2,0,1:T(8,128)(2,1)}, u32[]{:S(2)}, u32[]{:S(2)}) %all-to-all-start) | async-done | bytes 2097184 | tf_op jit(solution)/shard_map/all_to_all | solution.py:32
  65.2 4.6 all-to-all-start.3
  75.2 17.9 %all-to-all-done.3 = bf16[256,4,1024]{0,2,1:T(8,128)(2,1)} async-done(((bf16[256,4,1024]{0,2,1:T(8,128)(2,1)}), bf16[256,4,1024]{0,2,1:T(8,128)(2,1)}, u32[]{:S(2)}, u32[]{:S(2)}) %all-to-all-start.3) | async-done | bytes 2097184 | tf_op jit(solution)/shard_map/all_to_all | solution.py:35
  93.1 4.0 copy.75
  100.7 4.1 copy.80
  111.1 5.9 %maximum_bitcast_fusion = bf16[2,1536,128]{2,0,1:T(2,128)(2,1)S(1)} fusion(bf16[512,2,128]{2,1,0:T(2,128)(2,1)S(1)} %concatenate.20, bf16[1024,2,128]{2,1,0:T(2,128)(2,1)S(1)} %concatenate.19), kind=kLoop, calls=%fused_computation.51 | loop fusion | flops 393216 | bytes 1572864 | tf_op jit(solution)/shard_map/transpose | solution.py:71
  117.2 5.9 %maximum_bitcast_fusion.1 = bf16[2,1536,128]{2,0,1:T(2,128)(2,1)S(1)} fusion(bf16[512,2,128]{2,1,0:T(2,128)(2,1)S(1)} %concatenate.24, bf16[1024,2,128]{2,1,0:T(2,128)(2,1)S(1)} %concatenate.23), kind=kLoop, calls=%fused_computation.52 | loop fusion | flops 393216 | bytes 1572864 | tf_op jit(solution)/shard_map/transpose | solution.py:76
  123.3 185.4 %while.18 = (s32[]{:T(128)}, bf16[8,1024,128]{1,2,0:T(8,128)(2,1)}, bf16[8,1024,128]{2,1,0:T(8,128)(2,1)}, f32[8,1536,128]{2,1,0:T(8,128)}, f32[8,1536,128]{2,1,...) while((s32[]{:T(128)}, bf16[8,1024,128]{1,2,0:T(8,128)(2,1)}, ...), condition=%wide.region_4.6_spmd, body=%wide.region_0.5_spmd.sunk | while | flops 2443441152 | bytes 48017844 | solution.py:90
  184.6 3.8 fusion.72
  207.8 3.8 fusion.72
  308.7 6.9 %bitcast_reduce_fusion = (f32[2,1536,128]{2,1,0:T(8,128)}, f32[2,1536,128]{2,1,0:T(8,128)S(1)}) fusion(f32[8,1536,128]{2,1,0:T(8,128)} %get-tuple-element.151, f32[8,1536,128]{2,1,0:T(8,128)} %get-tuple-element.150), kind=kLoop, calls=%fused_computation.42 | loop fusion | flops 2359296 | bytes 15728640 | tf_op jit(solution)/shard_map/reduce_sum | solution.py:94
  331.2 5.1 %all-to-all-done.7 = bf16[4,256,256]{2,1,0:T(8,128)(2,1)S(1)} async-done(((bf16[4,256,256]{2,1,0:T(8,128)(2,1)}), bf16[4,256,256]{2,1,0:T(8,128)(2,1)S(1)}, u32[]{:S(2)}, u32[]{:S(2)}) %all-to-all-start.7) | async-done | bytes 524320 | tf_op jit(solution)/shard_map/all_to_all | solution.py:125
  336.3 4.1 all-to-all-start.6
  348.8 4.8 all-to-all-start.4
  363.6 10.8 %all-to-all-done.4 = bf16[4,256,1024]{2,1,0:T(8,128)(2,1)} async-done(((bf16[4,256,1024]{2,1,0:T(8,128)(2,1)}), bf16[4,256,1024]{2,1,0:T(8,128)(2,1)}, u32[]{:S(2)}, u32[]{:S(2)}) %all-to-all-start.4) | async-done | bytes 2097184 | tf_op jit(solution)/shard_map/all_to_all | solution.py:122
  381.5 3.9 copy.82
  385.4 4.1 copy.95
  389.5 8.1 %all-to-all-done.5 = bf16[4,256,1024]{2,1,0:T(8,128)(2,1)S(1)} async-done(((bf16[4,256,1024]{2,1,0:T(8,128)(2,1)}), bf16[4,256,1024]{2,1,0:T(8,128)(2,1)S(1)}, u32[]{:S(2)}, u32[]{:S(2)}) %all-to-all-start.5) | async-done | bytes 2097184 | tf_op jit(solution)/shard_map/all_to_all | solution.py:123
  400.3 4.1 copy.96
  404.4 79.4 %reduce-scatter.5.cloned.1.call-done = bf16[1,128,256]{2,1,0:T(8,128)(2,1)} async-done(((bf16[32,128,256]{2,1,0:T(8,128)(2,1)}), bf16[1,128,256]{2,1,0:T(8,128)(2,1)}) %reduce-scatter.5.cloned.1.call-update) | async-done | bytes 65552 | tf_op jit(solution)/shard_map/reduce_scatter | solution.py:113
  (155 shorter events, 217.2 us)
Async XLA Ops:
  7.2 8.1 %copy-start.3 = (bf16[256,1024]{1,0:T(8,128)(2,1)S(1)}, bf16[256,1024]{1,0:T(8,128)(2,1)}, u32[]{:S(2)}) copy-start(bf16[256,1024]{1,0:T(8,128)(2,1)} %param.14) | copy-start | bytes 1572868
  7.2 97.7 %all-gather.5.cloned.1.call-start = ((), (), s32[]{:S(2)}) async-start(), calls=%async_computation.11 | async-start | bytes 2162688 | tf_op jit(solution)/shard_map/all_gather | solution.py:39
  7.9 99.2 %all-gather.3.cloned.1.call-start = ((), (), s32[]{:S(2)}) async-start(), calls=%async_computation.10 | async-start | bytes 2162688 | tf_op jit(solution)/shard_map/all_gather | solution.py:38
  8.7 19.6 %copy-start.1 = (bf16[256,4096]{1,0:T(8,128)(2,1)S(1)}, bf16[256,4096]{1,0:T(8,128)(2,1)}, u32[]{:S(2)}) copy-start(bf16[256,4096]{1,0:T(8,128)(2,1)} %param.12) | copy-start | bytes 6291460
  10.7 14.1 %all-to-all-start.1 = ((bf16[256,4,256]{2,0,1:T(8,128)(2,1)}), bf16[256,4,256]{2,0,1:T(8,128)(2,1)S(1)}, u32[]{:S(2)}, u32[]{:S(2)}) async-start(bf16[256,4,256]{2,0,1:T(8,128)(2,1)} %bitcast.114), calls=%async_computation.1 | async-start | bytes 1048576 | tf_op jit(solution)/shard_map/all_to_all | solution.py:33
  24.7 11.8 %all-to-all-start.2 = ((bf16[256,4,256]{2,0,1:T(8,128)(2,1)}), bf16[256,4,256]{2,0,1:T(8,128)(2,1)S(1)}, u32[]{:S(2)}, u32[]{:S(2)}) async-start(bf16[256,4,256]{2,0,1:T(8,128)(2,1)} %bitcast.160), calls=%async_computation.2 | async-start | bytes 1048576 | tf_op jit(solution)/shard_map/all_to_all | solution.py:34
  36.5 5.3 %copy-start.2 = (bf16[256,4096]{1,0:T(8,128)(2,1)S(1)}, bf16[256,4096]{1,0:T(8,128)(2,1)}, u32[]{:S(2)}) copy-start(bf16[256,4096]{1,0:T(8,128)(2,1)} %param.15) | copy-start | bytes 6291460
  36.5 28.7 %all-to-all-start = ((bf16[256,4,1024]{2,0,1:T(8,128)(2,1)}), bf16[256,4,1024]{2,0,1:T(8,128)(2,1)}, u32[]{:S(2)}, u32[]{:S(2)}) async-start(bf16[256,4,1024]{2,0,1:T(8,128)(2,1)} %bitcast.112), calls=%async_computation | async-start | bytes 4194304 | tf_op jit(solution)/shard_map/all_to_all | solution.py:32
  44.3 25.6 %copy-start.6 = (pred[4]{0:T(512)(128)(4,1)}, pred[4]{0:T(512)(128)(4,1)S(1)}, u32[]{:S(2)}) copy-start(pred[4]{0:T(512)(128)(4,1)S(1)} %iota_compare_fusion.2) | copy-start | bytes 16
  65.2 4.7 copy-start.4
  65.2 27.8 %all-to-all-start.3 = ((bf16[256,4,1024]{0,2,1:T(8,128)(2,1)}), bf16[256,4,1024]{0,2,1:T(8,128)(2,1)}, u32[]{:S(2)}, u32[]{:S(2)}) async-start(bf16[256,4,1024]{0,2,1:T(8,128)(2,1)} %bitcast.20), calls=%async_computation.3 | async-start | bytes 4194304 | tf_op jit(solution)/shard_map/all_to_all | solution.py:35
  69.8 334.5 %reduce-scatter.3.cloned.1.call-start = ((), (), s32[]{:S(2)}) async-start(), calls=%async_computation.12 | async-start | bytes 2162688 | tf_op jit(solution)/shard_map/reduce_scatter | solution.py:110
  315.6 1.1 copy-start
  315.6 1.1 copy-start.5
  315.6 1.1 copy-start.7
  324.8 11.5 %all-to-all-start.7 = ((bf16[4,256,256]{2,1,0:T(8,128)(2,1)}), bf16[4,256,256]{2,1,0:T(8,128)(2,1)S(1)}, u32[]{:S(2)}, u32[]{:S(2)}) async-start(bf16[4,256,256]{2,1,0:T(8,128)(2,1)} %convert_element_type.72), calls=%async_computation.7 | async-start | bytes 1048576 | tf_op jit(solution)/shard_map/all_to_all | solution.py:125
  336.3 12.5 %all-to-all-start.6 = ((bf16[4,256,256]{2,1,0:T(8,128)(2,1)}), bf16[4,256,256]{2,1,0:T(8,128)(2,1)}, u32[]{:S(2)}, u32[]{:S(2)}) async-start(bf16[4,256,256]{2,1,0:T(8,128)(2,1)} %convert_element_type.70), calls=%async_computation.6 | async-start | bytes 1048576 | tf_op jit(solution)/shard_map/all_to_all | solution.py:124
  348.8 25.7 %all-to-all-start.4 = ((bf16[4,256,1024]{2,1,0:T(8,128)(2,1)}), bf16[4,256,1024]{2,1,0:T(8,128)(2,1)}, u32[]{:S(2)}, u32[]{:S(2)}) async-start(bf16[4,256,1024]{2,1,0:T(8,128)(2,1)} %copy.99), calls=%async_computation.4 | async-start | bytes 4194304 | tf_op jit(solution)/shard_map/all_to_all | solution.py:122
  353.5 130.2 %reduce-scatter.5.cloned.1.call-start = ((), (), s32[]{:S(2)}) async-start(), calls=%async_computation.13 | async-start | bytes 2162688 | tf_op jit(solution)/shard_map/reduce_scatter | solution.py:113
  374.4 23.2 %all-to-all-start.5 = ((bf16[4,256,1024]{2,1,0:T(8,128)(2,1)}), bf16[4,256,1024]{2,1,0:T(8,128)(2,1)S(1)}, u32[]{:S(2)}, u32[]{:S(2)}) async-start(bf16[4,256,1024]{2,1,0:T(8,128)(2,1)} %all_to_all.116), calls=%async_computation.5 | async-start | bytes 4194304 | tf_op jit(solution)/shard_map/all_to_all | solution.py:123
Sparse Core Ops, SparseCore 0:
  10.2 46.1 all-gather.4
  58.7 43.0 all-gather.2
  321.9 79.3 reduce-scatter.2
  405.3 78.3 reduce-scatter.4
where the time goes:
time: 493 us; the launch traced here: 490 us
  waiting for transfers between devices  159 us (32%)
  matrix products  138 us (28%)
  local copies, waits for them, and re-layouts  77 us (16%)
  other arithmetic  36.8 us (7%)
  starting transfers between devices  33.4 us (7%)
  loops' own time  31.5 us (6%)
  between operations  14.8 us (3%)
    reduce_scatter x1, waiting for transfers between devices, shards(): lax.psum_scatter(dense_v.astype(jnp.bfloat16), 'ctx', scatter_dimension=0...  79.4 us
    another operation x1, loops' own time, shards(): lax.map(per_head, jnp.arange(head_count, dtype=jnp.int32))  31.5 us
    dot_general x8, matrix products, head_grads(): jnp.dot(prob_half.T, grad_rows, preferred_element_type=jnp.float32)  29.9 us
    dot_general x8, matrix products, head_grads(): jnp.dot(grad_rows, value_rows.T, preferred_element_type=jnp.float32)  25.8 us
    dot_general x8, matrix products, head_grads(): jnp.dot(dscores.T, query_rows, preferred_element_type=jnp.float32)  23 us
    dot_general x8, matrix products, head_grads(): jnp.dot(prob_half, value_rows, preferred_element_type=jnp.float32)  21.9 us
    all_to_all x1, waiting for transfers between devices, shards(): lax.all_to_all(queries, 'tp', split_axis=1, concat_axis=0, tiled=True)  20.9 us
    dot_general x8, matrix products, head_grads(): jnp.dot(query_rows, key_rows.T, preferred_element_type=jnp.float32)  18.9 us
  transfers between devices with their start and end apart: 12, of which 8 were waited for; matrix products, arithmetic and copies ran while one was open for 13% of the time, Pallas kernels for 0%

commit v1 on v0

v1 whole, which is shorter than its diff:
```python
import functools
import math

import jax
import jax.numpy as jnp
from jax import lax
from jax.experimental import pallas as pl
from jax.experimental.pallas import tpu as pltpu
from jax.sharding import Mesh
from jax.sharding import PartitionSpec as P

HD = 128
SCALE = HD**-0.5
SCALE2 = SCALE * math.log2(math.e)
NEG = -1e30
F32 = jnp.float32
BF16 = jnp.bfloat16
NN = (((1,), (0,)), ((), ()))
NT = (((1,), (1,)), ((), ()))
TN = (((0,), (0,)), ((), ()))
TP = 4
CHUNK = 256
SLOTS = 4
BLOCK = 128
BEAC = SLOTS * BLOCK
KEYS = BEAC + TP * CHUNK
GROUP = 4
QW = GROUP * HD
PIECE = 2 * QW + 2 * HD


def mm(a, b, dims):
    return lax.dot_general(a, b, dims, preferred_element_type=F32)


def fold(x, op):
    return op(x.reshape(x.shape[0] // 8, 8, x.shape[1]), axis=0)


def chunk_grads(chunk, q, go, keys, vals, bias, scores, dk_acc, dv_acc):
    blocks = BEAC // CHUNK + chunk + 1
    peak = None
    for b in range(blocks):
        rows = pl.ds(b * CHUNK, CHUNK)
        s = mm(keys[rows, :], q, NT)
        if b < BEAC // CHUNK:
            part = bias[rows, :]
            s = s + jnp.concatenate([part, part], axis=1)
        if b == blocks - 1:
            key_pos = lax.broadcasted_iota(jnp.int32, (CHUNK, CHUNK), 0)
            query_pos = lax.broadcasted_iota(jnp.int32, (CHUNK, CHUNK), 1)
            s = jnp.where(key_pos <= query_pos, s, NEG)
        scores[rows, :] = s
        top = fold(s, jnp.max)
        peak = top if peak is None else jnp.maximum(peak, top)
    shift = jnp.max(peak, axis=0, keepdims=True) * SCALE2
    total = jnp.zeros((8, CHUNK), F32)
    for b in range(blocks):
        rows = pl.ds(b * CHUNK, CHUNK)
        w = jnp.exp2(scores[rows, :] * SCALE2 - shift)
        total = total + fold(w, jnp.sum)
        scores[rows, :] = w
    inv = 1.0 / jnp.sum(total, axis=0, keepdims=True)
    out = jnp.zeros((CHUNK, HD), F32)
    for b in range(blocks):
        rows = pl.ds(b * CHUNK, CHUNK)
        p = scores[rows, :] * inv
        scores[rows, :] = p
        pb = p.astype(BF16)
        dv_acc[rows, :] += mm(pb, go, NN)
        out = out + mm(pb, vals[rows, :], TN)
    out = out.astype(BF16)
    prod = go.astype(F32) * out.astype(F32)
    delta = lax.dot_general(
        jnp.ones((8, HD), F32), prod, NT, precision=lax.Precision.HIGHEST, preferred_element_type=F32
    )[0:1, :]
    dq = jnp.zeros((CHUNK, HD), F32)
    for b in range(blocks):
        rows = pl.ds(b * CHUNK, CHUNK)
        dp = mm(vals[rows, :], go, NT)
        ds = (scores[rows, :] * (dp - delta)).astype(BF16)
        dk_acc[rows, :] += mm(ds, q, NN)
        dq = dq + mm(ds, keys[rows, :], TN)
    return out, (dq * SCALE).astype(BF16)


S_A, S_B, S_COUNT, S_Y, S_SAME = 0, 4, 8, 9, 10


def attn_body(sc, *refs):
    pieces = [refs[4 * d : 4 * d + 4] for d in range(TP)]
    refs = refs[4 * TP :]
    near, far = refs[: 2 * SLOTS], refs[2 * SLOTS : 4 * SLOTS]
    refs = refs[4 * SLOTS :]
    outs, beac_out = refs[:TP], refs[TP]
    qs, gs, os, dqs, keys, vals, bias, scores, dk_acc, dv_acc = refs[TP + 1 :]
    head = pl.program_id(0)
    me = sc[S_Y]

    @pl.when(head == 0)
    def _():
        same = sc[S_SAME]
        for t, dst in ((0, keys), (1, vals)):
            for j in range(SLOTS):
                a, b = near[t * SLOTS + j][0], far[t * SLOTS + j][0]
                dst[pl.ds(j * BLOCK, BLOCK), :] = jnp.where(same == 1, a, b)
            for d in range(TP):
                at = pl.multiple_of(BEAC + lax.rem(me + d, TP) * CHUNK, CHUNK)
                dst[pl.ds(at, CHUNK), :] = pieces[d][2 + t][...]
        for j in range(SLOTS):
            row = jnp.where(j < sc[S_COUNT], 0.0, NEG)
            bias[pl.ds(j * BLOCK, BLOCK), :] = jnp.full((BLOCK, HD), row, F32)
        dk_acc[...] = jnp.zeros_like(dk_acc)
        dv_acc[...] = jnp.zeros_like(dv_acc)

    for d in range(TP):
        at = lax.rem(me + d, TP)
        qs[at] = pieces[d][0][...]
        gs[at] = pieces[d][1][...]
    for i in range(TP):
        o, dq = chunk_grads(i, qs[i], gs[i], keys, vals, bias, scores, dk_acc, dv_acc)
        os[i] = o
        dqs[i] = dq
    at_o = pl.multiple_of(head * HD, HD)
    at_q = pl.multiple_of(QW + head * HD, HD)
    for d in range(TP):
        at = lax.rem(me + d, TP)
        outs[d][:, pl.ds(at_o, HD)] = os[at]
        outs[d][:, pl.ds(at_q, HD)] = dqs[at]

    @pl.when(head == GROUP - 1)
    def _():
        for d in range(TP):
            at = pl.multiple_of(BEAC + lax.rem(me + d, TP) * CHUNK, CHUNK)
            outs[d][:, 2 * QW : 2 * QW + HD] = (dk_acc[pl.ds(at, CHUNK), :] * SCALE).astype(BF16)
            outs[d][:, 2 * QW + HD :] = dv_acc[pl.ds(at, CHUNK), :].astype(BF16)
        for j in range(SLOTS):
            rows = pl.ds(j * BLOCK, BLOCK)
            beac_out[j, :, :HD] = (dk_acc[rows, :] * SCALE).astype(BF16)
            beac_out[j, :, HD:] = dv_acc[rows, :].astype(BF16)


def attn(group, scalars, own, pieces, near, far):
    spec = pl.BlockSpec
    ops, in_specs = [], []
    kv_heads = 2
    for t in range(2):
        ops.append(own[t])
        in_specs.append(
            spec((CHUNK, HD), lambda h, sc: (0, (sc[S_Y] * kv_heads + group) * GROUP + h))
        )
    for t in range(2):
        ops.append(own[2 + t])
        in_specs.append(spec((CHUNK, HD), lambda h, sc: (0, sc[S_Y] * kv_heads + group)))
    for piece in pieces:
        ops += [piece] * 4
        in_specs += [
            spec((CHUNK, HD), lambda h, sc: (0, h)),
            spec((CHUNK, HD), lambda h, sc: (0, GROUP + h)),
            spec((CHUNK, HD), lambda h, sc: (0, 2 * GROUP)),
            spec((CHUNK, HD), lambda h, sc: (0, 2 * GROUP + 1)),
        ]
    for arr, base in ((near, S_A), (far, S_B)):
        for t in range(2):
            for j in range(SLOTS):
                ops.append(arr)
                in_specs.append(
                    spec((1, BLOCK, HD), lambda h, sc, at=base + j, t=t: (sc[at], 0, t))
                )
    out_specs = [spec((CHUNK, PIECE), lambda h, sc: (0, 0)) for _ in range(TP)]
    out_specs.append(spec((SLOTS, BLOCK, 2 * HD), lambda h, sc: (0, 0, 0)))
    out_shape = [jax.ShapeDtypeStruct((CHUNK, PIECE), BF16) for _ in range(TP)]
    out_shape.append(jax.ShapeDtypeStruct((SLOTS, BLOCK, 2 * HD), BF16))
    pairs = GROUP * CHUNK * CHUNK * 18
    return pl.pallas_call(
        attn_body,
        grid_spec=pltpu.PrefetchScalarGridSpec(
            num_scalar_prefetch=1,
            grid=(GROUP,),
            in_specs=in_specs,
            out_specs=out_specs,
            scratch_shapes=[
                pltpu.VMEM((TP, CHUNK, HD), BF16),
                pltpu.VMEM((TP, CHUNK, HD), BF16),
                pltpu.VMEM((TP, CHUNK, HD), BF16),
                pltpu.VMEM((TP, CHUNK, HD), BF16),
                pltpu.VMEM((KEYS, HD), BF16),
                pltpu.VMEM((KEYS, HD), BF16),
                pltpu.VMEM((BEAC, HD), F32),
                pltpu.VMEM((KEYS, CHUNK), F32),
                pltpu.VMEM((KEYS, HD), F32),
                pltpu.VMEM((KEYS, HD), F32),
            ],
        ),
        out_shape=out_shape,
        compiler_params=pltpu.CompilerParams(vmem_limit_bytes=24 << 20),
        cost_estimate=pl.CostEstimate(
            flops=6 * 2 * pairs * HD * 2, bytes_accessed=6 << 20, transcendentals=pairs
        ),
        name="attn",
    )(scalars, *ops)


def place_body(y_ref, *refs):
    n = 2 * TP
    ins, outs, bufs, in_sems, out_sems = refs[:n], refs[n : n + 4], refs[n + 4], refs[n + 5], refs[n + 6]
    me = y_ref[0]
    loads = [pltpu.make_async_copy(ins[i], bufs.at[i], in_sems.at[i]) for i in range(n)]
    for copy in loads:
        copy.start()
    stores = []
    for i in range(n):
        group, d = divmod(i, TP)
        src = lax.rem(me + d, TP) * 2 + group
        loads[i].wait()
        for t, (at, width) in enumerate(((0, QW), (QW, QW), (2 * QW, HD), (2 * QW + HD, HD))):
            col = pl.multiple_of(src * width, HD)
            copy = pltpu.make_async_copy(
                bufs.at[i, :, pl.ds(at, width)], outs[t].at[:, pl.ds(col, width)], out_sems.at[i, t]
            )
            copy.start()
            stores.append(copy)
    for copy in stores:
        copy.wait()


def place(y, pieces):
    anyspec = pl.BlockSpec(memory_space=pl.ANY)
    widths = (TP * 2 * QW, TP * 2 * QW, TP * 2 * HD, TP * 2 * HD)
    return pl.pallas_call(
        place_body,
        grid_spec=pltpu.PrefetchScalarGridSpec(
            num_scalar_prefetch=1,
            grid=(),
            in_specs=[anyspec] * len(pieces),
            out_specs=[anyspec] * 4,
            scratch_shapes=[
                pltpu.VMEM((2 * TP, CHUNK, PIECE), BF16),
                pltpu.SemaphoreType.DMA((2 * TP,)),
                pltpu.SemaphoreType.DMA((2 * TP, 4)),
            ],
        ),
        out_shape=[jax.ShapeDtypeStruct((CHUNK, w), BF16) for w in widths],
        compiler_params=pltpu.CompilerParams(vmem_limit_bytes=16 << 20),
        name="place",
    )(y, *pieces)


def shift(x, step):
    return lax.ppermute(x, "y", [(s, (s + step) % TP) for s in range(TP)])


def swap(x):
    return lax.ppermute(x, "core", [(0, 1), (1, 0)])


def shards(queries, keys_in, values_in, grad_output, beacon_keys, beacon_values, read_blocks, read_counts):
    y = lax.axis_index("y")
    core = lax.axis_index("core")
    chips = lax.axis_size("z") * lax.axis_size("x")

    def cut(a, to, group, width):
        return lax.dynamic_slice(a, (0, (to * 2 + group) * width), (CHUNK, width))

    both = [
        jnp.concatenate(
            [beacon_keys[:, g * HD : (g + 1) * HD], beacon_values[:, g * HD : (g + 1) * HD]], axis=1
        )
        for g in range(2)
    ]
    first = core == 0
    mine = jnp.where(first, both[0], both[1])
    other = swap(jnp.where(first, both[1], both[0]))
    chip_blocks = jnp.broadcast_to(jnp.stack([mine, other])[None], (chips, 2, BLOCK, 2 * HD))
    row, count = read_blocks[0], read_counts
    table = jnp.concatenate([row, count])
    peer_table = swap(table)

    recv = []
    for g in range(2):
        got = {}
        for d in (1, 3, 2):
            to = (y + d) % TP
            piece = jnp.concatenate(
                [
                    cut(queries, to, g, QW),
                    cut(grad_output, to, g, QW),
                    cut(keys_in, to, g, HD),
                    cut(values_in, to, g, HD),
                ],
                axis=1,
            )
            got[TP - d] = shift(piece, d)
        recv.append([got[1], got[2], got[3]])

    near = lax.all_to_all(chip_blocks, ("z", "x"), 0, 0, tiled=True)
    far = swap(near).reshape(chips * 2, BLOCK, 2 * HD)
    near = near.reshape(chips * 2, BLOCK, 2 * HD)

    own = (queries, grad_output, keys_in, values_in)
    chip, parity = row // 2, row % 2
    tables = [table, peer_table]
    back, beacs = [], []
    for g in range(2):
        scalars = jnp.concatenate(
            [
                chip * 2 + (parity ^ core),
                chip * 2 + (parity ^ core ^ 1),
                count,
                y[None],
                (core == g).astype(jnp.int32)[None],
            ]
        ).astype(jnp.int32)
        res = attn(g, scalars, own, recv[g], near, far)
        got = {0: res[0]}
        for d in (1, 3, 2):
            got[TP - d] = shift(res[d], d)
        back.append([got[d] for d in range(TP)])
        dense = jnp.zeros((chips, BLOCK, 2 * HD), F32)
        ids = jnp.arange(chips, dtype=jnp.int32)
        for terms, tab in ((res[TP], table), (swap(res[TP]), peer_table)):
            for j in range(SLOTS):
                use = (tab[j] == ids * 2 + core) & (j < tab[SLOTS])
                dense = dense + jnp.where(use[:, None, None], terms[j].astype(F32)[None], 0.0)
        parts = lax.all_to_all(dense.astype(BF16), ("z", "x"), 0, 0, tiled=True)
        beacs.append(jnp.sum(parts.astype(F32), axis=0).astype(BF16))
    out, dq, dk, dv = place(y[None].astype(jnp.int32), back[0] + back[1])
    dbk = jnp.concatenate([b[:, :HD] for b in beacs], axis=1)
    dbv = jnp.concatenate([b[:, HD:] for b in beacs], axis=1)
    return out, dq, dk, dv, dbk, dbv


def solution(mesh):
    split = Mesh(mesh.devices.reshape(4, 4, 2, 4), ("z", "x", "core", "y"))
    ctx = ("z", "x", "core")
    tokens = P(ctx + ("y",), None)
    beacon = P(ctx, "y")
    in_specs = (tokens,) * 4 + (beacon,) * 2 + (P(ctx, None), P(ctx))
    out_specs = (tokens,) * 4 + (beacon,) * 2
    return jax.shard_map(shards, mesh=split, in_specs=in_specs, out_specs=out_specs, check_vma=False)
```

time: 493 us -> 263 us (0.53)
  matrix products: 138 us -> 0 us
  Pallas kernels: 0 us -> 84.4 us
  waiting for transfers between devices: 159 us -> 90.6 us
  local copies, waits for them, and re-layouts: 77 us -> 17.9 us
  loops' own time: 31.5 us -> 0 us
  other arithmetic: 36.8 us -> 26.2 us
  between operations: 14.8 us -> 4.5 us
    dot_general x50 -> x0, matrix products: 138 us -> none  [the longest x8 29.9 us: head_grads(): jnp.dot(prob_half.T, grad_rows, preferred_element_type=jnp.float32)]
    pallas_call x0 -> x3, Pallas kernels: none -> 84.4 us  [the longest x2 80.1 us: attn(): pl.pallas_call(attn_body, grid_spec=pltpu.PrefetchScalarGridSpec(num_scal...]
    reduce_scatter x2 -> x0, waiting for transfers between devices: 79.4 us -> none  [the longest x1 79.4 us: shards(): lax.psum_scatter(dense_v.astype(jnp.bfloat16), 'ctx', scatter_dimension=0...]
    ppermute x0 -> x17, waiting for transfers between devices: none -> 64.3 us  [the longest x12 62.9 us: shift(): return lax.ppermute(x, 'y', [(s, (s + step) % TP) for s in range(TP)])]
    all_to_all x8 -> x3, waiting for transfers between devices: 78.2 us -> 26.3 us  [the longest x1 26.3 us: shards(): near = lax.all_to_all(chip_blocks, ('z', 'x'), 0, 0, tiled=True)]
    another operation x1 -> x0, loops' own time: 31.5 us -> none  [shards(): lax.map(per_head, jnp.arange(head_count, dtype=jnp.int32))]
    all_to_all x11 -> x0, local copies, waits for them, and re-layouts: 25.1 us -> none  [the longest x3 10.3 us: shards(): lax.all_to_all(seg_out, 'tp', split_axis=0, concat_axis=1, tiled=True)]
    reduce_sum x17 -> x2, other arithmetic: 23.1 us -> 2.75 us  [shards(): beacs.append(jnp.sum(parts.astype(F32), axis=0).astype(BF16))]
  transfers between devices with their start and end apart: 12 -> 20, of which waited for: 8 -> 9; matrix products, arithmetic and copies ran while one was open for 13% -> 11% of each run, Pallas kernels for 0% -> 32%
where the time goes in v1:
time: 263 us; the launch traced here: 261 us
  waiting for transfers between devices  90.6 us (34%)
  Pallas kernels  84.4 us (32%)
  starting transfers between devices  37.8 us (14%)
  other arithmetic  26.2 us (10%)
  local copies, waits for them, and re-layouts  17.9 us (7%)
  between operations  4.5 us (2%)
    pallas_call x2, Pallas kernels, attn(): pl.pallas_call(attn_body, grid_spec=pltpu.PrefetchScalarGridSpec(num_scal...  80.1 us
    ppermute x12, waiting for transfers between devices, shift(): return lax.ppermute(x, 'y', [(s, (s + step) % TP) for s in range(TP)])  62.9 us
    all_to_all x1, waiting for transfers between devices, shards(): near = lax.all_to_all(chip_blocks, ('z', 'x'), 0, 0, tiled=True)  26.3 us
    ppermute x12, starting transfers between devices, shift(): return lax.ppermute(x, 'y', [(s, (s + step) % TP) for s in range(TP)])  17.8 us
    all_to_all x2, starting transfers between devices, shards(): parts = lax.all_to_all(dense.astype(BF16), ('z', 'x'), 0, 0, tiled=True)  11.2 us
    concatenate x6, other arithmetic, shards(): jnp.concatenate([cut(queries, to, g, QW), cut(grad_output, to, g, QW), cu...  10.8 us
    unnamed x38, local copies, waits for them, and re-layouts  9.85 us
    all_to_all x1, starting transfers between devices, shards(): near = lax.all_to_all(chip_blocks, ('z', 'x'), 0, 0, tiled=True)  8.12 us
  transfers between devices with their start and end apart: 20, of which 9 were waited for; matrix products, arithmetic and copies ran while one was open for 11% of the time, Pallas kernels for 32%

profile of v1, /device:TPU:0, one launch (start us, length us, event | category | flops | bytes accessed | tf_op | source)
XLA Modules:
  0.0 261.4 jit_solution(11549625874622415096)
XLA Ops:
  4.4 8.1 %all-to-all-start = ((bf16[16,2,128,256]{3,2,1,0:T(8,128)(2,1)}), bf16[16,2,128,256]{3,2,1,0:T(8,128)(2,1)S(1)}, u32[]{:S(2)}, u32[]{:S(2)}) async-start(bf16[16,2,128,256]{3,2,1,0:T(8,128)(2,1)} %broadcast_in_dim.307), calls=%async_computation | async-start | bytes 4194304 | tf_op jit(solution)/shard_map/all_to_all | solution.py:296
  13.6 3.2 %constant_dynamic-slice_fusion.2 = (bf16[256,512]{1,0:T(8,128)(2,1)}, bf16[256,512]{1,0:T(8,128)(2,1)}, bf16[256,512]{1,0:T(8,128)(2,1)}, bf16[256,512]{1,0:T(8,...) fusion(bf16[256,4096]{1,0:T(8,128)(2,1)} %refs_1_.3, ...), kind=kLoop, calls=%fused_computation.39 | loop fusion | bytes 6291480 | tf_op jit(solution)/shard_map/dynamic_slice | solution.py:263
  19.3 26.3 %all-to-all-done = bf16[16,2,128,256]{3,2,1,0:T(8,128)(2,1)S(1)} async-done(((bf16[16,2,128,256]{3,2,1,0:T(8,128)(2,1)}), bf16[16,2,128,256]{3,2,1,0:T(8,128)(2,1)S(1)}, u32[]{:S(2)}, u32[]{:S(2)}) %all-to-all-start) | async-done | bytes 2097184 | tf_op jit(solution)/shard_map/all_to_all | solution.py:296
  45.6 2.0 pad_maximum_fusion.1
  47.6 3.2 %collective-permute-start.1 = (bf16[256,1280]{1,0:T(8,128)(2,1)}, bf16[256,1280]{1,0:T(8,128)(2,1)}, u32[]{:S(2)}, u32[]{:S(2)}) collective-permute-start(bf16[256,1280]{1,0:T(8,128)(2,1)} %pad_maximum_fusion.1), channel_id=1, source_target_pairs={{0,2},{1,3},{2,0},{3,1},{4,6},{5,7},{6,4},{7,5},{8,10},{9,11},{10,... | collective-permute-start | bytes 1966088 | tf_op jit(solution)/shard_map/ppermute | solution.py:250
  50.8 1.9 pad_maximum_fusion
  55.4 2.0 pad_maximum_fusion.5
  57.4 2.0 pad_maximum_fusion.3
  62.0 2.0 pad_maximum_fusion.4
  70.5 2.3 collective-permute-start.8
  73.3 8.2 %collective-permute-done.refs_4_.refs_5_.refs_6_.refs_7_ = bf16[256,1280]{1,0:T(8,128)(2,1)} collective-permute-done((bf16[256,1280]{1,0:T(8,128)(2,1)}, bf16[256,1280]{1,0:T(8,128)(2,1)}, u32[]{:S(2)}, u32[]{:S(2)}) %collective-permute-start) | collective-permute-done | bytes 655392 | tf_op jit(solution)/shard_map/ppermute | solution.py:250
  85.2 39.7 %attn.2 = (bf16[256,1280]{1,0:T(8,128)(2,1)S(1)}, bf16[256,1280]{1,0:T(8,128)(2,1)S(1)}, bf16[256,1280]{1,0:T(8,128)(2,1)S(1)}, bf16[256,1280]{1,0:T(8,128)(2,1)S(1)}, bf16[4,128,256]{2,1,0:T(8,128)(2,1)S(1)}) custom-call(s32[11]{0:T(128)S(1)} %concatenate.65.sc, bf16[256,4096]{1,0:T(8,128)(2,1)S(1)} %copy-done, bf16[256,4096]{1,0:T(8,128)(2,1)S(1)} %copy-done.2, ...), custom_call_target="tpu_custom_call" | custom-call | flops 14495514624 | bytes 6291456 | tf_op jit(solution)/shard_map/attn/pallas_call | solution.py:175
  126.6 2.9 %add_convert_fusion.1 = bf16[16,128,256]{2,1,0:T(8,128)(2,1)} fusion(f32[128,256]{1,0:T(8,128)S(1)} %get-tuple-element.66, f32[128,256]{1,0:T(8,128)S(1)} %get-tuple-element.67, f32[128,256]{1,0:T(8,128)S(1)} %get-tuple-element.68, f32[128,256]{1,0:T(8,128)S(1)} %get-tuple-element.65, f32[128,256]{1,0:T(8,128)S(1)} %get-tuple-element.62, ...), kind=kLoop, calls=%fused_computation.1 | loop fusion | flops 8388608 | bytes 2097280 | tf_op jit(solution)/shard_map/convert_element_type | solution.py:325
  129.6 4.6 %all-to-all-start.1 = ((bf16[16,128,256]{2,1,0:T(8,128)(2,1)}), bf16[16,128,256]{2,1,0:T(8,128)(2,1)}, u32[]{:S(2)}, u32[]{:S(2)}) async-start(bf16[16,128,256]{2,1,0:T(8,128)(2,1)} %add_convert_fusion.1), calls=%async_computation.1 | async-start | bytes 2097152 | tf_op jit(solution)/shard_map/all_to_all | solution.py:325
  139.4 40.4 %attn.3 = (bf16[256,1280]{1,0:T(8,128)(2,1)S(1)}, bf16[256,1280]{1,0:T(8,128)(2,1)S(1)}, bf16[256,1280]{1,0:T(8,128)(2,1)S(1)}, bf16[256,1280]{1,0:T(8,128)(2,1)}, bf16[4,128,256]{2,1,0:T(8,128)(2,1)S(1)}) custom-call(s32[11]{0:T(128)S(1)} %concatenate.77.sc, bf16[256,4096]{1,0:T(8,128)(2,1)S(1)} %copy-done.1, bf16[256,4096]{1,0:T(8,128)(2,1)S(1)} %copy-done.3, ...), custom_call_target="tpu_custom_call" | custom-call | flops 14495514624 | bytes 6291456 | tf_op jit(solution)/shard_map/attn/pallas_call | solution.py:175
  180.3 2.6 %collective-permute-start.11 = (bf16[256,1280]{1,0:T(8,128)(2,1)}, bf16[256,1280]{1,0:T(8,128)(2,1)S(1)}, u32[]{:S(2)}, u32[]{:S(2)}) collective-permute-start(bf16[256,1280]{1,0:T(8,128)(2,1)} %get-tuple-element.25), channel_id=1, source_target_pairs={{0,3},{1,0},{2,1},{3,2},{4,7},{5,4},{6,5},{7,6},{8,11},{9,8},{10,9... | collective-permute-start | bytes 1966088 | tf_op jit(solution)/shard_map/ppermute | solution.py:250
  183.0 2.9 %add_convert_fusion = bf16[16,128,256]{2,1,0:T(8,128)(2,1)} fusion(f32[128,256]{1,0:T(8,128)S(1)} %get-tuple-element.74, f32[128,256]{1,0:T(8,128)S(1)} %get-tuple-element.75, f32[128,256]{1,0:T(8,128)S(1)} %get-tuple-element.76, f32[128,256]{1,0:T(8,128)S(1)} %get-tuple-element.73, f32[128,256]{1,0:T(8,128)S(1)} %get-tuple-element.70, ...), kind=kLoop, calls=%fused_computation | loop fusion | flops 8388608 | bytes 2097280 | tf_op jit(solution)/shard_map/convert_element_type | solution.py:325
  186.0 6.6 %all-to-all-start.2 = ((bf16[16,128,256]{2,1,0:T(8,128)(2,1)}), bf16[16,128,256]{2,1,0:T(8,128)(2,1)}, u32[]{:S(2)}, u32[]{:S(2)}) async-start(bf16[16,128,256]{2,1,0:T(8,128)(2,1)} %add_convert_fusion), calls=%async_computation.2 | async-start | bytes 2097152 | tf_op jit(solution)/shard_map/all_to_all | solution.py:325
  194.9 1.8 collective-permute-start.5
  198.2 14.0 %collective-permute-done.11.refs_5_ = bf16[256,1280]{1,0:T(8,128)(2,1)S(1)} collective-permute-done((bf16[256,1280]{1,0:T(8,128)(2,1)}, bf16[256,1280]{1,0:T(8,128)(2,1)S(1)}, u32[]{:S(2)}, u32[]{:S(2)}) %collective-permute-start.11) | collective-permute-done | bytes 655392 | tf_op jit(solution)/shard_map/ppermute | solution.py:250
  212.3 13.9 %collective-permute-done.13.refs_7_ = bf16[256,1280]{1,0:T(8,128)(2,1)S(1)} collective-permute-done((bf16[256,1280]{1,0:T(8,128)(2,1)}, bf16[256,1280]{1,0:T(8,128)(2,1)S(1)}, u32[]{:S(2)}, u32[]{:S(2)}) %collective-permute-start.13) | collective-permute-done | bytes 655392 | tf_op jit(solution)/shard_map/ppermute | solution.py:250
  226.2 13.5 %collective-permute-done.5.refs_1_ = bf16[256,1280]{1,0:T(8,128)(2,1)S(1)} collective-permute-done((bf16[256,1280]{1,0:T(8,128)(2,1)}, bf16[256,1280]{1,0:T(8,128)(2,1)S(1)}, u32[]{:S(2)}, u32[]{:S(2)}) %collective-permute-start.5) | collective-permute-done | bytes 655392 | tf_op jit(solution)/shard_map/ppermute | solution.py:250
  240.2 12.8 %collective-permute-done.7.refs_3_ = bf16[256,1280]{1,0:T(8,128)(2,1)S(1)} collective-permute-done((bf16[256,1280]{1,0:T(8,128)(2,1)S(1)}, bf16[256,1280]{1,0:T(8,128)(2,1)S(1)}, u32[]{:S(2)}, u32[]{:S(2)}) %collective-permute-start.7) | collective-permute-done | bytes 655392 | tf_op jit(solution)/shard_map/ppermute | solution.py:250
  253.0 4.3 %place.1 = (bf16[256,4096]{1,0:T(8,128)(2,1)}, bf16[256,4096]{1,0:T(8,128)(2,1)}, bf16[256,1024]{1,0:T(8,128)(2,1)}, bf16[256,1024]{1,0:T(8,128)(2,1)}) custom-call(s32[1]{0:T(128)} %bitcast.y_ref, bf16[256,1280]{1,0:T(8,128)(2,1)S(1)} %get-tuple-element.20.refs_0_, bf16[256,1280]{1,0:T(8,128)(2,1)S(1)} %collective-permute-done.5.refs_1_, ...), custom_call_target="tpu_custom_call" | custom-call | tf_op jit(solution)/shard_map/place/pallas_call | solution.py:230
  (93 shorter events, 35.5 us)
Async XLA Ops:
  1.5 1.3 collective-permute-start.3
  4.4 41.2 %all-to-all-start = ((bf16[16,2,128,256]{3,2,1,0:T(8,128)(2,1)}), bf16[16,2,128,256]{3,2,1,0:T(8,128)(2,1)S(1)}, u32[]{:S(2)}, u32[]{:S(2)}) async-start(bf16[16,2,128,256]{3,2,1,0:T(8,128)(2,1)} %broadcast_in_dim.307), calls=%async_computation | async-start | bytes 4194304 | tf_op jit(solution)/shard_map/all_to_all | solution.py:296
  16.9 37.5 %copy-start.18 = (s32[1,4]{1,0:T(1,128)S(1)}, s32[1,4]{1,0:T(1,128)}, u32[]{:S(2)}) copy-start(s32[1,4]{1,0:T(1,128)} %param.14) | copy-start | bytes 52
  17.8 51.9 %collective-permute-start.2 = (bf16[256,1280]{1,0:T(8,128)(2,1)}, bf16[256,1280]{1,0:T(8,128)(2,1)S(1)}, u32[]{:S(2)}, u32[]{:S(2)}) collective-permute-start(bf16[256,1280]{1,0:T(8,128)(2,1)} %pad_maximum_fusion.2), channel_id=1, source_target_pairs={{0,1},{1,2},{2,3},{3,0},{4,5},{5,6},{6,7},{7,4},{8,9},{9,10},{10,1... | collective-permute-start | bytes 1966088 | tf_op jit(solution)/shard_map/ppermute | solution.py:250
  45.6 35.9 %collective-permute-start.4 = (bf16[16,2,128,256]{3,2,1,0:T(8,128)(2,1)S(1)}, bf16[16,2,128,256]{3,2,1,0:T(8,128)(2,1)}, u32[]{:S(2)}, u32[]{:S(2)}) collective-permute-start(bf16[16,2,128,256]{3,2,1,0:T(8,128)(2,1)S(1)} %all-to-all-done), channel_id=1, source_target_pairs={{0,4},{4,0},{1,5},{5,1},{2,6},{6,2},{3,7},{7,3},{8,12},{12,8},{9,1... | collective-permute-start | bytes 6291464 | tf_op jit(solution)/shard_map/ppermute | solution.py:254
  47.6 25.2 %collective-permute-start.1 = (bf16[256,1280]{1,0:T(8,128)(2,1)}, bf16[256,1280]{1,0:T(8,128)(2,1)}, u32[]{:S(2)}, u32[]{:S(2)}) collective-permute-start(bf16[256,1280]{1,0:T(8,128)(2,1)} %pad_maximum_fusion.1), channel_id=1, source_target_pairs={{0,2},{1,3},{2,0},{3,1},{4,6},{5,7},{6,4},{7,5},{8,10},{9,11},{10,... | collective-permute-start | bytes 1966088 | tf_op jit(solution)/shard_map/ppermute | solution.py:250
  52.7 28.7 %collective-permute-start = (bf16[256,1280]{1,0:T(8,128)(2,1)}, bf16[256,1280]{1,0:T(8,128)(2,1)}, u32[]{:S(2)}, u32[]{:S(2)}) collective-permute-start(bf16[256,1280]{1,0:T(8,128)(2,1)} %pad_maximum_fusion), channel_id=1, source_target_pairs={{0,3},{1,0},{2,1},{3,2},{4,7},{5,4},{6,5},{7,6},{8,11},{9,8},{10,9... | collective-permute-start | bytes 1966088 | tf_op jit(solution)/shard_map/ppermute | solution.py:250
  54.5 9.5 %collective-permute-start.14 = (s32[5]{0:T(128)S(1)}, s32[5]{0:T(128)S(1)}, u32[]{:S(2)}, u32[]{:S(2)}) collective-permute-start(s32[5]{0:T(128)S(1)} %pad_add_fusion), channel_id=1, source_target_pairs={{0,4},{4,0},{1,5},{5,1},{2,6},{6,2},{3,7},{7,3},{8,12},{12,8},{9,1... | collective-permute-start | bytes 68 | tf_op jit(solution)/shard_map/ppermute | solution.py:254
  54.7 26.7 %copy-start = (bf16[256,4096]{1,0:T(8,128)(2,1)S(1)}, bf16[256,4096]{1,0:T(8,128)(2,1)}, u32[]{:S(2)}) copy-start(bf16[256,4096]{1,0:T(8,128)(2,1)} %refs_0_.3) | copy-start | bytes 6291460
  64.0 70.1 %collective-permute-start.10 = (bf16[256,1280]{1,0:T(8,128)(2,1)}, bf16[256,1280]{1,0:T(8,128)(2,1)}, u32[]{:S(2)}, u32[]{:S(2)}) collective-permute-start(bf16[256,1280]{1,0:T(8,128)(2,1)} %pad_maximum_fusion.5), channel_id=1, source_target_pairs={{0,1},{1,2},{2,3},{3,0},{4,5},{5,6},{6,7},{7,4},{8,9},{9,10},{10,1... | collective-permute-start | bytes 1966088 | tf_op jit(solution)/shard_map/ppermute | solution.py:250
  70.5 63.6 %collective-permute-start.8 = (bf16[256,1280]{1,0:T(8,128)(2,1)}, bf16[256,1280]{1,0:T(8,128)(2,1)}, u32[]{:S(2)}, u32[]{:S(2)}) collective-permute-start(bf16[256,1280]{1,0:T(8,128)(2,1)} %pad_maximum_fusion.3), channel_id=1, source_target_pairs={{0,3},{1,0},{2,1},{3,2},{4,7},{5,4},{6,5},{7,6},{8,11},{9,8},{10,9... | collective-permute-start | bytes 1966088 | tf_op jit(solution)/shard_map/ppermute | solution.py:250
  72.8 61.4 %collective-permute-start.9 = (bf16[256,1280]{1,0:T(8,128)(2,1)}, bf16[256,1280]{1,0:T(8,128)(2,1)}, u32[]{:S(2)}, u32[]{:S(2)}) collective-permute-start(bf16[256,1280]{1,0:T(8,128)(2,1)} %pad_maximum_fusion.4), channel_id=1, source_target_pairs={{0,2},{1,3},{2,0},{3,1},{4,6},{5,7},{6,4},{7,5},{8,10},{9,11},{10,... | collective-permute-start | bytes 1966088 | tf_op jit(solution)/shard_map/ppermute | solution.py:250
  125.0 1.6 collective-permute-start.15
  129.6 56.4 %all-to-all-start.1 = ((bf16[16,128,256]{2,1,0:T(8,128)(2,1)}), bf16[16,128,256]{2,1,0:T(8,128)(2,1)}, u32[]{:S(2)}, u32[]{:S(2)}) async-start(bf16[16,128,256]{2,1,0:T(8,128)(2,1)} %add_convert_fusion.1), calls=%async_computation.1 | async-start | bytes 2097152 | tf_op jit(solution)/shard_map/all_to_all | solution.py:325
  179.8 3.1 %collective-permute-start.16 = (bf16[4,128,256]{2,1,0:T(8,128)(2,1)S(1)}, bf16[4,128,256]{2,1,0:T(8,128)(2,1)S(1)}, u32[]{:S(2)}, u32[]{:S(2)}) collective-permute-start(bf16[4,128,256]{2,1,0:T(8,128)(2,1)S(1)} %get-tuple-element.33), channel_id=1, source_target_pairs={{0,4},{4,0},{1,5},{5,1},{2,6},{6,2},{3,7},{7,3},{8,12},{12,8},{9,1... | collective-permute-start | bytes 786440 | tf_op jit(solution)/shard_map/ppermute | solution.py:254
  180.3 32.0 %collective-permute-start.11 = (bf16[256,1280]{1,0:T(8,128)(2,1)}, bf16[256,1280]{1,0:T(8,128)(2,1)S(1)}, u32[]{:S(2)}, u32[]{:S(2)}) collective-permute-start(bf16[256,1280]{1,0:T(8,128)(2,1)} %get-tuple-element.25), channel_id=1, source_target_pairs={{0,3},{1,0},{2,1},{3,2},{4,7},{5,4},{6,5},{7,6},{8,11},{9,8},{10,9... | collective-permute-start | bytes 1966088 | tf_op jit(solution)/shard_map/ppermute | solution.py:250
  183.0 13.7 %copy-start.12 = (bf16[256,1280]{1,0:T(8,128)(2,1)S(1)}, bf16[256,1280]{1,0:T(8,128)(2,1)}, u32[]{:S(2)}) copy-start(bf16[256,1280]{1,0:T(8,128)(2,1)} %copy-done.11) | copy-start | bytes 1966084
  183.0 29.2 %copy-start.10 = (bf16[256,1280]{1,0:T(8,128)(2,1)S(1)}, bf16[256,1280]{1,0:T(8,128)(2,1)}, u32[]{:S(2)}) copy-start(bf16[256,1280]{1,0:T(8,128)(2,1)} %copy-done.9) | copy-start | bytes 1966084
  186.0 72.7 %all-to-all-start.2 = ((bf16[16,128,256]{2,1,0:T(8,128)(2,1)}), bf16[16,128,256]{2,1,0:T(8,128)(2,1)}, u32[]{:S(2)}, u32[]{:S(2)}) async-start(bf16[16,128,256]{2,1,0:T(8,128)(2,1)} %add_convert_fusion), calls=%async_computation.2 | async-start | bytes 2097152 | tf_op jit(solution)/shard_map/all_to_all | solution.py:325
  192.6 19.6 %collective-permute-start.12 = (bf16[256,1280]{1,0:T(8,128)(2,1)}, bf16[256,1280]{1,0:T(8,128)(2,1)S(1)}, u32[]{:S(2)}, u32[]{:S(2)}) collective-permute-start(bf16[256,1280]{1,0:T(8,128)(2,1)} %copy-done.17), channel_id=1, source_target_pairs={{0,2},{1,3},{2,0},{3,1},{4,6},{5,7},{6,4},{7,5},{8,10},{9,11},{10,... | collective-permute-start | bytes 1966088 | tf_op jit(solution)/shard_map/ppermute | solution.py:250
  193.5 32.7 %collective-permute-start.13 = (bf16[256,1280]{1,0:T(8,128)(2,1)}, bf16[256,1280]{1,0:T(8,128)(2,1)S(1)}, u32[]{:S(2)}, u32[]{:S(2)}) collective-permute-start(bf16[256,1280]{1,0:T(8,128)(2,1)} %copy-done.16), channel_id=1, source_target_pairs={{0,1},{1,2},{2,3},{3,0},{4,5},{5,6},{6,7},{7,4},{8,9},{9,10},{10,1... | collective-permute-start | bytes 1966088 | tf_op jit(solution)/shard_map/ppermute | solution.py:250
  194.9 44.8 %collective-permute-start.5 = (bf16[256,1280]{1,0:T(8,128)(2,1)}, bf16[256,1280]{1,0:T(8,128)(2,1)S(1)}, u32[]{:S(2)}, u32[]{:S(2)}) collective-permute-start(bf16[256,1280]{1,0:T(8,128)(2,1)} %copy-done.13), channel_id=1, source_target_pairs={{0,3},{1,0},{2,1},{3,2},{4,7},{5,4},{6,5},{7,6},{8,11},{9,8},{10,9... | collective-permute-start | bytes 1966088 | tf_op jit(solution)/shard_map/ppermute | solution.py:250
  196.7 43.5 %collective-permute-start.6 = (bf16[256,1280]{1,0:T(8,128)(2,1)S(1)}, bf16[256,1280]{1,0:T(8,128)(2,1)S(1)}, u32[]{:S(2)}, u32[]{:S(2)}) collective-permute-start(bf16[256,1280]{1,0:T(8,128)(2,1)S(1)} %copy-done.12), channel_id=1, source_target_pairs={{0,2},{1,3},{2,0},{3,1},{4,6},{5,7},{6,4},{7,5},{8,10},{9,11},{10,... | collective-permute-start | bytes 1966088 | tf_op jit(solution)/shard_map/ppermute | solution.py:250
  212.3 40.8 %collective-permute-start.7 = (bf16[256,1280]{1,0:T(8,128)(2,1)S(1)}, bf16[256,1280]{1,0:T(8,128)(2,1)S(1)}, u32[]{:S(2)}, u32[]{:S(2)}) collective-permute-start(bf16[256,1280]{1,0:T(8,128)(2,1)S(1)} %copy-done.10), channel_id=1, source_target_pairs={{0,1},{1,2},{2,3},{3,0},{4,5},{5,6},{6,7},{7,4},{8,9},{9,10},{10,1... | collective-permute-start | bytes 1966088 | tf_op jit(solution)/shard_map/ppermute | solution.py:250
  (15 other events, 37.7 us)

commit v2 on v1

--- a/solution.py
+++ b/solution.py
@@ -8,6 +8,7 @@
 from jax.experimental.pallas import tpu as pltpu
 from jax.sharding import Mesh
 from jax.sharding import PartitionSpec as P
+
 
 HD = 128
 SCALE = HD**-0.5
@@ -27,6 +28,7 @@
 GROUP = 4
 QW = GROUP * HD
 PIECE = 2 * QW + 2 * HD
+SPANS = ((0, QW), (QW, QW), (2 * QW, HD), (2 * QW + HD, HD))
 
 
 def mm(a, b, dims):
@@ -193,12 +195,60 @@
             ],
         ),
         out_shape=out_shape,
-        compiler_params=pltpu.CompilerParams(vmem_limit_bytes=24 << 20),
+        compiler_params=pltpu.CompilerParams(vmem_limit_bytes=60 << 20),
         cost_estimate=pl.CostEstimate(
             flops=6 * 2 * pairs * HD * 2, bytes_accessed=6 << 20, transcendentals=pairs
         ),
         name="attn",
     )(scalars, *ops)
+
+
+def split_body(group, y_ref, *refs):
+    ins, outs, bufs, in_sems, out_sems = refs[:4], refs[4:7], refs[7], refs[8], refs[9]
+    me = y_ref[0]
+    loads = []
+    for i in range(TP - 1):
+        src = lax.rem(me + i + 1, TP) * 2 + group
+        row = []
+        for t, (at, width) in enumerate(SPANS):
+            col = pl.multiple_of(src * width, HD)
+            copy = pltpu.make_async_copy(
+                ins[t].at[:, pl.ds(col, width)], bufs.at[i, :, pl.ds(at, width)], in_sems.at[i, t]
+            )
+            copy.start()
+            row.append(copy)
+        loads.append(row)
+    stores = []
+    for i in range(TP - 1):
+        for copy in loads[i]:
+            copy.wait()
+        copy = pltpu.make_async_copy(bufs.at[i], outs[i], out_sems.at[i])
+        copy.start()
+        stores.append(copy)
+    for copy in stores:
+        copy.wait()
+
+
+def split(group, y, own):
+    anyspec = pl.BlockSpec(memory_space=pl.ANY)
+    return pl.pallas_call(
+        functools.partial(split_body, group),
+        grid_spec=pltpu.PrefetchScalarGridSpec(
+            num_scalar_prefetch=1,
+            grid=(),
+            in_specs=[anyspec] * 4,
+            out_specs=[anyspec] * (TP - 1),
+            scratch_shapes=[
+                pltpu.VMEM((TP - 1, CHUNK, PIECE), BF16),
+                pltpu.SemaphoreType.DMA((TP - 1, 4)),
+                pltpu.SemaphoreType.DMA((TP - 1,)),
+            ],
+        ),
+        out_shape=[jax.ShapeDtypeStruct((CHUNK, PIECE), BF16)] * (TP - 1),
+        compiler_params=pltpu.CompilerParams(vmem_limit_bytes=60 << 20),
+        cost_estimate=pl.CostEstimate(flops=0, bytes_accessed=4 << 20, transcendentals=0),
+        name="split",
+    )(y, *own)
 
 
 def place_body(y_ref, *refs):
@@ -213,7 +263,7 @@
         group, d = divmod(i, TP)
         src = lax.rem(me + d, TP) * 2 + group
         loads[i].wait()
-        for t, (at, width) in enumerate(((0, QW), (QW, QW), (2 * QW, HD), (2 * QW + HD, HD))):
+        for t, (at, width) in enumerate(SPANS):
             col = pl.multiple_of(src * width, HD)
             copy = pltpu.make_async_copy(
                 bufs.at[i, :, pl.ds(at, width)], outs[t].at[:, pl.ds(col, width)], out_sems.at[i, t]
@@ -241,7 +291,7 @@
             ],
         ),
         out_shape=[jax.ShapeDtypeStruct((CHUNK, w), BF16) for w in widths],
-        compiler_params=pltpu.CompilerParams(vmem_limit_bytes=16 << 20),
+        compiler_params=pltpu.CompilerParams(vmem_limit_bytes=60 << 20),
         name="place",
     )(y, *pieces)
 
@@ -250,17 +300,18 @@
     return lax.ppermute(x, "y", [(s, (s + step) % TP) for s in range(TP)])
 
 
+def to_chips(x):
+    return lax.all_to_all(x, ("z", "x"), 0, 0, tiled=True)
+
+
 def swap(x):
     return lax.ppermute(x, "core", [(0, 1), (1, 0)])
 
 
-def shards(queries, keys_in, values_in, grad_output, beacon_keys, beacon_values, read_blocks, read_counts):
+def layer(queries, keys_in, values_in, grad_output, beacon_keys, beacon_values, read_blocks, read_counts):
     y = lax.axis_index("y")
     core = lax.axis_index("core")
     chips = lax.axis_size("z") * lax.axis_size("x")
-
-    def cut(a, to, group, width):
-        return lax.dynamic_slice(a, (0, (to * 2 + group) * width), (CHUNK, width))
 
     both = [
         jnp.concatenate(
@@ -276,30 +327,21 @@
     table = jnp.concatenate([row, count])
     peer_table = swap(table)
 
+    own = (queries, grad_output, keys_in, values_in)
+    place_at = y[None].astype(jnp.int32)
     recv = []
     for g in range(2):
         got = {}
+        sent = split(g, place_at, own)
         for d in (1, 3, 2):
-            to = (y + d) % TP
-            piece = jnp.concatenate(
-                [
-                    cut(queries, to, g, QW),
-                    cut(grad_output, to, g, QW),
-                    cut(keys_in, to, g, HD),
-                    cut(values_in, to, g, HD),
-                ],
-                axis=1,
-            )
-            got[TP - d] = shift(piece, d)
+            got[TP - d] = shift(sent[d - 1], d)
         recv.append([got[1], got[2], got[3]])
 
-    near = lax.all_to_all(chip_blocks, ("z", "x"), 0, 0, tiled=True)
+    near = to_chips(chip_blocks)
     far = swap(near).reshape(chips * 2, BLOCK, 2 * HD)
     near = near.reshape(chips * 2, BLOCK, 2 * HD)
 
-    own = (queries, grad_output, keys_in, values_in)
     chip, parity = row // 2, row % 2
-    tables = [table, peer_table]
     back, beacs = [], []
     for g in range(2):
         scalars = jnp.concatenate(
@@ -322,9 +364,9 @@
             for j in range(SLOTS):
                 use = (tab[j] == ids * 2 + core) & (j < tab[SLOTS])
                 dense = dense + jnp.where(use[:, None, None], terms[j].astype(F32)[None], 0.0)
-        parts = lax.all_to_all(dense.astype(BF16), ("z", "x"), 0, 0, tiled=True)
+        parts = to_chips(dense.astype(BF16))
         beacs.append(jnp.sum(parts.astype(F32), axis=0).astype(BF16))
-    out, dq, dk, dv = place(y[None].astype(jnp.int32), back[0] + back[1])
+    out, dq, dk, dv = place(place_at, back[0] + back[1])
     dbk = jnp.concatenate([b[:, :HD] for b in beacs], axis=1)
     dbv = jnp.concatenate([b[:, HD:] for b in beacs], axis=1)
     return out, dq, dk, dv, dbk, dbv
@@ -337,4 +379,4 @@
     beacon = P(ctx, "y")
     in_specs = (tokens,) * 4 + (beacon,) * 2 + (P(ctx, None), P(ctx))
     out_specs = (tokens,) * 4 + (beacon,) * 2
-    return jax.shard_map(shards, mesh=split, in_specs=in_specs, out_specs=out_specs, check_vma=False)
+    return jax.shard_map(layer, mesh=split, in_specs=in_specs, out_specs=out_specs, check_vma=False)

time: 263 us -> 253 us (0.962)
  blocking collectives: 0 us -> 36.5 us
  waiting for transfers between devices: 90.6 us -> 68.9 us
  local copies, waits for them, and re-layouts: 17.9 us -> 4.39 us
  other arithmetic: 26.2 us -> 14.6 us
  Pallas kernels: 84.4 us -> 93.4 us
  starting transfers between devices: 37.8 us -> 29.4 us
    all_to_all x0 -> x1, blocking collectives: none -> 36.5 us  [to_chips(): return lax.all_to_all(x, ('z', 'x'), 0, 0, tiled=True)]
    all_to_all x3 -> x2, waiting for transfers between devices: 26.3 us -> 0.01 us  [to_chips(): return lax.all_to_all(x, ('z', 'x'), 0, 0, tiled=True)]
    concatenate x9 -> x3, other arithmetic: 12.2 us -> 1.36 us  [the longest x1 0.64 us: layer(): dbv = jnp.concatenate([b[:, HD:] for b in beacs], axis=1)]
    unnamed x38 -> x12, local copies, waits for them, and re-layouts: 9.85 us -> 0.83 us
    all_to_all x3 -> x2, starting transfers between devices: 19.3 us -> 10.5 us  [to_chips(): return lax.all_to_all(x, ('z', 'x'), 0, 0, tiled=True)]
    pallas_call x0 -> x2, Pallas kernels: none -> 5.66 us  [split(): pl.pallas_call(functools.partial(split_body, group), grid_spec=pltpu.Pref...]
    ppermute x12, waiting for transfers between devices: 62.9 us -> 67.7 us  [shift(): return lax.ppermute(x, 'y', [(s, (s + step) % TP) for s in range(TP)])]
    dynamic_slice x2 -> x0, local copies, waits for them, and re-layouts: 4.2 us -> none  [cut(): return lax.dynamic_slice(a, (0, (to * 2 + group) * width), (CHUNK, width))]
  transfers between devices with their start and end apart: 20 -> 19, of which waited for: 9 -> 9; matrix products, arithmetic and copies ran while one was open for 11% -> 6% of each run, Pallas kernels for 32% -> 37%
where the time goes in v2:
time: 253 us; the launch traced here: 251 us
  Pallas kernels  93.4 us (37%)
  waiting for transfers between devices  68.9 us (27%)
  blocking collectives  36.5 us (14%)
  starting transfers between devices  29.4 us (12%)
  other arithmetic  14.6 us (6%)
  local copies, waits for them, and re-layouts  4.39 us (2%)
  between operations  4.04 us (2%)
    pallas_call x2, Pallas kernels, attn(): pl.pallas_call(attn_body, grid_spec=pltpu.PrefetchScalarGridSpec(num_scal...  82.9 us
    ppermute x12, waiting for transfers between devices, shift(): return lax.ppermute(x, 'y', [(s, (s + step) % TP) for s in range(TP)])  67.7 us
    all_to_all x1, blocking collectives, to_chips(): return lax.all_to_all(x, ('z', 'x'), 0, 0, tiled=True)  36.5 us
    ppermute x12, starting transfers between devices, shift(): return lax.ppermute(x, 'y', [(s, (s + step) % TP) for s in range(TP)])  18.2 us
    all_to_all x2, starting transfers between devices, to_chips(): return lax.all_to_all(x, ('z', 'x'), 0, 0, tiled=True)  10.5 us
    convert_element_type x2, other arithmetic, layer(): parts = to_chips(dense.astype(BF16))  5.84 us
    pallas_call x2, Pallas kernels, split(): pl.pallas_call(functools.partial(split_body, group), grid_spec=pltpu.Pref...  5.66 us
  transfers between devices with their start and end apart: 19, of which 9 were waited for; matrix products, arithmetic and copies ran while one was open for 6% of the time, Pallas kernels for 37%

profile of v2, /device:TPU:0, one launch (start us, length us, event | category | flops | bytes accessed | tf_op | source)
XLA Modules:
  0.0 251.2 jit_solution(2698317273501185939)
XLA Ops:
  3.1 36.5 %all_to_all.15 = bf16[16,2,128,256]{3,2,1,0:T(8,128)(2,1)S(1)} all-to-all(bf16[16,2,128,256]{3,2,1,0:T(8,128)(2,1)S(1)} %broadcast_in_dim.307), channel_id=1, replica_groups=mesh['z'=4,'x'=4,'core'=2,'y'=4] {'z','x'}, dimensions={0} | all-to-all | bytes 4194304 | tf_op jit(solution)/shard_map/all_to_all | solution.py:304
  39.6 3.2 %split.2 = (bf16[256,1280]{1,0:T(8,128)(2,1)}, bf16[256,1280]{1,0:T(8,128)(2,1)}, bf16[256,1280]{1,0:T(8,128)(2,1)}) custom-call(s32[1]{0:T(128)} %bitcast.y_ref, bf16[256,4096]{1,0:T(8,128)(2,1)} %refs_0_.7, bf16[256,4096]{1,0:T(8,128)(2,1)} %refs_1_.7, bf16[256,1024]{1,0:T(8,128)(2,1)} %refs_2_.7, bf16[256,1024]{1,0:T(8,128)(2,1)} %refs_3_.7), custom_call_target="tpu_custom_call" | custom-call | bytes 4194304 | tf_op jit(solution)/shard_map/split/pallas_call | solution.py:234
  42.8 3.1 %collective-permute-start = (bf16[256,1280]{1,0:T(8,128)(2,1)}, bf16[256,1280]{1,0:T(8,128)(2,1)S(1)}, u32[]{:S(2)}, u32[]{:S(2)}) collective-permute-start(bf16[256,1280]{1,0:T(8,128)(2,1)} %get-tuple-element.26), channel_id=1, source_target_pairs={{0,3},{1,0},{2,1},{3,2},{4,7},{5,4},{6,5},{7,6},{8,11},{9,8},{10,9... | collective-permute-start | bytes 1966088 | tf_op jit(solution)/shard_map/ppermute | solution.py:300
  48.3 2.4 split.3
  52.7 1.2 compare_and_fusion.4
  53.9 1.3 compare_and_fusion.6
  55.2 2.0 collective-permute-start.10
  61.5 12.8 %collective-permute-done.refs_4_.refs_5_.refs_6_.refs_7_ = bf16[256,1280]{1,0:T(8,128)(2,1)S(1)} collective-permute-done((bf16[256,1280]{1,0:T(8,128)(2,1)}, bf16[256,1280]{1,0:T(8,128)(2,1)S(1)}, u32[]{:S(2)}, u32[]{:S(2)}) %collective-permute-start) | collective-permute-done | bytes 655392 | tf_op jit(solution)/shard_map/ppermute | solution.py:300
  74.2 3.6 %collective-permute-start.8 = (bf16[256,1280]{1,0:T(8,128)(2,1)}, bf16[256,1280]{1,0:T(8,128)(2,1)}, u32[]{:S(2)}, u32[]{:S(2)}) collective-permute-start(bf16[256,1280]{1,0:T(8,128)(2,1)} %get-tuple-element.33), channel_id=1, source_target_pairs={{0,3},{1,0},{2,1},{3,2},{4,7},{5,4},{6,5},{7,6},{8,11},{9,8},{10,9... | collective-permute-start | bytes 1966088 | tf_op jit(solution)/shard_map/ppermute | solution.py:300
  78.0 41.4 %attn.2 = (bf16[256,1280]{1,0:T(8,128)(2,1)}, bf16[256,1280]{1,0:T(8,128)(2,1)}, bf16[256,1280]{1,0:T(8,128)(2,1)}, bf16[256,1280]{1,0:T(8,128)(2,1)}, bf16[4,128,256]{2,1,0:T(8,128)(2,1)}) custom-call(s32[11]{0:T(128)} %concatenate.47.sc, bf16[256,4096]{1,0:T(8,128)(2,1)} %refs_0_.7, bf16[256,4096]{1,0:T(8,128)(2,1)} %refs_1_.7, bf16[256,1024]{1,0:T(8,128)(2,1)} %refs_2_.7, ...), custom_call_target="tpu_custom_call" | custom-call | flops 14495514624 | bytes 6291456 | tf_op jit(solution)/shard_map/attn/pallas_call | solution.py:177
  121.7 2.9 %add_convert_fusion.1 = bf16[16,128,256]{2,1,0:T(8,128)(2,1)} fusion(f32[128,256]{1,0:T(8,128)S(1)} %get-tuple-element.54, f32[128,256]{1,0:T(8,128)S(1)} %get-tuple-element.55, f32[128,256]{1,0:T(8,128)S(1)} %get-tuple-element.56, f32[128,256]{1,0:T(8,128)S(1)} %get-tuple-element.53, f32[128,256]{1,0:T(8,128)S(1)} %get-tuple-element.50, ...), kind=kLoop, calls=%fused_computation.1 | loop fusion | flops 8388608 | bytes 2097280 | tf_op jit(solution)/shard_map/convert_element_type | solution.py:367
  124.7 3.9 %all-to-all-start.1 = ((bf16[16,128,256]{2,1,0:T(8,128)(2,1)}), bf16[16,128,256]{2,1,0:T(8,128)(2,1)S(1)}, u32[]{:S(2)}, u32[]{:S(2)}) async-start(bf16[16,128,256]{2,1,0:T(8,128)(2,1)} %add_convert_fusion.1), calls=%async_computation.1 | async-start | bytes 2097152 | tf_op jit(solution)/shard_map/all_to_all | solution.py:304
  129.4 41.5 %attn.3 = (bf16[256,1280]{1,0:T(8,128)(2,1)}, bf16[256,1280]{1,0:T(8,128)(2,1)}, bf16[256,1280]{1,0:T(8,128)(2,1)}, bf16[256,1280]{1,0:T(8,128)(2,1)}, bf16[4,128,256]{2,1,0:T(8,128)(2,1)}) custom-call(s32[11]{0:T(128)} %concatenate.56.sc, bf16[256,4096]{1,0:T(8,128)(2,1)} %refs_0_.7, bf16[256,4096]{1,0:T(8,128)(2,1)} %refs_1_.7, bf16[256,1024]{1,0:T(8,128)(2,1)} %refs_2_.7, ...), custom_call_target="tpu_custom_call" | custom-call | flops 14495514624 | bytes 6291456 | tf_op jit(solution)/shard_map/attn/pallas_call | solution.py:177
  171.4 2.3 collective-permute-start.11
  174.8 2.9 %add_convert_fusion = bf16[16,128,256]{2,1,0:T(8,128)(2,1)} fusion(f32[128,256]{1,0:T(8,128)S(1)} %get-tuple-element.62, f32[128,256]{1,0:T(8,128)S(1)} %get-tuple-element.63, f32[128,256]{1,0:T(8,128)S(1)} %get-tuple-element.64, f32[128,256]{1,0:T(8,128)S(1)} %get-tuple-element.61, f32[128,256]{1,0:T(8,128)S(1)} %get-tuple-element.58, ...), kind=kLoop, calls=%fused_computation | loop fusion | flops 8388608 | bytes 2097280 | tf_op jit(solution)/shard_map/convert_element_type | solution.py:367
  177.7 6.6 %all-to-all-start.2 = ((bf16[16,128,256]{2,1,0:T(8,128)(2,1)}), bf16[16,128,256]{2,1,0:T(8,128)(2,1)S(1)}, u32[]{:S(2)}, u32[]{:S(2)}) async-start(bf16[16,128,256]{2,1,0:T(8,128)(2,1)} %add_convert_fusion), calls=%async_computation.2 | async-start | bytes 2097152 | tf_op jit(solution)/shard_map/all_to_all | solution.py:304
  184.4 1.9 collective-permute-start.12
  187.1 2.4 collective-permute-start.5
  190.0 13.1 %collective-permute-done.11.refs_5_ = bf16[256,1280]{1,0:T(8,128)(2,1)S(1)} collective-permute-done((bf16[256,1280]{1,0:T(8,128)(2,1)}, bf16[256,1280]{1,0:T(8,128)(2,1)S(1)}, u32[]{:S(2)}, u32[]{:S(2)}) %collective-permute-start.11) | collective-permute-done | bytes 655392 | tf_op jit(solution)/shard_map/ppermute | solution.py:300
  203.8 14.2 %collective-permute-done.13.refs_7_ = bf16[256,1280]{1,0:T(8,128)(2,1)} collective-permute-done((bf16[256,1280]{1,0:T(8,128)(2,1)}, bf16[256,1280]{1,0:T(8,128)(2,1)}, u32[]{:S(2)}, u32[]{:S(2)}) %collective-permute-start.13) | collective-permute-done | bytes 655392 | tf_op jit(solution)/shard_map/ppermute | solution.py:300
  218.0 12.5 %collective-permute-done.5.refs_1_ = bf16[256,1280]{1,0:T(8,128)(2,1)} collective-permute-done((bf16[256,1280]{1,0:T(8,128)(2,1)}, bf16[256,1280]{1,0:T(8,128)(2,1)}, u32[]{:S(2)}, u32[]{:S(2)}) %collective-permute-start.5) | collective-permute-done | bytes 655392 | tf_op jit(solution)/shard_map/ppermute | solution.py:300
  230.5 1.5 collective-permute-done.6.refs_2_
  232.0 12.7 %collective-permute-done.7.refs_3_ = bf16[256,1280]{1,0:T(8,128)(2,1)} collective-permute-done((bf16[256,1280]{1,0:T(8,128)(2,1)}, bf16[256,1280]{1,0:T(8,128)(2,1)}, u32[]{:S(2)}, u32[]{:S(2)}) %collective-permute-start.7) | collective-permute-done | bytes 655392 | tf_op jit(solution)/shard_map/ppermute | solution.py:300
  244.8 4.8 %place.1 = (bf16[256,4096]{1,0:T(8,128)(2,1)}, bf16[256,4096]{1,0:T(8,128)(2,1)}, bf16[256,1024]{1,0:T(8,128)(2,1)}, bf16[256,1024]{1,0:T(8,128)(2,1)}) custom-call(s32[1]{0:T(128)} %bitcast.y_ref, bf16[256,1280]{1,0:T(8,128)(2,1)} %get-tuple-element.29.refs_0_, bf16[256,1280]{1,0:T(8,128)(2,1)} %collective-permute-done.5.refs_1_, ...), custom_call_target="tpu_custom_call" | custom-call | tf_op jit(solution)/shard_map/place/pallas_call | solution.py:280
  (60 shorter events, 16.5 us)
Async XLA Ops:
  1.5 1.3 collective-permute-start.3
  39.6 3.2 %copy-start = (bf16[16,2,128,256]{3,2,1,0:T(8,128)(2,1)}, bf16[16,2,128,256]{3,2,1,0:T(8,128)(2,1)S(1)}, u32[]{:S(2)}) copy-start(bf16[16,2,128,256]{3,2,1,0:T(8,128)(2,1)S(1)} %all_to_all.15) | copy-start | bytes 6291460
  39.6 38.4 %collective-permute-start.4 = (bf16[16,2,128,256]{3,2,1,0:T(8,128)(2,1)S(1)}, bf16[16,2,128,256]{3,2,1,0:T(8,128)(2,1)}, u32[]{:S(2)}, u32[]{:S(2)}) collective-permute-start(bf16[16,2,128,256]{3,2,1,0:T(8,128)(2,1)S(1)} %all_to_all.15), channel_id=1, source_target_pairs={{0,4},{4,0},{1,5},{5,1},{2,6},{6,2},{3,7},{7,3},{8,12},{12,8},{9,1... | collective-permute-start | bytes 6291464 | tf_op jit(solution)/shard_map/ppermute | solution.py:308
  39.6 8.6 %copy-start.3 = (s32[1,4]{1,0:T(1,128)S(1)}, s32[1,4]{1,0:T(1,128)}, u32[]{:S(2)}) copy-start(s32[1,4]{1,0:T(1,128)} %param.14) | copy-start | bytes 52
  42.8 31.4 %collective-permute-start = (bf16[256,1280]{1,0:T(8,128)(2,1)}, bf16[256,1280]{1,0:T(8,128)(2,1)S(1)}, u32[]{:S(2)}, u32[]{:S(2)}) collective-permute-start(bf16[256,1280]{1,0:T(8,128)(2,1)} %get-tuple-element.26), channel_id=1, source_target_pairs={{0,3},{1,0},{2,1},{3,2},{4,7},{5,4},{6,5},{7,6},{8,11},{9,8},{10,9... | collective-permute-start | bytes 1966088 | tf_op jit(solution)/shard_map/ppermute | solution.py:300
  45.9 31.9 %collective-permute-start.1 = (bf16[256,1280]{1,0:T(8,128)(2,1)}, bf16[256,1280]{1,0:T(8,128)(2,1)}, u32[]{:S(2)}, u32[]{:S(2)}) collective-permute-start(bf16[256,1280]{1,0:T(8,128)(2,1)} %get-tuple-element.27), channel_id=1, source_target_pairs={{0,2},{1,3},{2,0},{3,1},{4,6},{5,7},{6,4},{7,5},{8,10},{9,11},{10,... | collective-permute-start | bytes 1966088 | tf_op jit(solution)/shard_map/ppermute | solution.py:300
  46.6 31.4 %collective-permute-start.2 = (bf16[256,1280]{1,0:T(8,128)(2,1)}, bf16[256,1280]{1,0:T(8,128)(2,1)}, u32[]{:S(2)}, u32[]{:S(2)}) collective-permute-start(bf16[256,1280]{1,0:T(8,128)(2,1)} %get-tuple-element.28), channel_id=1, source_target_pairs={{0,1},{1,2},{2,3},{3,0},{4,5},{5,6},{6,7},{7,4},{8,9},{9,10},{10,1... | collective-permute-start | bytes 1966088 | tf_op jit(solution)/shard_map/ppermute | solution.py:300
  48.3 6.9 %collective-permute-start.14 = (s32[5]{0:T(128)S(1)}, s32[5]{0:T(128)S(1)}, u32[]{:S(2)}, u32[]{:S(2)}) collective-permute-start(s32[5]{0:T(128)S(1)} %pad_add_fusion), channel_id=1, source_target_pairs={{0,4},{4,0},{1,5},{5,1},{2,6},{6,2},{3,7},{7,3},{8,12},{12,8},{9,1... | collective-permute-start | bytes 68 | tf_op jit(solution)/shard_map/ppermute | solution.py:308
  55.2 73.3 %collective-permute-start.10 = (bf16[256,1280]{1,0:T(8,128)(2,1)}, bf16[256,1280]{1,0:T(8,128)(2,1)S(1)}, u32[]{:S(2)}, u32[]{:S(2)}) collective-permute-start(bf16[256,1280]{1,0:T(8,128)(2,1)} %get-tuple-element.35), channel_id=1, source_target_pairs={{0,1},{1,2},{2,3},{3,0},{4,5},{5,6},{6,7},{7,4},{8,9},{9,10},{10,1... | collective-permute-start | bytes 1966088 | tf_op jit(solution)/shard_map/ppermute | solution.py:300
  74.2 3.8 %copy-start.5 = (bf16[256,1280]{1,0:T(8,128)(2,1)}, bf16[256,1280]{1,0:T(8,128)(2,1)S(1)}, u32[]{:S(2)}) copy-start(bf16[256,1280]{1,0:T(8,128)(2,1)S(1)} %collective-permute-done.refs_4_.refs_5_.refs_6_.refs_7_) | copy-start | bytes 1966084
  74.2 54.3 %collective-permute-start.8 = (bf16[256,1280]{1,0:T(8,128)(2,1)}, bf16[256,1280]{1,0:T(8,128)(2,1)}, u32[]{:S(2)}, u32[]{:S(2)}) collective-permute-start(bf16[256,1280]{1,0:T(8,128)(2,1)} %get-tuple-element.33), channel_id=1, source_target_pairs={{0,3},{1,0},{2,1},{3,2},{4,7},{5,4},{6,5},{7,6},{8,11},{9,8},{10,9... | collective-permute-start | bytes 1966088 | tf_op jit(solution)/shard_map/ppermute | solution.py:300
  77.8 50.8 %collective-permute-start.9 = (bf16[256,1280]{1,0:T(8,128)(2,1)}, bf16[256,1280]{1,0:T(8,128)(2,1)}, u32[]{:S(2)}, u32[]{:S(2)}) collective-permute-start(bf16[256,1280]{1,0:T(8,128)(2,1)} %get-tuple-element.34), channel_id=1, source_target_pairs={{0,2},{1,3},{2,0},{3,1},{4,6},{5,7},{6,4},{7,5},{8,10},{9,11},{10,... | collective-permute-start | bytes 1966088 | tf_op jit(solution)/shard_map/ppermute | solution.py:300
  119.4 2.3 collective-permute-start.15
  124.7 53.1 %all-to-all-start.1 = ((bf16[16,128,256]{2,1,0:T(8,128)(2,1)}), bf16[16,128,256]{2,1,0:T(8,128)(2,1)S(1)}, u32[]{:S(2)}, u32[]{:S(2)}) async-start(bf16[16,128,256]{2,1,0:T(8,128)(2,1)} %add_convert_fusion.1), calls=%async_computation.1 | async-start | bytes 2097152 | tf_op jit(solution)/shard_map/all_to_all | solution.py:304
  170.9 3.8 %collective-permute-start.16 = (bf16[4,128,256]{2,1,0:T(8,128)(2,1)}, bf16[4,128,256]{2,1,0:T(8,128)(2,1)S(1)}, u32[]{:S(2)}, u32[]{:S(2)}) collective-permute-start(bf16[4,128,256]{2,1,0:T(8,128)(2,1)} %get-tuple-element.45), channel_id=1, source_target_pairs={{0,4},{4,0},{1,5},{5,1},{2,6},{6,2},{3,7},{7,3},{8,12},{12,8},{9,1... | collective-permute-start | bytes 786440 | tf_op jit(solution)/shard_map/ppermute | solution.py:308
  171.4 31.7 %collective-permute-start.11 = (bf16[256,1280]{1,0:T(8,128)(2,1)}, bf16[256,1280]{1,0:T(8,128)(2,1)S(1)}, u32[]{:S(2)}, u32[]{:S(2)}) collective-permute-start(bf16[256,1280]{1,0:T(8,128)(2,1)} %get-tuple-element.37), channel_id=1, source_target_pairs={{0,3},{1,0},{2,1},{3,2},{4,7},{5,4},{6,5},{7,6},{8,11},{9,8},{10,9... | collective-permute-start | bytes 1966088 | tf_op jit(solution)/shard_map/ppermute | solution.py:300
  177.7 72.0 %all-to-all-start.2 = ((bf16[16,128,256]{2,1,0:T(8,128)(2,1)}), bf16[16,128,256]{2,1,0:T(8,128)(2,1)S(1)}, u32[]{:S(2)}, u32[]{:S(2)}) async-start(bf16[16,128,256]{2,1,0:T(8,128)(2,1)} %add_convert_fusion), calls=%async_computation.2 | async-start | bytes 2097152 | tf_op jit(solution)/shard_map/all_to_all | solution.py:304
  184.4 19.4 %collective-permute-start.12 = (bf16[256,1280]{1,0:T(8,128)(2,1)}, bf16[256,1280]{1,0:T(8,128)(2,1)S(1)}, u32[]{:S(2)}, u32[]{:S(2)}) collective-permute-start(bf16[256,1280]{1,0:T(8,128)(2,1)} %get-tuple-element.38), channel_id=1, source_target_pairs={{0,2},{1,3},{2,0},{3,1},{4,6},{5,7},{6,4},{7,5},{8,10},{9,11},{10,... | collective-permute-start | bytes 1966088 | tf_op jit(solution)/shard_map/ppermute | solution.py:300
  186.2 31.8 %collective-permute-start.13 = (bf16[256,1280]{1,0:T(8,128)(2,1)}, bf16[256,1280]{1,0:T(8,128)(2,1)}, u32[]{:S(2)}, u32[]{:S(2)}) collective-permute-start(bf16[256,1280]{1,0:T(8,128)(2,1)} %get-tuple-element.39), channel_id=1, source_target_pairs={{0,1},{1,2},{2,3},{3,0},{4,5},{5,6},{6,7},{7,4},{8,9},{9,10},{10,1... | collective-permute-start | bytes 1966088 | tf_op jit(solution)/shard_map/ppermute | solution.py:300
  187.1 43.4 %collective-permute-start.5 = (bf16[256,1280]{1,0:T(8,128)(2,1)}, bf16[256,1280]{1,0:T(8,128)(2,1)}, u32[]{:S(2)}, u32[]{:S(2)}) collective-permute-start(bf16[256,1280]{1,0:T(8,128)(2,1)} %get-tuple-element.30), channel_id=1, source_target_pairs={{0,3},{1,0},{2,1},{3,2},{4,7},{5,4},{6,5},{7,6},{8,11},{9,8},{10,9... | collective-permute-start | bytes 1966088 | tf_op jit(solution)/shard_map/ppermute | solution.py:300
  189.5 42.6 %collective-permute-start.6 = (bf16[256,1280]{1,0:T(8,128)(2,1)}, bf16[256,1280]{1,0:T(8,128)(2,1)}, u32[]{:S(2)}, u32[]{:S(2)}) collective-permute-start(bf16[256,1280]{1,0:T(8,128)(2,1)} %get-tuple-element.31), channel_id=1, source_target_pairs={{0,2},{1,3},{2,0},{3,1},{4,6},{5,7},{6,4},{7,5},{8,10},{9,11},{10,... | collective-permute-start | bytes 1966088 | tf_op jit(solution)/shard_map/ppermute | solution.py:300
  203.1 41.7 %copy-start.1 = (bf16[256,1280]{1,0:T(8,128)(2,1)}, bf16[256,1280]{1,0:T(8,128)(2,1)S(1)}, u32[]{:S(2)}) copy-start(bf16[256,1280]{1,0:T(8,128)(2,1)S(1)} %collective-permute-done.11.refs_5_) | copy-start | bytes 1966084
  203.1 41.7 %collective-permute-start.7 = (bf16[256,1280]{1,0:T(8,128)(2,1)}, bf16[256,1280]{1,0:T(8,128)(2,1)}, u32[]{:S(2)}, u32[]{:S(2)}) collective-permute-start(bf16[256,1280]{1,0:T(8,128)(2,1)} %get-tuple-element.32), channel_id=1, source_target_pairs={{0,1},{1,2},{2,3},{3,0},{4,5},{5,6},{6,7},{7,4},{8,9},{9,10},{10,1... | collective-permute-start | bytes 1966088 | tf_op jit(solution)/shard_map/ppermute | solution.py:300
  203.8 41.0 %copy-start.2 = (bf16[256,1280]{1,0:T(8,128)(2,1)}, bf16[256,1280]{1,0:T(8,128)(2,1)S(1)}, u32[]{:S(2)}) copy-start(bf16[256,1280]{1,0:T(8,128)(2,1)S(1)} %collective-permute-done.12.refs_6_) | copy-start | bytes 1966084
  (1 other events, 0.8 us)

commit v3 on v2

--- a/solution.py
+++ b/solution.py
@@ -18,7 +18,6 @@
 BF16 = jnp.bfloat16
 NN = (((1,), (0,)), ((), ()))
 NT = (((1,), (1,)), ((), ()))
-TN = (((0,), (0,)), ((), ()))
 TP = 4
 CHUNK = 256
 SLOTS = 4
@@ -39,51 +38,75 @@
     return op(x.reshape(x.shape[0] // 8, 8, x.shape[1]), axis=0)
 
 
-def chunk_grads(chunk, q, go, keys, vals, bias, scores, dk_acc, dv_acc):
+def chunk_steps(chunk, q_ref, go_ref, o_ref, dq_ref, keys, vals, keys_t, vals_t, bias, scores, probs, dscores):
     blocks = BEAC // CHUNK + chunk + 1
-    peak = None
-    for b in range(blocks):
-        rows = pl.ds(b * CHUNK, CHUNK)
-        s = mm(keys[rows, :], q, NT)
+    depth = blocks * CHUNK
+    cols = slice(chunk * CHUNK, (chunk + 1) * CHUNK)
+    scores = scores.at[chunk]
+    held = {}
+
+    def at(b):
+        return pl.ds(b * CHUNK, CHUNK)
+
+    def score(b):
+        s = mm(keys[at(b), :], q_ref[chunk], NT)
         if b < BEAC // CHUNK:
-            part = bias[rows, :]
+            part = bias[at(b), :]
             s = s + jnp.concatenate([part, part], axis=1)
         if b == blocks - 1:
             key_pos = lax.broadcasted_iota(jnp.int32, (CHUNK, CHUNK), 0)
             query_pos = lax.broadcasted_iota(jnp.int32, (CHUNK, CHUNK), 1)
             s = jnp.where(key_pos <= query_pos, s, NEG)
-        scores[rows, :] = s
+        scores[at(b), :] = s
         top = fold(s, jnp.max)
-        peak = top if peak is None else jnp.maximum(peak, top)
-    shift = jnp.max(peak, axis=0, keepdims=True) * SCALE2
-    total = jnp.zeros((8, CHUNK), F32)
-    for b in range(blocks):
-        rows = pl.ds(b * CHUNK, CHUNK)
-        w = jnp.exp2(scores[rows, :] * SCALE2 - shift)
-        total = total + fold(w, jnp.sum)
-        scores[rows, :] = w
-    inv = 1.0 / jnp.sum(total, axis=0, keepdims=True)
-    out = jnp.zeros((CHUNK, HD), F32)
-    for b in range(blocks):
-        rows = pl.ds(b * CHUNK, CHUNK)
-        p = scores[rows, :] * inv
-        scores[rows, :] = p
-        pb = p.astype(BF16)
-        dv_acc[rows, :] += mm(pb, go, NN)
-        out = out + mm(pb, vals[rows, :], TN)
-    out = out.astype(BF16)
-    prod = go.astype(F32) * out.astype(F32)
-    delta = lax.dot_general(
-        jnp.ones((8, HD), F32), prod, NT, precision=lax.Precision.HIGHEST, preferred_element_type=F32
-    )[0:1, :]
-    dq = jnp.zeros((CHUNK, HD), F32)
-    for b in range(blocks):
-        rows = pl.ds(b * CHUNK, CHUNK)
-        dp = mm(vals[rows, :], go, NT)
-        ds = (scores[rows, :] * (dp - delta)).astype(BF16)
-        dk_acc[rows, :] += mm(ds, q, NN)
-        dq = dq + mm(ds, keys[rows, :], TN)
-    return out, (dq * SCALE).astype(BF16)
+        held["top"] = top if b == 0 else jnp.maximum(held["top"], top)
+
+    def peak():
+        held["shift"] = jnp.max(held["top"], axis=0, keepdims=True) * SCALE2
+        held["sum"] = jnp.zeros((8, CHUNK), F32)
+
+    def weigh(b):
+        w = jnp.exp2(scores[at(b), :] * SCALE2 - held["shift"])
+        held["sum"] = held["sum"] + fold(w, jnp.sum)
+        scores[at(b), :] = w
+
+    def invert():
+        held["inv"] = 1.0 / jnp.sum(held["sum"], axis=0, keepdims=True)
+
+    def normal(b):
+        p = scores[at(b), :] * held["inv"]
+        scores[at(b), :] = p
+        probs[at(b), cols] = p.astype(BF16)
+
+    def attend():
+        out = mm(vals_t[:, :depth], probs[:depth, cols], NN).T.astype(BF16)
+        o_ref[chunk] = out
+        prod = go_ref[chunk].astype(F32) * out.astype(F32)
+        held["delta"] = lax.dot_general(
+            jnp.ones((8, HD), F32), prod, NT, precision=lax.Precision.HIGHEST, preferred_element_type=F32
+        )[0:1, :]
+
+    def dscore(b):
+        dp = mm(vals[at(b), :], go_ref[chunk], NT)
+        dscores[at(b), cols] = (scores[at(b), :] * (dp - held["delta"])).astype(BF16)
+
+    def dquery():
+        dq_ref[chunk] = (mm(keys_t[:, :depth], dscores[:depth, cols], NN).T * SCALE).astype(BF16)
+
+    each = range(blocks)
+    steps = [functools.partial(score, b) for b in each] + [peak]
+    steps += [functools.partial(weigh, b) for b in each] + [invert]
+    steps += [functools.partial(normal, b) for b in each] + [attend]
+    return steps + [functools.partial(dscore, b) for b in each] + [dquery]
+
+
+def interleave(sequences, lag):
+    items, start = [], 0.0
+    for n, steps in enumerate(sequences):
+        items += [(start + t, n, step) for t, step in enumerate(steps)]
+        start += lag * len(steps)
+    for _, _, step in sorted(items, key=lambda item: item[:2]):
+        step()
 
 
 S_A, S_B, S_COUNT, S_Y, S_SAME = 0, 4, 8, 9, 10
@@ -95,7 +118,7 @@
     near, far = refs[: 2 * SLOTS], refs[2 * SLOTS : 4 * SLOTS]
     refs = refs[4 * SLOTS :]
     outs, beac_out = refs[:TP], refs[TP]
-    qs, gs, os, dqs, keys, vals, bias, scores, dk_acc, dv_acc = refs[TP + 1 :]
+    qs, gs, os, dqs, keys, vals, keys_t, vals_t, bias, scores, probs, dscores, dk_acc, dv_acc = refs[TP + 1 :]
     head = pl.program_id(0)
     me = sc[S_Y]
 
@@ -112,6 +135,8 @@
         for j in range(SLOTS):
             row = jnp.where(j < sc[S_COUNT], 0.0, NEG)
             bias[pl.ds(j * BLOCK, BLOCK), :] = jnp.full((BLOCK, HD), row, F32)
+        keys_t[...] = keys[...].T
+        vals_t[...] = vals[...].T
         dk_acc[...] = jnp.zeros_like(dk_acc)
         dv_acc[...] = jnp.zeros_like(dv_acc)
 
@@ -119,10 +144,15 @@
         at = lax.rem(me + d, TP)
         qs[at] = pieces[d][0][...]
         gs[at] = pieces[d][1][...]
-    for i in range(TP):
-        o, dq = chunk_grads(i, qs[i], gs[i], keys, vals, bias, scores, dk_acc, dv_acc)
-        os[i] = o
-        dqs[i] = dq
+    tables = (keys, vals, keys_t, vals_t, bias, scores, probs, dscores)
+    interleave([chunk_steps(i, qs, gs, os, dqs, *tables) for i in range(TP)], 0.3)
+    q_all = qs[...].reshape(TP * CHUNK, HD)
+    go_all = gs[...].reshape(TP * CHUNK, HD)
+    for b in range(KEYS // CHUNK):
+        rows = pl.ds(b * CHUNK, CHUNK)
+        first = max(0, b - BEAC // CHUNK) * CHUNK
+        dv_acc[rows, :] += mm(probs[rows, first:], go_all[first:], NN)
+        dk_acc[rows, :] += mm(dscores[rows, first:], q_all[first:], NN)
     at_o = pl.multiple_of(head * HD, HD)
     at_q = pl.multiple_of(QW + head * HD, HD)
     for d in range(TP):
@@ -188,8 +218,12 @@
                 pltpu.VMEM((TP, CHUNK, HD), BF16),
                 pltpu.VMEM((KEYS, HD), BF16),
                 pltpu.VMEM((KEYS, HD), BF16),
+                pltpu.VMEM((HD, KEYS), BF16),
+                pltpu.VMEM((HD, KEYS), BF16),
                 pltpu.VMEM((BEAC, HD), F32),
-                pltpu.VMEM((KEYS, CHUNK), F32),
+                pltpu.VMEM((TP, KEYS, CHUNK), F32),
+                pltpu.VMEM((KEYS, TP * CHUNK), BF16),
+                pltpu.VMEM((KEYS, TP * CHUNK), BF16),
                 pltpu.VMEM((KEYS, HD), F32),
                 pltpu.VMEM((KEYS, HD), F32),
             ],
@@ -251,17 +285,16 @@
     )(y, *own)
 
 
-def place_body(y_ref, *refs):
-    n = 2 * TP
-    ins, outs, bufs, in_sems, out_sems = refs[:n], refs[n : n + 4], refs[n + 4], refs[n + 5], refs[n + 6]
+def place_body(group, y_ref, *refs):
+    ins, refs = refs[:TP], refs[TP if group == 0 else TP + 4 :]
+    outs, bufs, in_sems, out_sems = refs[:4], refs[4], refs[5], refs[6]
     me = y_ref[0]
-    loads = [pltpu.make_async_copy(ins[i], bufs.at[i], in_sems.at[i]) for i in range(n)]
+    loads = [pltpu.make_async_copy(ins[i], bufs.at[i], in_sems.at[i]) for i in range(TP)]
     for copy in loads:
         copy.start()
     stores = []
-    for i in range(n):
-        group, d = divmod(i, TP)
-        src = lax.rem(me + d, TP) * 2 + group
+    for i in range(TP):
+        src = lax.rem(me + i, TP) * 2 + group
         loads[i].wait()
         for t, (at, width) in enumerate(SPANS):
             col = pl.multiple_of(src * width, HD)
@@ -274,26 +307,44 @@
         copy.wait()
 
 
-def place(y, pieces):
+def place(group, y, pieces, placed):
     anyspec = pl.BlockSpec(memory_space=pl.ANY)
     widths = (TP * 2 * QW, TP * 2 * QW, TP * 2 * HD, TP * 2 * HD)
     return pl.pallas_call(
-        place_body,
+        functools.partial(place_body, group),
         grid_spec=pltpu.PrefetchScalarGridSpec(
             num_scalar_prefetch=1,
             grid=(),
-            in_specs=[anyspec] * len(pieces),
+            in_specs=[anyspec] * (TP + len(placed)),
             out_specs=[anyspec] * 4,
             scratch_shapes=[
-                pltpu.VMEM((2 * TP, CHUNK, PIECE), BF16),
-                pltpu.SemaphoreType.DMA((2 * TP,)),
-                pltpu.SemaphoreType.DMA((2 * TP, 4)),
+                pltpu.VMEM((TP, CHUNK, PIECE), BF16),
+                pltpu.SemaphoreType.DMA((TP,)),
+                pltpu.SemaphoreType.DMA((TP, 4)),
             ],
         ),
         out_shape=[jax.ShapeDtypeStruct((CHUNK, w), BF16) for w in widths],
+        input_output_aliases={1 + TP + t: t for t in range(len(placed))},
         compiler_params=pltpu.CompilerParams(vmem_limit_bytes=60 << 20),
+        cost_estimate=pl.CostEstimate(flops=0, bytes_accessed=5 << 20, transcendentals=0),
         name="place",
-    )(y, *pieces)
+    )(y, *pieces, *placed)
+
+
+def table_body(in_ref, out_ref):
+    for i in range(in_ref.shape[0]):
+        out_ref[i] = in_ref[i]
+
+
+def through_smem(x):
+    smem = pl.BlockSpec(memory_space=pltpu.SMEM)
+    return pl.pallas_call(
+        table_body,
+        in_specs=[smem],
+        out_specs=smem,
+        out_shape=jax.ShapeDtypeStruct(x.shape, x.dtype),
+        name="table",
+    )(x)
 
 
 def shift(x, step):
@@ -353,6 +404,8 @@
                 (core == g).astype(jnp.int32)[None],
             ]
         ).astype(jnp.int32)
+        if g == 0:
+            scalars = through_smem(scalars)
         res = attn(g, scalars, own, recv[g], near, far)
         got = {0: res[0]}
         for d in (1, 3, 2):
@@ -362,11 +415,14 @@
         ids = jnp.arange(chips, dtype=jnp.int32)
         for terms, tab in ((res[TP], table), (swap(res[TP]), peer_table)):
             for j in range(SLOTS):
-                use = (tab[j] == ids * 2 + core) & (j < tab[SLOTS])
-                dense = dense + jnp.where(use[:, None, None], terms[j].astype(F32)[None], 0.0)
+                use = ((tab[j] == ids * 2 + core) & (j < tab[SLOTS])).astype(F32)
+                dense = dense + use[:, None, None] * terms[j].astype(F32)[None]
         parts = to_chips(dense.astype(BF16))
         beacs.append(jnp.sum(parts.astype(F32), axis=0).astype(BF16))
-    out, dq, dk, dv = place(place_at, back[0] + back[1])
+    placed = ()
+    for g in range(2):
+        placed = place(g, place_at, back[g], placed)
+    out, dq, dk, dv = placed
     dbk = jnp.concatenate([b[:, :HD] for b in beacs], axis=1)
     dbv = jnp.concatenate([b[:, HD:] for b in beacs], axis=1)
     return out, dq, dk, dv, dbk, dbv

time: 253 us -> 223 us (0.88)
  Pallas kernels: 93.4 us -> 66.9 us
  waiting for transfers between devices: 68.9 us -> 53.2 us
  starting transfers between devices: 29.4 us -> 42.6 us
    pallas_call x2, Pallas kernels: 82.9 us -> 55.3 us  [attn(): pl.pallas_call(attn_body, grid_spec=pltpu.PrefetchScalarGridSpec(num_scal...]
    ppermute x12, waiting for transfers between devices: 67.7 us -> 51.6 us  [shift(): return lax.ppermute(x, 'y', [(s, (s + step) % TP) for s in range(TP)])]
    ppermute x12, starting transfers between devices: 18.2 us -> 30.5 us  [shift(): return lax.ppermute(x, 'y', [(s, (s + step) % TP) for s in range(TP)])]
    convert_element_type x0 -> x4, other arithmetic: none -> 5.04 us  [layer(): use = ((tab[j] == ids * 2 + core) & (j < tab[SLOTS])).astype(F32)]
    and x4 -> x0, other arithmetic: 4.96 us -> none  [layer(): use = (tab[j] == ids * 2 + core) & (j < tab[SLOTS])]
    pallas_call x1 -> x3, Pallas kernels: 4.81 us -> 6.64 us  [the longest x2 5.45 us: place(): pl.pallas_call(functools.partial(place_body, group), grid_spec=pltpu.Pref...]
  transfers between devices with their start and end apart: 19 -> 19, of which waited for: 9 -> 7; matrix products, arithmetic and copies ran while one was open for 6% -> 7% of each run, Pallas kernels for 37% -> 30%
where the time goes in v3:
time: 223 us; the launch traced here: 221 us
  Pallas kernels  66.9 us (30%)
  waiting for transfers between devices  53.2 us (24%)
  starting transfers between devices  42.6 us (19%)
  blocking collectives  36.5 us (16%)
  other arithmetic  13.4 us (6%)
  local copies, waits for them, and re-layouts  4.48 us (2%)
  between operations  4.31 us (2%)
    pallas_call x2, Pallas kernels, attn(): pl.pallas_call(attn_body, grid_spec=pltpu.PrefetchScalarGridSpec(num_scal...  55.3 us
    ppermute x12, waiting for transfers between devices, shift(): return lax.ppermute(x, 'y', [(s, (s + step) % TP) for s in range(TP)])  51.6 us
    all_to_all x1, blocking collectives, to_chips(): return lax.all_to_all(x, ('z', 'x'), 0, 0, tiled=True)  36.5 us
    ppermute x12, starting transfers between devices, shift(): return lax.ppermute(x, 'y', [(s, (s + step) % TP) for s in range(TP)])  30.5 us
    all_to_all x2, starting transfers between devices, to_chips(): return lax.all_to_all(x, ('z', 'x'), 0, 0, tiled=True)  10.9 us
    pallas_call x2, Pallas kernels, place(): pl.pallas_call(functools.partial(place_body, group), grid_spec=pltpu.Pref...  5.45 us
    convert_element_type x4, other arithmetic, layer(): use = ((tab[j] == ids * 2 + core) & (j < tab[SLOTS])).astype(F32)  5.04 us
    pallas_call x2, Pallas kernels, split(): pl.pallas_call(functools.partial(split_body, group), grid_spec=pltpu.Pref...  4.91 us
  transfers between devices with their start and end apart: 19, of which 7 were waited for; matrix products, arithmetic and copies ran while one was open for 7% of the time, Pallas kernels for 30%

profile of v3, /device:TPU:0, one launch (start us, length us, event | category | flops | bytes accessed | tf_op | source)
XLA Modules:
  0.0 221.3 jit_solution(11240159328392206021)
XLA Ops:
  3.1 36.5 %all_to_all.15 = bf16[16,2,128,256]{3,2,1,0:T(8,128)(2,1)S(1)} all-to-all(bf16[16,2,128,256]{3,2,1,0:T(8,128)(2,1)S(1)} %broadcast_in_dim.17), channel_id=1, replica_groups=mesh['z'=4,'x'=4,'core'=2,'y'=4] {'z','x'}, dimensions={0} | all-to-all | bytes 4194304 | tf_op jit(solution)/shard_map/all_to_all | solution.py:355
  40.9 2.5 %split.3 = (bf16[256,1280]{1,0:T(8,128)(2,1)}, bf16[256,1280]{1,0:T(8,128)(2,1)}, bf16[256,1280]{1,0:T(8,128)(2,1)}) custom-call(s32[1]{0:T(128)} %bitcast.y_ref, bf16[256,4096]{1,0:T(8,128)(2,1)} %refs_0_.7, bf16[256,4096]{1,0:T(8,128)(2,1)} %refs_1_.7, bf16[256,1024]{1,0:T(8,128)(2,1)} %refs_2_.7, bf16[256,1024]{1,0:T(8,128)(2,1)} %refs_3_.7), custom_call_target="tpu_custom_call" | custom-call | bytes 4194304 | tf_op jit(solution)/shard_map/split/pallas_call | solution.py:268
  43.4 3.1 %collective-permute-start.8 = (bf16[256,1280]{1,0:T(8,128)(2,1)}, bf16[256,1280]{1,0:T(8,128)(2,1)S(1)}, u32[]{:S(2)}, u32[]{:S(2)}) collective-permute-start(bf16[256,1280]{1,0:T(8,128)(2,1)} %get-tuple-element.37), channel_id=1, source_target_pairs={{0,3},{1,0},{2,1},{3,2},{4,7},{5,4},{6,5},{7,6},{8,11},{9,8},{10,9... | collective-permute-start | bytes 1966088 | tf_op jit(solution)/shard_map/ppermute | solution.py:351
  48.1 2.5 %split.2 = (bf16[256,1280]{1,0:T(8,128)(2,1)}, bf16[256,1280]{1,0:T(8,128)(2,1)}, bf16[256,1280]{1,0:T(8,128)(2,1)}) custom-call(s32[1]{0:T(128)} %bitcast.y_ref, bf16[256,4096]{1,0:T(8,128)(2,1)} %refs_0_.7, bf16[256,4096]{1,0:T(8,128)(2,1)} %refs_1_.7, bf16[256,1024]{1,0:T(8,128)(2,1)} %refs_2_.7, bf16[256,1024]{1,0:T(8,128)(2,1)} %refs_3_.7), custom_call_target="tpu_custom_call" | custom-call | bytes 4194304 | tf_op jit(solution)/shard_map/split/pallas_call | solution.py:268
  53.6 1.3 and_convert_fusion.6
  56.2 2.4 %collective-permute-start = (bf16[256,1280]{1,0:T(8,128)(2,1)}, bf16[256,1280]{1,0:T(8,128)(2,1)S(1)}, u32[]{:S(2)}, u32[]{:S(2)}) collective-permute-start(bf16[256,1280]{1,0:T(8,128)(2,1)} %get-tuple-element.30), channel_id=1, source_target_pairs={{0,3},{1,0},{2,1},{3,2},{4,7},{5,4},{6,5},{7,6},{8,11},{9,8},{10,9... | collective-permute-start | bytes 1966088 | tf_op jit(solution)/shard_map/ppermute | solution.py:351
  61.9 1.3 and_convert_fusion.2
  63.2 12.7 %collective-permute-done.8.refs_4_.refs_5_.refs_6_.refs_7_ = bf16[256,1280]{1,0:T(8,128)(2,1)S(1)} collective-permute-done((bf16[256,1280]{1,0:T(8,128)(2,1)}, bf16[256,1280]{1,0:T(8,128)(2,1)S(1)}, u32[]{:S(2)}, u32[]{:S(2)}) %collective-permute-start.8) | collective-permute-done | bytes 655392 | tf_op jit(solution)/shard_map/ppermute | solution.py:351
  75.9 4.4 %collective-permute-start.2 = (bf16[256,1280]{1,0:T(8,128)(2,1)}, bf16[256,1280]{1,0:T(8,128)(2,1)}, u32[]{:S(2)}, u32[]{:S(2)}) collective-permute-start(bf16[256,1280]{1,0:T(8,128)(2,1)} %get-tuple-element.32), channel_id=1, source_target_pairs={{0,1},{1,2},{2,3},{3,0},{4,5},{5,6},{6,7},{7,4},{8,9},{9,10},{10,1... | collective-permute-start | bytes 1966088 | tf_op jit(solution)/shard_map/ppermute | solution.py:351
  80.4 27.7 %attn.3 = (bf16[256,1280]{1,0:T(8,128)(2,1)}, bf16[256,1280]{1,0:T(8,128)(2,1)}, bf16[256,1280]{1,0:T(8,128)(2,1)}, bf16[256,1280]{1,0:T(8,128)(2,1)}, bf16[4,128,256]{2,1,0:T(8,128)(2,1)}) custom-call(s32[11]{0:T(128)} %table.1.sc, bf16[256,4096]{1,0:T(8,128)(2,1)} %refs_0_.7, bf16[256,4096]{1,0:T(8,128)(2,1)} %refs_1_.7, bf16[256,1024]{1,0:T(8,128)(2,1)} %refs_2_.7, ...), custom_call_target="tpu_custom_call" | custom-call | flops 14495514624 | bytes 6291456 | tf_op jit(solution)/shard_map/attn/pallas_call | solution.py:207
  110.4 2.3 %add_convert_fusion.1 = bf16[16,128,256]{2,1,0:T(8,128)(2,1)} fusion(f32[128,256]{1,0:T(8,128)S(1)} %get-tuple-element.62, f32[16]{0:T(128)S(1)} %get-tuple-element.94, f32[128,256]{1,0:T(8,128)S(1)} %get-tuple-element.63, f32[16]{0:T(128)S(1)} %get-tuple-element.95, f32[128,256]{1,0:T(8,128)S(1)} %get-tuple-element.64, f32[16]{0:T(128)S(1)} %get-tuple-element.96, ...), kind=kLoop, calls=%fused_computation.1 | loop fusion | flops 8388608 | bytes 2097664 | tf_op jit(solution)/shard_map/convert_element_type | solution.py:420
  112.6 3.8 %all-to-all-start.1 = ((bf16[16,128,256]{2,1,0:T(8,128)(2,1)}), bf16[16,128,256]{2,1,0:T(8,128)(2,1)S(1)}, u32[]{:S(2)}, u32[]{:S(2)}) async-start(bf16[16,128,256]{2,1,0:T(8,128)(2,1)} %add_convert_fusion.1), calls=%async_computation.1 | async-start | bytes 2097152 | tf_op jit(solution)/shard_map/all_to_all | solution.py:355
  117.4 27.7 %attn.2 = (bf16[256,1280]{1,0:T(8,128)(2,1)}, bf16[256,1280]{1,0:T(8,128)(2,1)}, bf16[256,1280]{1,0:T(8,128)(2,1)}, bf16[256,1280]{1,0:T(8,128)(2,1)}, bf16[4,128,256]{2,1,0:T(8,128)(2,1)}) custom-call(s32[11]{0:T(128)} %concatenate.47.sc, bf16[256,4096]{1,0:T(8,128)(2,1)} %refs_0_.7, bf16[256,4096]{1,0:T(8,128)(2,1)} %refs_1_.7, bf16[256,1024]{1,0:T(8,128)(2,1)} %refs_2_.7, ...), custom_call_target="tpu_custom_call" | custom-call | flops 14495514624 | bytes 6291456 | tf_op jit(solution)/shard_map/attn/pallas_call | solution.py:207
  146.9 2.3 %add_convert_fusion = bf16[16,128,256]{2,1,0:T(8,128)(2,1)} fusion(f32[128,256]{1,0:T(8,128)S(1)} %get-tuple-element.70, f32[128,256]{1,0:T(8,128)S(1)} %get-tuple-element.71, f32[128,256]{1,0:T(8,128)S(1)} %get-tuple-element.72, f32[128,256]{1,0:T(8,128)S(1)} %get-tuple-element.69, f32[128,256]{1,0:T(8,128)S(1)} %get-tuple-element.66, ...), kind=kLoop, calls=%fused_computation | loop fusion | flops 8388608 | bytes 2097664 | tf_op jit(solution)/shard_map/convert_element_type | solution.py:420
  149.3 7.0 %all-to-all-start.2 = ((bf16[16,128,256]{2,1,0:T(8,128)(2,1)}), bf16[16,128,256]{2,1,0:T(8,128)(2,1)S(1)}, u32[]{:S(2)}, u32[]{:S(2)}) async-start(bf16[16,128,256]{2,1,0:T(8,128)(2,1)} %add_convert_fusion), calls=%async_computation.2 | async-start | bytes 2097152 | tf_op jit(solution)/shard_map/all_to_all | solution.py:355
  156.3 1.7 collective-permute-start.12
  158.1 3.2 %collective-permute-start.5 = (bf16[256,1280]{1,0:T(8,128)(2,1)}, bf16[256,1280]{1,0:T(8,128)(2,1)}, u32[]{:S(2)}, u32[]{:S(2)}) collective-permute-start(bf16[256,1280]{1,0:T(8,128)(2,1)} %get-tuple-element.34), channel_id=1, source_target_pairs={{0,3},{1,0},{2,1},{3,2},{4,7},{5,4},{6,5},{7,6},{8,11},{9,8},{10,9... | collective-permute-start | bytes 1966088 | tf_op jit(solution)/shard_map/ppermute | solution.py:351
  162.0 1.3 collective-permute-done.11.refs_1_
  163.3 13.2 %collective-permute-start.7 = (bf16[256,1280]{1,0:T(8,128)(2,1)}, bf16[256,1280]{1,0:T(8,128)(2,1)}, u32[]{:S(2)}, u32[]{:S(2)}) collective-permute-start(bf16[256,1280]{1,0:T(8,128)(2,1)} %get-tuple-element.36), channel_id=1, source_target_pairs={{0,1},{1,2},{2,3},{3,0},{4,5},{5,6},{6,7},{7,4},{8,9},{9,10},{10,1... | collective-permute-start | bytes 1966088 | tf_op jit(solution)/shard_map/ppermute | solution.py:351
  176.6 13.4 %collective-permute-done.13.refs_3_ = bf16[256,1280]{1,0:T(8,128)(2,1)} collective-permute-done((bf16[256,1280]{1,0:T(8,128)(2,1)}, bf16[256,1280]{1,0:T(8,128)(2,1)}, u32[]{:S(2)}, u32[]{:S(2)}) %collective-permute-start.13) | collective-permute-done | bytes 655392 | tf_op jit(solution)/shard_map/ppermute | solution.py:351
  190.0 2.7 %place.2 = (bf16[256,4096]{1,0:T(8,128)(2,1)}, bf16[256,4096]{1,0:T(8,128)(2,1)}, bf16[256,1024]{1,0:T(8,128)(2,1)}, bf16[256,1024]{1,0:T(8,128)(2,1)}) custom-call(s32[1]{0:T(128)} %bitcast.y_ref, bf16[256,1280]{1,0:T(8,128)(2,1)} %get-tuple-element.40.refs_0_, bf16[256,1280]{1,0:T(8,128)(2,1)} %copy-done.1, bf16[256,1280]{1,0:T(8,128)(2,1)} %copy-done.2, ...), custom_call_target="tpu_custom_call" | custom-call | bytes 5242880 | tf_op jit(solution)/shard_map/place/pallas_call | solution.py:313
  192.7 11.3 %collective-permute-done.6.refs_2_ = bf16[256,1280]{1,0:T(8,128)(2,1)} collective-permute-done((bf16[256,1280]{1,0:T(8,128)(2,1)}, bf16[256,1280]{1,0:T(8,128)(2,1)}, u32[]{:S(2)}, u32[]{:S(2)}) %collective-permute-start.6) | collective-permute-done | bytes 655392 | tf_op jit(solution)/shard_map/ppermute | solution.py:351
  204.0 12.9 %collective-permute-done.7.refs_3_ = bf16[256,1280]{1,0:T(8,128)(2,1)} collective-permute-done((bf16[256,1280]{1,0:T(8,128)(2,1)}, bf16[256,1280]{1,0:T(8,128)(2,1)}, u32[]{:S(2)}, u32[]{:S(2)}) %collective-permute-start.7) | collective-permute-done | bytes 655392 | tf_op jit(solution)/shard_map/ppermute | solution.py:351
  216.9 2.7 %place.3 = (bf16[256,4096]{1,0:T(8,128)(2,1)}, bf16[256,4096]{1,0:T(8,128)(2,1)}, bf16[256,1024]{1,0:T(8,128)(2,1)}, bf16[256,1024]{1,0:T(8,128)(2,1)}) custom-call(s32[1]{0:T(128)} %bitcast.y_ref, bf16[256,1280]{1,0:T(8,128)(2,1)} %get-tuple-element.33.refs_0_, ...), custom_call_target="tpu_custom_call", output_to_operand_aliasing={{0}: (5, {}), {1}: (6, {}), {2}: (7, {}), {3}: (8, {})} | custom-call | bytes 5242880 | tf_op jit(solution)/shard_map/place/pallas_call | solution.py:313
  (62 shorter events, 17.1 us)
Async XLA Ops:
  1.5 1.3 collective-permute-start.3
  3.1 37.2 %copy-start.3 = (s32[1,4]{1,0:T(1,128)S(1)}, s32[1,4]{1,0:T(1,128)}, u32[]{:S(2)}) copy-start(s32[1,4]{1,0:T(1,128)} %param.14) | copy-start | bytes 52
  39.6 3.7 %copy-start = (bf16[16,2,128,256]{3,2,1,0:T(8,128)(2,1)}, bf16[16,2,128,256]{3,2,1,0:T(8,128)(2,1)S(1)}, u32[]{:S(2)}) copy-start(bf16[16,2,128,256]{3,2,1,0:T(8,128)(2,1)S(1)} %all_to_all.15) | copy-start | bytes 6291460
  39.6 40.8 %collective-permute-start.4 = (bf16[16,2,128,256]{3,2,1,0:T(8,128)(2,1)S(1)}, bf16[16,2,128,256]{3,2,1,0:T(8,128)(2,1)}, u32[]{:S(2)}, u32[]{:S(2)}) collective-permute-start(bf16[16,2,128,256]{3,2,1,0:T(8,128)(2,1)S(1)} %all_to_all.15), channel_id=1, source_target_pairs={{0,4},{4,0},{1,5},{5,1},{2,6},{6,2},{3,7},{7,3},{8,12},{12,8},{9,1... | collective-permute-start | bytes 6291464 | tf_op jit(solution)/shard_map/ppermute | solution.py:359
  40.4 15.8 %collective-permute-start.14 = (s32[5]{0:T(128)S(1)}, s32[5]{0:T(128)S(1)}, u32[]{:S(2)}, u32[]{:S(2)}) collective-permute-start(s32[5]{0:T(128)S(1)} %pad_add_fusion), channel_id=1, source_target_pairs={{0,4},{4,0},{1,5},{5,1},{2,6},{6,2},{3,7},{7,3},{8,12},{12,8},{9,1... | collective-permute-start | bytes 68 | tf_op jit(solution)/shard_map/ppermute | solution.py:359
  43.4 32.6 %collective-permute-start.8 = (bf16[256,1280]{1,0:T(8,128)(2,1)}, bf16[256,1280]{1,0:T(8,128)(2,1)S(1)}, u32[]{:S(2)}, u32[]{:S(2)}) collective-permute-start(bf16[256,1280]{1,0:T(8,128)(2,1)} %get-tuple-element.37), channel_id=1, source_target_pairs={{0,3},{1,0},{2,1},{3,2},{4,7},{5,4},{6,5},{7,6},{8,11},{9,8},{10,9... | collective-permute-start | bytes 1966088 | tf_op jit(solution)/shard_map/ppermute | solution.py:351
  46.4 29.5 %collective-permute-start.9 = (bf16[256,1280]{1,0:T(8,128)(2,1)}, bf16[256,1280]{1,0:T(8,128)(2,1)}, u32[]{:S(2)}, u32[]{:S(2)}) collective-permute-start(bf16[256,1280]{1,0:T(8,128)(2,1)} %get-tuple-element.38), channel_id=1, source_target_pairs={{0,2},{1,3},{2,0},{3,1},{4,6},{5,7},{6,4},{7,5},{8,10},{9,11},{10,... | collective-permute-start | bytes 1966088 | tf_op jit(solution)/shard_map/ppermute | solution.py:351
  47.1 33.3 %collective-permute-start.10 = (bf16[256,1280]{1,0:T(8,128)(2,1)}, bf16[256,1280]{1,0:T(8,128)(2,1)}, u32[]{:S(2)}, u32[]{:S(2)}) collective-permute-start(bf16[256,1280]{1,0:T(8,128)(2,1)} %get-tuple-element.39), channel_id=1, source_target_pairs={{0,1},{1,2},{2,3},{3,0},{4,5},{5,6},{6,7},{7,4},{8,9},{9,10},{10,1... | collective-permute-start | bytes 1966088 | tf_op jit(solution)/shard_map/ppermute | solution.py:351
  56.2 60.3 %collective-permute-start = (bf16[256,1280]{1,0:T(8,128)(2,1)}, bf16[256,1280]{1,0:T(8,128)(2,1)S(1)}, u32[]{:S(2)}, u32[]{:S(2)}) collective-permute-start(bf16[256,1280]{1,0:T(8,128)(2,1)} %get-tuple-element.30), channel_id=1, source_target_pairs={{0,3},{1,0},{2,1},{3,2},{4,7},{5,4},{6,5},{7,6},{8,11},{9,8},{10,9... | collective-permute-start | bytes 1966088 | tf_op jit(solution)/shard_map/ppermute | solution.py:351
  75.9 4.5 %copy-start.5 = (bf16[256,1280]{1,0:T(8,128)(2,1)}, bf16[256,1280]{1,0:T(8,128)(2,1)S(1)}, u32[]{:S(2)}) copy-start(bf16[256,1280]{1,0:T(8,128)(2,1)S(1)} %collective-permute-done.8.refs_4_.refs_5_.refs_6_.refs_7_) | copy-start | bytes 1966084
  75.9 40.6 %collective-permute-start.1 = (bf16[256,1280]{1,0:T(8,128)(2,1)}, bf16[256,1280]{1,0:T(8,128)(2,1)}, u32[]{:S(2)}, u32[]{:S(2)}) collective-permute-start(bf16[256,1280]{1,0:T(8,128)(2,1)} %get-tuple-element.31), channel_id=1, source_target_pairs={{0,2},{1,3},{2,0},{3,1},{4,6},{5,7},{6,4},{7,5},{8,10},{9,11},{10,... | collective-permute-start | bytes 1966088 | tf_op jit(solution)/shard_map/ppermute | solution.py:351
  75.9 40.6 %collective-permute-start.2 = (bf16[256,1280]{1,0:T(8,128)(2,1)}, bf16[256,1280]{1,0:T(8,128)(2,1)}, u32[]{:S(2)}, u32[]{:S(2)}) collective-permute-start(bf16[256,1280]{1,0:T(8,128)(2,1)} %get-tuple-element.32), channel_id=1, source_target_pairs={{0,1},{1,2},{2,3},{3,0},{4,5},{5,6},{6,7},{7,4},{8,9},{9,10},{10,1... | collective-permute-start | bytes 1966088 | tf_op jit(solution)/shard_map/ppermute | solution.py:351
  108.0 2.3 %collective-permute-start.15 = (bf16[4,128,256]{2,1,0:T(8,128)(2,1)}, bf16[4,128,256]{2,1,0:T(8,128)(2,1)S(1)}, u32[]{:S(2)}, u32[]{:S(2)}) collective-permute-start(bf16[4,128,256]{2,1,0:T(8,128)(2,1)} %get-tuple-element.52), channel_id=1, source_target_pairs={{0,4},{4,0},{1,5},{5,1},{2,6},{6,2},{3,7},{7,3},{8,12},{12,8},{9,1... | collective-permute-start | bytes 786440 | tf_op jit(solution)/shard_map/ppermute | solution.py:359
  112.6 36.6 %all-to-all-start.1 = ((bf16[16,128,256]{2,1,0:T(8,128)(2,1)}), bf16[16,128,256]{2,1,0:T(8,128)(2,1)S(1)}, u32[]{:S(2)}, u32[]{:S(2)}) async-start(bf16[16,128,256]{2,1,0:T(8,128)(2,1)} %add_convert_fusion.1), calls=%async_computation.1 | async-start | bytes 2097152 | tf_op jit(solution)/shard_map/all_to_all | solution.py:355
  145.0 1.9 collective-permute-start.16
  145.5 17.8 %collective-permute-start.11 = (bf16[256,1280]{1,0:T(8,128)(2,1)}, bf16[256,1280]{1,0:T(8,128)(2,1)S(1)}, u32[]{:S(2)}, u32[]{:S(2)}) collective-permute-start(bf16[256,1280]{1,0:T(8,128)(2,1)} %get-tuple-element.41), channel_id=1, source_target_pairs={{0,3},{1,0},{2,1},{3,2},{4,7},{5,4},{6,5},{7,6},{8,11},{9,8},{10,9... | collective-permute-start | bytes 1966088 | tf_op jit(solution)/shard_map/ppermute | solution.py:351
  149.3 70.5 %all-to-all-start.2 = ((bf16[16,128,256]{2,1,0:T(8,128)(2,1)}), bf16[16,128,256]{2,1,0:T(8,128)(2,1)S(1)}, u32[]{:S(2)}, u32[]{:S(2)}) async-start(bf16[16,128,256]{2,1,0:T(8,128)(2,1)} %add_convert_fusion), calls=%async_computation.2 | async-start | bytes 2097152 | tf_op jit(solution)/shard_map/all_to_all | solution.py:355
  156.3 20.3 %collective-permute-start.12 = (bf16[256,1280]{1,0:T(8,128)(2,1)}, bf16[256,1280]{1,0:T(8,128)(2,1)S(1)}, u32[]{:S(2)}, u32[]{:S(2)}) collective-permute-start(bf16[256,1280]{1,0:T(8,128)(2,1)} %get-tuple-element.42), channel_id=1, source_target_pairs={{0,2},{1,3},{2,0},{3,1},{4,6},{5,7},{6,4},{7,5},{8,10},{9,11},{10,... | collective-permute-start | bytes 1966088 | tf_op jit(solution)/shard_map/ppermute | solution.py:351
  158.0 31.9 %collective-permute-start.13 = (bf16[256,1280]{1,0:T(8,128)(2,1)}, bf16[256,1280]{1,0:T(8,128)(2,1)}, u32[]{:S(2)}, u32[]{:S(2)}) collective-permute-start(bf16[256,1280]{1,0:T(8,128)(2,1)} %get-tuple-element.43), channel_id=1, source_target_pairs={{0,1},{1,2},{2,3},{3,0},{4,5},{5,6},{6,7},{7,4},{8,9},{9,10},{10,1... | collective-permute-start | bytes 1966088 | tf_op jit(solution)/shard_map/ppermute | solution.py:351
  158.1 34.6 %collective-permute-start.5 = (bf16[256,1280]{1,0:T(8,128)(2,1)}, bf16[256,1280]{1,0:T(8,128)(2,1)}, u32[]{:S(2)}, u32[]{:S(2)}) collective-permute-start(bf16[256,1280]{1,0:T(8,128)(2,1)} %get-tuple-element.34), channel_id=1, source_target_pairs={{0,3},{1,0},{2,1},{3,2},{4,7},{5,4},{6,5},{7,6},{8,11},{9,8},{10,9... | collective-permute-start | bytes 1966088 | tf_op jit(solution)/shard_map/ppermute | solution.py:351
  161.3 42.7 %collective-permute-start.6 = (bf16[256,1280]{1,0:T(8,128)(2,1)}, bf16[256,1280]{1,0:T(8,128)(2,1)}, u32[]{:S(2)}, u32[]{:S(2)}) collective-permute-start(bf16[256,1280]{1,0:T(8,128)(2,1)} %get-tuple-element.35), channel_id=1, source_target_pairs={{0,2},{1,3},{2,0},{3,1},{4,6},{5,7},{6,4},{7,5},{8,10},{9,11},{10,... | collective-permute-start | bytes 1966088 | tf_op jit(solution)/shard_map/ppermute | solution.py:351
  163.3 26.6 %copy-start.1 = (bf16[256,1280]{1,0:T(8,128)(2,1)}, bf16[256,1280]{1,0:T(8,128)(2,1)S(1)}, u32[]{:S(2)}) copy-start(bf16[256,1280]{1,0:T(8,128)(2,1)S(1)} %collective-permute-done.11.refs_1_) | copy-start | bytes 1966084
  163.3 53.6 %collective-permute-start.7 = (bf16[256,1280]{1,0:T(8,128)(2,1)}, bf16[256,1280]{1,0:T(8,128)(2,1)}, u32[]{:S(2)}, u32[]{:S(2)}) collective-permute-start(bf16[256,1280]{1,0:T(8,128)(2,1)} %get-tuple-element.36), channel_id=1, source_target_pairs={{0,1},{1,2},{2,3},{3,0},{4,5},{5,6},{6,7},{7,4},{8,9},{9,10},{10,1... | collective-permute-start | bytes 1966088 | tf_op jit(solution)/shard_map/ppermute | solution.py:351
  176.6 13.4 %copy-start.2 = (bf16[256,1280]{1,0:T(8,128)(2,1)}, bf16[256,1280]{1,0:T(8,128)(2,1)S(1)}, u32[]{:S(2)}) copy-start(bf16[256,1280]{1,0:T(8,128)(2,1)S(1)} %collective-permute-done.12.refs_2_) | copy-start | bytes 1966084
  (1 other events, 0.9 us)

commit v4 on v3

--- a/solution.py
+++ b/solution.py
@@ -18,6 +18,7 @@
 BF16 = jnp.bfloat16
 NN = (((1,), (0,)), ((), ()))
 NT = (((1,), (1,)), ((), ()))
+VMEM = 66_500_000
 TP = 4
 CHUNK = 256
 SLOTS = 4
@@ -25,6 +26,7 @@
 BEAC = SLOTS * BLOCK
 KEYS = BEAC + TP * CHUNK
 GROUP = 4
+STEP = 2
 QW = GROUP * HD
 PIECE = 2 * QW + 2 * HD
 SPANS = ((0, QW), (QW, QW), (2 * QW, HD), (2 * QW + HD, HD))
@@ -38,7 +40,7 @@
     return op(x.reshape(x.shape[0] // 8, 8, x.shape[1]), axis=0)
 
 
-def chunk_steps(chunk, q_ref, go_ref, o_ref, dq_ref, keys, vals, keys_t, vals_t, bias, scores, probs, dscores):
+def chunk_steps(chunk, q_ref, go_ref, o_ref, dq_ref, scores, probs, dscores, keys, vals, keys_t, vals_t, bias):
     blocks = BEAC // CHUNK + chunk + 1
     depth = blocks * CHUNK
     cols = slice(chunk * CHUNK, (chunk + 1) * CHUNK)
@@ -100,16 +102,34 @@
     return steps + [functools.partial(dscore, b) for b in each] + [dquery]
 
 
-def interleave(sequences, lag):
-    items, start = [], 0.0
-    for n, steps in enumerate(sequences):
-        items += [(start + t, n, step) for t, step in enumerate(steps)]
-        start += lag * len(steps)
+def key_steps(q_ref, go_ref, probs, dscores, dk_acc, dv_acc):
+    def terms(b):
+        rows = pl.ds(b * CHUNK, CHUNK)
+        first = max(0, b - BEAC // CHUNK)
+        go = go_ref[first:].reshape(-1, HD)
+        dv_acc[rows, :] += mm(probs[rows, first * CHUNK :], go, NN)
+        q = q_ref[first:].reshape(-1, HD)
+        dk_acc[rows, :] += mm(dscores[rows, first * CHUNK :], q, NN)
+
+    return [functools.partial(terms, b) for b in range(KEYS // CHUNK)]
+
+
+def interleave(heads, lag, tail_lag):
+    items, start, n = [], 0.0, 0
+    for chunks, tail in heads:
+        end = 0.0
+        for steps in chunks:
+            items += [(start + t, n, step) for t, step in enumerate(steps)]
+            end = max(end, start + len(steps))
+            start += lag * len(steps)
+            n += 1
+        items += [(end + tail_lag * t, n, step) for t, step in enumerate(tail)]
+        n += 1
     for _, _, step in sorted(items, key=lambda item: item[:2]):
         step()
 
 
-S_A, S_B, S_COUNT, S_Y, S_SAME = 0, 4, 8, 9, 10
+S_NEAR, S_COUNT, S_Y, S_CORE, S_OWN, S_PEER, S_GROUP = 0, 4, 5, 6, 7, 12, 17
 
 
 def attn_body(sc, *refs):
@@ -124,11 +144,11 @@
 
     @pl.when(head == 0)
     def _():
-        same = sc[S_SAME]
+        same = sc[S_CORE]
         for t, dst in ((0, keys), (1, vals)):
             for j in range(SLOTS):
                 a, b = near[t * SLOTS + j][0], far[t * SLOTS + j][0]
-                dst[pl.ds(j * BLOCK, BLOCK), :] = jnp.where(same == 1, a, b)
+                dst[pl.ds(j * BLOCK, BLOCK), :] = jnp.where(same == sc[S_GROUP], a, b)
             for d in range(TP):
                 at = pl.multiple_of(BEAC + lax.rem(me + d, TP) * CHUNK, CHUNK)
                 dst[pl.ds(at, CHUNK), :] = pieces[d][2 + t][...]
@@ -142,25 +162,26 @@
 
     for d in range(TP):
         at = lax.rem(me + d, TP)
-        qs[at] = pieces[d][0][...]
-        gs[at] = pieces[d][1][...]
-    tables = (keys, vals, keys_t, vals_t, bias, scores, probs, dscores)
-    interleave([chunk_steps(i, qs, gs, os, dqs, *tables) for i in range(TP)], 0.3)
-    q_all = qs[...].reshape(TP * CHUNK, HD)
-    go_all = gs[...].reshape(TP * CHUNK, HD)
-    for b in range(KEYS // CHUNK):
-        rows = pl.ds(b * CHUNK, CHUNK)
-        first = max(0, b - BEAC // CHUNK) * CHUNK
-        dv_acc[rows, :] += mm(probs[rows, first:], go_all[first:], NN)
-        dk_acc[rows, :] += mm(dscores[rows, first:], q_all[first:], NN)
-    at_o = pl.multiple_of(head * HD, HD)
-    at_q = pl.multiple_of(QW + head * HD, HD)
+        for e in range(STEP):
+            cols = slice(e * HD, (e + 1) * HD)
+            qs[e, at] = pieces[d][0][:, cols]
+            gs[e, at] = pieces[d][1][:, cols]
+    tables = (keys, vals, keys_t, vals_t, bias)
+    heads = []
+    for e in range(STEP):
+        mid = (scores.at[e], probs.at[e], dscores.at[e])
+        chunks = [chunk_steps(i, qs.at[e], gs.at[e], os.at[e], dqs.at[e], *mid, *tables) for i in range(TP)]
+        heads.append((chunks, key_steps(qs.at[e], gs.at[e], *mid[1:], dk_acc, dv_acc)))
+    interleave(heads, 0.3, 2.0)
     for d in range(TP):
         at = lax.rem(me + d, TP)
-        outs[d][:, pl.ds(at_o, HD)] = os[at]
-        outs[d][:, pl.ds(at_q, HD)] = dqs[at]
-
-    @pl.when(head == GROUP - 1)
+        for e in range(STEP):
+            at_o = pl.multiple_of((head * STEP + e) * HD, HD)
+            at_q = pl.multiple_of(QW + (head * STEP + e) * HD, HD)
+            outs[d][:, pl.ds(at_o, HD)] = os[e, at]
+            outs[d][:, pl.ds(at_q, HD)] = dqs[e, at]
+
+    @pl.when(head == GROUP // STEP - 1)
     def _():
         for d in range(TP):
             at = pl.multiple_of(BEAC + lax.rem(me + d, TP) * CHUNK, CHUNK)
@@ -172,33 +193,34 @@
             beac_out[j, :, HD:] = dv_acc[rows, :].astype(BF16)
 
 
-def attn(group, scalars, own, pieces, near, far):
+def attn(scalars, own, pieces, near, far):
     spec = pl.BlockSpec
     ops, in_specs = [], []
     kv_heads = 2
     for t in range(2):
         ops.append(own[t])
         in_specs.append(
-            spec((CHUNK, HD), lambda h, sc: (0, (sc[S_Y] * kv_heads + group) * GROUP + h))
+            spec((CHUNK, STEP * HD), lambda h, sc: (0, (sc[S_Y] * kv_heads + sc[S_GROUP]) * (GROUP // STEP) + h))
         )
     for t in range(2):
         ops.append(own[2 + t])
-        in_specs.append(spec((CHUNK, HD), lambda h, sc: (0, sc[S_Y] * kv_heads + group)))
+        in_specs.append(spec((CHUNK, HD), lambda h, sc: (0, sc[S_Y] * kv_heads + sc[S_GROUP])))
     for piece in pieces:
         ops += [piece] * 4
         in_specs += [
-            spec((CHUNK, HD), lambda h, sc: (0, h)),
-            spec((CHUNK, HD), lambda h, sc: (0, GROUP + h)),
+            spec((CHUNK, STEP * HD), lambda h, sc: (0, h)),
+            spec((CHUNK, STEP * HD), lambda h, sc: (0, GROUP // STEP + h)),
             spec((CHUNK, HD), lambda h, sc: (0, 2 * GROUP)),
             spec((CHUNK, HD), lambda h, sc: (0, 2 * GROUP + 1)),
         ]
-    for arr, base in ((near, S_A), (far, S_B)):
-        for t in range(2):
-            for j in range(SLOTS):
-                ops.append(arr)
-                in_specs.append(
-                    spec((1, BLOCK, HD), lambda h, sc, at=base + j, t=t: (sc[at], 0, t))
-                )
+    for t in range(2):
+        for j in range(SLOTS):
+            ops.append(near)
+            in_specs.append(spec((1, BLOCK, HD), lambda h, sc, j=j, t=t: (sc[S_NEAR + j], 0, t)))
+    for t in range(2):
+        for j in range(SLOTS):
+            ops.append(far)
+            in_specs.append(spec((1, BLOCK, HD), lambda h, sc, j=j, t=t: (j, 0, t)))
     out_specs = [spec((CHUNK, PIECE), lambda h, sc: (0, 0)) for _ in range(TP)]
     out_specs.append(spec((SLOTS, BLOCK, 2 * HD), lambda h, sc: (0, 0, 0)))
     out_shape = [jax.ShapeDtypeStruct((CHUNK, PIECE), BF16) for _ in range(TP)]
@@ -208,28 +230,28 @@
         attn_body,
         grid_spec=pltpu.PrefetchScalarGridSpec(
             num_scalar_prefetch=1,
-            grid=(GROUP,),
+            grid=(GROUP // STEP,),
             in_specs=in_specs,
             out_specs=out_specs,
             scratch_shapes=[
-                pltpu.VMEM((TP, CHUNK, HD), BF16),
-                pltpu.VMEM((TP, CHUNK, HD), BF16),
-                pltpu.VMEM((TP, CHUNK, HD), BF16),
-                pltpu.VMEM((TP, CHUNK, HD), BF16),
+                pltpu.VMEM((STEP, TP, CHUNK, HD), BF16),
+                pltpu.VMEM((STEP, TP, CHUNK, HD), BF16),
+                pltpu.VMEM((STEP, TP, CHUNK, HD), BF16),
+                pltpu.VMEM((STEP, TP, CHUNK, HD), BF16),
                 pltpu.VMEM((KEYS, HD), BF16),
                 pltpu.VMEM((KEYS, HD), BF16),
                 pltpu.VMEM((HD, KEYS), BF16),
                 pltpu.VMEM((HD, KEYS), BF16),
                 pltpu.VMEM((BEAC, HD), F32),
-                pltpu.VMEM((TP, KEYS, CHUNK), F32),
-                pltpu.VMEM((KEYS, TP * CHUNK), BF16),
-                pltpu.VMEM((KEYS, TP * CHUNK), BF16),
+                pltpu.VMEM((STEP, TP, KEYS, CHUNK), F32),
+                pltpu.VMEM((STEP, KEYS, TP * CHUNK), BF16),
+                pltpu.VMEM((STEP, KEYS, TP * CHUNK), BF16),
                 pltpu.VMEM((KEYS, HD), F32),
                 pltpu.VMEM((KEYS, HD), F32),
             ],
         ),
         out_shape=out_shape,
-        compiler_params=pltpu.CompilerParams(vmem_limit_bytes=60 << 20),
+        compiler_params=pltpu.CompilerParams(vmem_limit_bytes=VMEM),
         cost_estimate=pl.CostEstimate(
             flops=6 * 2 * pairs * HD * 2, bytes_accessed=6 << 20, transcendentals=pairs
         ),
@@ -279,7 +301,7 @@
             ],
         ),
         out_shape=[jax.ShapeDtypeStruct((CHUNK, PIECE), BF16)] * (TP - 1),
-        compiler_params=pltpu.CompilerParams(vmem_limit_bytes=60 << 20),
+        compiler_params=pltpu.CompilerParams(vmem_limit_bytes=VMEM),
         cost_estimate=pl.CostEstimate(flops=0, bytes_accessed=4 << 20, transcendentals=0),
         name="split",
     )(y, *own)
@@ -325,24 +347,108 @@
         ),
         out_shape=[jax.ShapeDtypeStruct((CHUNK, w), BF16) for w in widths],
         input_output_aliases={1 + TP + t: t for t in range(len(placed))},
-        compiler_params=pltpu.CompilerParams(vmem_limit_bytes=60 << 20),
+        compiler_params=pltpu.CompilerParams(vmem_limit_bytes=VMEM),
         cost_estimate=pl.CostEstimate(flops=0, bytes_accessed=5 << 20, transcendentals=0),
         name="place",
     )(y, *pieces, *placed)
 
 
-def table_body(in_ref, out_ref):
-    for i in range(in_ref.shape[0]):
-        out_ref[i] = in_ref[i]
-
-
-def through_smem(x):
+def pick_body(tab_ref, *refs):
+    for j in range(SLOTS):
+        refs[SLOTS][j] = refs[j][0]
+
+
+def pick(tables, gathered):
+    def block(j):
+        def at(i, tab):
+            b = tab[S_PEER + j]
+            return (b - lax.rem(b, 2) + (lax.rem(b, 2) ^ tab[S_CORE]), 0, 0)
+
+        return pl.BlockSpec((1, BLOCK, 2 * HD), at)
+
+    return pl.pallas_call(
+        pick_body,
+        grid_spec=pltpu.PrefetchScalarGridSpec(
+            num_scalar_prefetch=1,
+            grid=(1,),
+            in_specs=[block(j) for j in range(SLOTS)],
+            out_specs=pl.BlockSpec((SLOTS, BLOCK, 2 * HD), lambda i, tab: (0, 0, 0)),
+        ),
+        out_shape=jax.ShapeDtypeStruct((SLOTS, BLOCK, 2 * HD), BF16),
+        compiler_params=pltpu.CompilerParams(vmem_limit_bytes=VMEM),
+        cost_estimate=pl.CostEstimate(flops=0, bytes_accessed=1 << 19, transcendentals=0),
+        name="pick",
+    )(tables, *([gathered] * SLOTS))
+
+
+def scatter_body(tab_ref, own_ref, peer_ref, out_ref):
+    out_ref[...] = jnp.zeros_like(out_ref)
+    for terms, base in ((own_ref, S_OWN), (peer_ref, S_PEER)):
+        for j in range(SLOTS):
+            block = tab_ref[base + j]
+
+            @pl.when((lax.rem(block, 2) == tab_ref[S_CORE]) & (j < tab_ref[base + SLOTS]))
+            def _():
+                chip = lax.div(block, 2)
+                out_ref[chip] = (out_ref[chip].astype(F32) + terms[j].astype(F32)).astype(BF16)
+
+
+def scatter(tables, own, peer, chips):
+    whole = pl.BlockSpec((SLOTS, BLOCK, 2 * HD), lambda i, tab: (0, 0, 0))
+    return pl.pallas_call(
+        scatter_body,
+        grid_spec=pltpu.PrefetchScalarGridSpec(
+            num_scalar_prefetch=1,
+            grid=(1,),
+            in_specs=[whole, whole],
+            out_specs=pl.BlockSpec((chips, BLOCK, 2 * HD), lambda i, tab: (0, 0, 0)),
+        ),
+        out_shape=jax.ShapeDtypeStruct((chips, BLOCK, 2 * HD), BF16),
+        compiler_params=pltpu.CompilerParams(vmem_limit_bytes=VMEM),
+        cost_estimate=pl.CostEstimate(flops=0, bytes_accessed=2 << 20, transcendentals=0),
+        name="scatter",
+    )(tables, own, peer)
+
+
+def total_body(parts_ref, *refs):
+    dbk_ref, dbv_ref = refs[-2:]
+    total = parts_ref[0].astype(F32)
+    for n in range(1, parts_ref.shape[0]):
+        total = total + parts_ref[n].astype(F32)
+    dbk_ref[...] = total[:, :HD].astype(BF16)
+    dbv_ref[...] = total[:, HD:].astype(BF16)
+
+
+def total(group, parts, summed):
+    column = pl.BlockSpec((BLOCK, HD), lambda i: (0, group))
+    return pl.pallas_call(
+        total_body,
+        grid=(1,),
+        in_specs=[pl.BlockSpec(parts.shape, lambda i: (0, 0, 0))]
+        + [pl.BlockSpec(memory_space=pl.ANY)] * len(summed),
+        out_specs=[column] * 2,
+        out_shape=[jax.ShapeDtypeStruct((BLOCK, 2 * HD), BF16)] * 2,
+        input_output_aliases={1 + t: t for t in range(len(summed))},
+        compiler_params=pltpu.CompilerParams(vmem_limit_bytes=VMEM),
+        cost_estimate=pl.CostEstimate(flops=0, bytes_accessed=1 << 20, transcendentals=0),
+        name="total",
+    )(parts, *summed)
+
+
+def table_body(in_ref, *out_refs):
+    for group, out_ref in enumerate(out_refs):
+        for i in range(S_GROUP):
+            out_ref[i] = in_ref[i]
+        out_ref[S_GROUP] = group
+
+
+def group_tables(x):
     smem = pl.BlockSpec(memory_space=pltpu.SMEM)
     return pl.pallas_call(
         table_body,
         in_specs=[smem],
-        out_specs=smem,
-        out_shape=jax.ShapeDtypeStruct(x.shape, x.dtype),
+        out_specs=[smem] * 2,
+        out_shape=[jax.ShapeDtypeStruct((S_GROUP + 1,), x.dtype)] * 2,
         name="table",
     )(x)
 
@@ -389,43 +495,28 @@
         recv.append([got[1], got[2], got[3]])
 
     near = to_chips(chip_blocks)
-    far = swap(near).reshape(chips * 2, BLOCK, 2 * HD)
     near = near.reshape(chips * 2, BLOCK, 2 * HD)
 
     chip, parity = row // 2, row % 2
-    back, beacs = [], []
+    scalars = [chip * 2 + (parity ^ core), count, y[None], core[None], table, peer_table]
+    scalars = group_tables(jnp.concatenate(scalars).astype(jnp.int32))
+    far = swap(pick(scalars[0], near))
+    back, summed = [], ()
     for g in range(2):
-        scalars = jnp.concatenate(
-            [
-                chip * 2 + (parity ^ core),
-                chip * 2 + (parity ^ core ^ 1),
-                count,
-                y[None],
-                (core == g).astype(jnp.int32)[None],
-            ]
-        ).astype(jnp.int32)
-        if g == 0:
-            scalars = through_smem(scalars)
-        res = attn(g, scalars, own, recv[g], near, far)
+        res = attn(scalars[g], own, recv[g], near, far)
         got = {0: res[0]}
         for d in (1, 3, 2):
             got[TP - d] = shift(res[d], d)
         back.append([got[d] for d in range(TP)])
-        dense = jnp.zeros((chips, BLOCK, 2 * HD), F32)
-        ids = jnp.arange(chips, dtype=jnp.int32)
-        for terms, tab in ((res[TP], table), (swap(res[TP]), peer_table)):
-            for j in range(SLOTS):
-                use = ((tab[j] == ids * 2 + core) & (j < tab[SLOTS])).astype(F32)
-                dense = dense + use[:, None, None] * terms[j].astype(F32)[None]
-        parts = to_chips(dense.astype(BF16))
-        beacs.append(jnp.sum(parts.astype(F32), axis=0).astype(BF16))
+        peer = swap(res[TP])
+        dense = scatter(scalars[g], res[TP], peer, chips)
+        parts = to_chips(dense)
+        summed = total(g, parts, summed)
     placed = ()
     for g in range(2):
         placed = place(g, place_at, back[g], placed)
     out, dq, dk, dv = placed
-    dbk = jnp.concatenate([b[:, :HD] for b in beacs], axis=1)
-    dbv = jnp.concatenate([b[:, HD:] for b in beacs], axis=1)
-    return out, dq, dk, dv, dbk, dbv
+    return out, dq, dk, dv, *summed
 
 
 def solution(mesh):

time: 223 us -> 199 us (0.89)
  blocking collectives: 36.5 us -> 0 us
  waiting for transfers between devices: 53.2 us -> 77.6 us
  other arithmetic: 13.4 us -> 0.14 us
  Pallas kernels: 66.9 us -> 73.1 us
  starting transfers between devices: 42.6 us -> 39.4 us
  between operations: 4.31 us -> 1.5 us
    all_to_all x1 -> x0, blocking collectives: 36.5 us -> none  [to_chips(): return lax.all_to_all(x, ('z', 'x'), 0, 0, tiled=True)]
    all_to_all x2 -> x3, waiting for transfers between devices: 0.01 us -> 22.2 us  [to_chips(): return lax.all_to_all(x, ('z', 'x'), 0, 0, tiled=True)]
    pallas_call x1 -> x6, Pallas kernels: 1.19 us -> 13.3 us  [the longest x2 5.64 us: scatter(): pl.pallas_call(scatter_body, grid_spec=pltpu.PrefetchScalarGridSpec(num_s...]
    ppermute x12, starting transfers between devices: 30.5 us -> 19.3 us  [shift(): return lax.ppermute(x, 'y', [(s, (s + step) % TP) for s in range(TP)])]
    convert_element_type x6 -> x0, other arithmetic: 9.64 us -> none  [the longest x4 5.04 us: layer(): use = ((tab[j] == ids * 2 + core) & (j < tab[SLOTS])).astype(F32)]
    all_to_all x2 -> x3, starting transfers between devices: 10.9 us -> 19.7 us  [to_chips(): return lax.all_to_all(x, ('z', 'x'), 0, 0, tiled=True)]
    pallas_call x2, Pallas kernels: 55.3 us -> 49.4 us  [attn(): pl.pallas_call(attn_body, grid_spec=pltpu.PrefetchScalarGridSpec(num_scal...]
    ppermute x5, waiting for transfers between devices: 1.53 us -> 3.97 us  [swap(): return lax.ppermute(x, 'core', [(0, 1), (1, 0)])]
  transfers between devices with their start and end apart: 19 -> 20, of which waited for: 7 -> 8; matrix products, arithmetic and copies ran while one was open for 7% -> 0% of each run, Pallas kernels for 30% -> 36%
where the time goes in v4:
time: 199 us; the launch traced here: 197 us
  waiting for transfers between devices  77.6 us (39%)
  Pallas kernels  73.1 us (37%)
  starting transfers between devices  39.4 us (20%)
  local copies, waits for them, and re-layouts  5.12 us (3%)
    ppermute x12, waiting for transfers between devices, shift(): return lax.ppermute(x, 'y', [(s, (s + step) % TP) for s in range(TP)])  51.4 us
    pallas_call x2, Pallas kernels, attn(): pl.pallas_call(attn_body, grid_spec=pltpu.PrefetchScalarGridSpec(num_scal...  49.4 us
    all_to_all x3, waiting for transfers between devices, to_chips(): return lax.all_to_all(x, ('z', 'x'), 0, 0, tiled=True)  22.2 us
    all_to_all x3, starting transfers between devices, to_chips(): return lax.all_to_all(x, ('z', 'x'), 0, 0, tiled=True)  19.7 us
    ppermute x12, starting transfers between devices, shift(): return lax.ppermute(x, 'y', [(s, (s + step) % TP) for s in range(TP)])  19.3 us
    pallas_call x2, Pallas kernels, scatter(): pl.pallas_call(scatter_body, grid_spec=pltpu.PrefetchScalarGridSpec(num_s...  5.64 us
    pallas_call x2, Pallas kernels, place(): pl.pallas_call(functools.partial(place_body, group), grid_spec=pltpu.Pref...  5.45 us
    pallas_call x2, Pallas kernels, split(): pl.pallas_call(functools.partial(split_body, group), grid_spec=pltpu.Pref...  4.94 us
  transfers between devices with their start and end apart: 20, of which 8 were waited for; matrix products, arithmetic and copies ran while one was open for 0% of the time, Pallas kernels for 36%

profile of v4, /device:TPU:0, one launch (start us, length us, event | category | flops | bytes accessed | tf_op | source)
XLA Modules:
  0.0 196.9 jit_solution(5989405979623276028)
XLA Ops:
  4.4 8.0 %all-to-all-start = ((bf16[16,2,128,256]{3,2,1,0:T(8,128)(2,1)}), bf16[16,2,128,256]{3,2,1,0:T(8,128)(2,1)}, u32[]{:S(2)}, u32[]{:S(2)}) async-start(bf16[16,2,128,256]{3,2,1,0:T(8,128)(2,1)} %broadcast_in_dim.15), calls=%async_computation | async-start | bytes 4194304 | tf_op jit(solution)/shard_map/all_to_all | solution.py:461
  12.5 2.4 %split.3 = (bf16[256,1280]{1,0:T(8,128)(2,1)}, bf16[256,1280]{1,0:T(8,128)(2,1)}, bf16[256,1280]{1,0:T(8,128)(2,1)}) custom-call(s32[1]{0:T(128)} %bitcast.y_ref, bf16[256,4096]{1,0:T(8,128)(2,1)} %refs_0_.7, bf16[256,4096]{1,0:T(8,128)(2,1)} %refs_1_.7, bf16[256,1024]{1,0:T(8,128)(2,1)} %refs_2_.7, bf16[256,1024]{1,0:T(8,128)(2,1)} %refs_3_.7), custom_call_target="tpu_custom_call" | custom-call | bytes 4194304 | tf_op jit(solution)/shard_map/split/pallas_call | solution.py:290
  14.9 3.1 %collective-permute-start.9 = (bf16[256,1280]{1,0:T(8,128)(2,1)}, bf16[256,1280]{1,0:T(8,128)(2,1)}, u32[]{:S(2)}, u32[]{:S(2)}) collective-permute-start(bf16[256,1280]{1,0:T(8,128)(2,1)} %get-tuple-element.45), channel_id=1, source_target_pairs={{0,3},{1,0},{2,1},{3,2},{4,7},{5,4},{6,5},{7,6},{8,11},{9,8},{10,9... | collective-permute-start | bytes 1966088 | tf_op jit(solution)/shard_map/ppermute | solution.py:457
  23.4 22.2 %all-to-all-done = bf16[16,2,128,256]{3,2,1,0:T(8,128)(2,1)} async-done(((bf16[16,2,128,256]{3,2,1,0:T(8,128)(2,1)}), bf16[16,2,128,256]{3,2,1,0:T(8,128)(2,1)}, u32[]{:S(2)}, u32[]{:S(2)}) %all-to-all-start) | async-done | bytes 2097184 | tf_op jit(solution)/shard_map/all_to_all | solution.py:461
  45.6 2.5 %pick.1 = bf16[4,128,256]{2,1,0:T(8,128)(2,1)} custom-call(s32[18]{0:T(128)} %get-tuple-element.40.tab_ref.sc, bf16[32,128,256]{2,1,0:T(8,128)(2,1)} %bitcast.8.refs_0_.refs_1_.refs_2_.refs_3_.refs_16_.refs_17_.refs_18_.refs_19_.refs_20_.refs_21_.refs_22_.refs_23_, ...), custom_call_target="tpu_custom_call" | custom-call | bytes 524288 | tf_op jit(solution)/shard_map/pick/pallas_call | solution.py:369
  48.0 2.5 %split.2 = (bf16[256,1280]{1,0:T(8,128)(2,1)}, bf16[256,1280]{1,0:T(8,128)(2,1)}, bf16[256,1280]{1,0:T(8,128)(2,1)}) custom-call(s32[1]{0:T(128)} %bitcast.y_ref, bf16[256,4096]{1,0:T(8,128)(2,1)} %refs_0_.7, bf16[256,4096]{1,0:T(8,128)(2,1)} %refs_1_.7, bf16[256,1024]{1,0:T(8,128)(2,1)} %refs_2_.7, bf16[256,1024]{1,0:T(8,128)(2,1)} %refs_3_.7), custom_call_target="tpu_custom_call" | custom-call | bytes 4194304 | tf_op jit(solution)/shard_map/split/pallas_call | solution.py:290
  50.5 3.1 %collective-permute-start.1 = (bf16[256,1280]{1,0:T(8,128)(2,1)}, bf16[256,1280]{1,0:T(8,128)(2,1)}, u32[]{:S(2)}, u32[]{:S(2)}) collective-permute-start(bf16[256,1280]{1,0:T(8,128)(2,1)} %get-tuple-element.37), channel_id=1, source_target_pairs={{0,3},{1,0},{2,1},{3,2},{4,7},{5,4},{6,5},{7,6},{8,11},{9,8},{10,9... | collective-permute-start | bytes 1966088 | tf_op jit(solution)/shard_map/ppermute | solution.py:457
  55.9 24.7 %attn.3 = (bf16[256,1280]{1,0:T(8,128)(2,1)}, bf16[256,1280]{1,0:T(8,128)(2,1)}, bf16[256,1280]{1,0:T(8,128)(2,1)}, bf16[256,1280]{1,0:T(8,128)(2,1)}, bf16[4,128,256]{2,1,0:T(8,128)(2,1)}) custom-call(s32[18]{0:T(128)} %get-tuple-element.40.tab_ref.sc, bf16[256,4096]{1,0:T(8,128)(2,1)} %refs_0_.7, bf16[256,4096]{1,0:T(8,128)(2,1)} %refs_1_.7, ...), custom_call_target="tpu_custom_call" | custom-call | flops 14495514624 | bytes 6291456 | tf_op jit(solution)/shard_map/attn/pallas_call | solution.py:229
  80.7 2.4 %collective-permute-start.12 = (bf16[256,1280]{1,0:T(8,128)(2,1)}, bf16[256,1280]{1,0:T(8,128)(2,1)}, u32[]{:S(2)}, u32[]{:S(2)}) collective-permute-start(bf16[256,1280]{1,0:T(8,128)(2,1)} %get-tuple-element.49), channel_id=1, source_target_pairs={{0,3},{1,0},{2,1},{3,2},{4,7},{5,4},{6,5},{7,6},{8,11},{9,8},{10,9... | collective-permute-start | bytes 1966088 | tf_op jit(solution)/shard_map/ppermute | solution.py:457
  83.8 2.8 %scatter.3 = bf16[16,128,256]{2,1,0:T(8,128)(2,1)} custom-call(s32[18]{0:T(128)} %get-tuple-element.40.tab_ref.sc, bf16[4,128,256]{2,1,0:T(8,128)(2,1)} %get-tuple-element.61.own_ref, bf16[4,128,256]{2,1,0:T(8,128)(2,1)} %copy-done), custom_call_target="tpu_custom_call" | custom-call | bytes 2097152 | tf_op jit(solution)/shard_map/scatter/pallas_call | solution.py:398
  86.6 4.6 %all-to-all-start.2 = ((bf16[16,128,256]{2,1,0:T(8,128)(2,1)}), bf16[16,128,256]{2,1,0:T(8,128)(2,1)}, u32[]{:S(2)}, u32[]{:S(2)}) async-start(bf16[16,128,256]{2,1,0:T(8,128)(2,1)} %scatter.3), calls=%async_computation.2 | async-start | bytes 2097152 | tf_op jit(solution)/shard_map/all_to_all | solution.py:461
  91.2 24.8 %attn.2 = (bf16[256,1280]{1,0:T(8,128)(2,1)}, bf16[256,1280]{1,0:T(8,128)(2,1)}, bf16[256,1280]{1,0:T(8,128)(2,1)}, bf16[256,1280]{1,0:T(8,128)(2,1)}, bf16[4,128,256]{2,1,0:T(8,128)(2,1)}) custom-call(s32[18]{0:T(128)} %get-tuple-element.36.sc.tab_ref, bf16[256,4096]{1,0:T(8,128)(2,1)} %refs_0_.7, bf16[256,4096]{1,0:T(8,128)(2,1)} %refs_1_.7, ...), custom_call_target="tpu_custom_call" | custom-call | flops 14495514624 | bytes 6291456 | tf_op jit(solution)/shard_map/attn/pallas_call | solution.py:229
  118.5 2.8 %scatter.2 = bf16[16,128,256]{2,1,0:T(8,128)(2,1)} custom-call(s32[18]{0:T(128)} %get-tuple-element.36.sc.tab_ref, bf16[4,128,256]{2,1,0:T(8,128)(2,1)} %get-tuple-element.60.own_ref, bf16[4,128,256]{2,1,0:T(8,128)(2,1)} %copy-done.1), custom_call_target="tpu_custom_call" | custom-call | bytes 2097152 | tf_op jit(solution)/shard_map/scatter/pallas_call | solution.py:398
  121.4 7.1 %all-to-all-start.1 = ((bf16[16,128,256]{2,1,0:T(8,128)(2,1)}), bf16[16,128,256]{2,1,0:T(8,128)(2,1)}, u32[]{:S(2)}, u32[]{:S(2)}) async-start(bf16[16,128,256]{2,1,0:T(8,128)(2,1)} %scatter.2), calls=%async_computation.1 | async-start | bytes 2097152 | tf_op jit(solution)/shard_map/all_to_all | solution.py:461
  128.5 1.8 collective-permute-start.6
  131.9 2.8 %collective-permute-start.7 = (bf16[256,1280]{1,0:T(8,128)(2,1)}, bf16[256,1280]{1,0:T(8,128)(2,1)}, u32[]{:S(2)}, u32[]{:S(2)}) collective-permute-start(bf16[256,1280]{1,0:T(8,128)(2,1)} %get-tuple-element.43), channel_id=1, source_target_pairs={{0,2},{1,3},{2,0},{3,1},{4,6},{5,7},{6,4},{7,5},{8,10},{9,11},{10,... | collective-permute-start | bytes 1966088 | tf_op jit(solution)/shard_map/ppermute | solution.py:457
  136.0 13.5 %collective-permute-done.13.refs_2_ = bf16[256,1280]{1,0:T(8,128)(2,1)} collective-permute-done((bf16[256,1280]{1,0:T(8,128)(2,1)S(1)}, bf16[256,1280]{1,0:T(8,128)(2,1)}, u32[]{:S(2)}, u32[]{:S(2)}) %collective-permute-start.13) | collective-permute-done | bytes 655392 | tf_op jit(solution)/shard_map/ppermute | solution.py:457
  149.5 14.1 %collective-permute-done.14.refs_3_ = bf16[256,1280]{1,0:T(8,128)(2,1)} collective-permute-done((bf16[256,1280]{1,0:T(8,128)(2,1)S(1)}, bf16[256,1280]{1,0:T(8,128)(2,1)}, u32[]{:S(2)}, u32[]{:S(2)}) %collective-permute-start.14) | collective-permute-done | bytes 655392 | tf_op jit(solution)/shard_map/ppermute | solution.py:457
  163.6 2.7 %place.2 = (bf16[256,4096]{1,0:T(8,128)(2,1)}, bf16[256,4096]{1,0:T(8,128)(2,1)}, bf16[256,1024]{1,0:T(8,128)(2,1)}, bf16[256,1024]{1,0:T(8,128)(2,1)}) custom-call(s32[1]{0:T(128)} %bitcast.y_ref, bf16[256,1280]{1,0:T(8,128)(2,1)} %get-tuple-element.48.refs_0_, bf16[256,1280]{1,0:T(8,128)(2,1)} %collective-permute-done.12.refs_1_, ...), custom_call_target="tpu_custom_call" | custom-call | bytes 5242880 | tf_op jit(solution)/shard_map/place/pallas_call | solution.py:335
  166.4 11.3 %collective-permute-done.7.refs_2_ = bf16[256,1280]{1,0:T(8,128)(2,1)} collective-permute-done((bf16[256,1280]{1,0:T(8,128)(2,1)}, bf16[256,1280]{1,0:T(8,128)(2,1)}, u32[]{:S(2)}, u32[]{:S(2)}) %collective-permute-start.7) | collective-permute-done | bytes 655392 | tf_op jit(solution)/shard_map/ppermute | solution.py:457
  177.6 12.6 %collective-permute-done.8.refs_3_ = bf16[256,1280]{1,0:T(8,128)(2,1)} collective-permute-done((bf16[256,1280]{1,0:T(8,128)(2,1)}, bf16[256,1280]{1,0:T(8,128)(2,1)}, u32[]{:S(2)}, u32[]{:S(2)}) %collective-permute-start.8) | collective-permute-done | bytes 655392 | tf_op jit(solution)/shard_map/ppermute | solution.py:457
  190.2 2.7 %place.3 = (bf16[256,4096]{1,0:T(8,128)(2,1)}, bf16[256,4096]{1,0:T(8,128)(2,1)}, bf16[256,1024]{1,0:T(8,128)(2,1)}, bf16[256,1024]{1,0:T(8,128)(2,1)}) custom-call(s32[1]{0:T(128)} %bitcast.y_ref, bf16[256,1280]{1,0:T(8,128)(2,1)} %get-tuple-element.41.refs_0_, ...), custom_call_target="tpu_custom_call", output_to_operand_aliasing={{0}: (5, {}), {1}: (6, {}), {2}: (7, {}), {3}: (8, {})} | custom-call | bytes 5242880 | tf_op jit(solution)/shard_map/place/pallas_call | solution.py:335
  192.9 2.0 %total.2 = (bf16[128,256]{1,0:T(8,128)(2,1)}, bf16[128,256]{1,0:T(8,128)(2,1)}) custom-call(bf16[16,128,256]{2,1,0:T(8,128)(2,1)} %all-to-all-done.2.parts_ref), custom_call_target="tpu_custom_call" | custom-call | bytes 1048576 | tf_op jit(solution)/shard_map/total/pallas_call | solution.py:424
  194.9 2.0 %total.3 = (bf16[128,256]{1,0:T(8,128)(2,1)}, bf16[128,256]{1,0:T(8,128)(2,1)}) custom-call(bf16[16,128,256]{2,1,0:T(8,128)(2,1)} %all-to-all-done.1.parts_ref, bf16[128,256]{1,0:T(8,128)(2,1)} %get-tuple-element.62.refs_0_, bf16[128,256]{1,0:T(8,128)(2,1)} %get-tuple-element.63.refs_1_), custom_call_target="tpu_custom_call", output_to_operand_aliasing={{0}: (1, {}), {1}: (2, {})} | custom-call | bytes 1048576 | tf_op jit(solution)/shard_map/total/pallas_call | solution.py:424
  (48 shorter events, 17.0 us)
Async XLA Ops:
  1.5 1.3 collective-permute-start.4
  4.4 41.1 %all-to-all-start = ((bf16[16,2,128,256]{3,2,1,0:T(8,128)(2,1)}), bf16[16,2,128,256]{3,2,1,0:T(8,128)(2,1)}, u32[]{:S(2)}, u32[]{:S(2)}) async-start(bf16[16,2,128,256]{3,2,1,0:T(8,128)(2,1)} %broadcast_in_dim.15), calls=%async_computation | async-start | bytes 4194304 | tf_op jit(solution)/shard_map/all_to_all | solution.py:461
  12.5 7.8 %copy-start.2 = (s32[1,4]{1,0:T(1,128)S(1)}, s32[1,4]{1,0:T(1,128)}, u32[]{:S(2)}) copy-start(s32[1,4]{1,0:T(1,128)} %param.14) | copy-start | bytes 52
  14.9 38.7 %collective-permute-start.9 = (bf16[256,1280]{1,0:T(8,128)(2,1)}, bf16[256,1280]{1,0:T(8,128)(2,1)}, u32[]{:S(2)}, u32[]{:S(2)}) collective-permute-start(bf16[256,1280]{1,0:T(8,128)(2,1)} %get-tuple-element.45), channel_id=1, source_target_pairs={{0,3},{1,0},{2,1},{3,2},{4,7},{5,4},{6,5},{7,6},{8,11},{9,8},{10,9... | collective-permute-start | bytes 1966088 | tf_op jit(solution)/shard_map/ppermute | solution.py:457
  18.0 36.2 %collective-permute-start.10 = (bf16[256,1280]{1,0:T(8,128)(2,1)}, bf16[256,1280]{1,0:T(8,128)(2,1)}, u32[]{:S(2)}, u32[]{:S(2)}) collective-permute-start(bf16[256,1280]{1,0:T(8,128)(2,1)} %get-tuple-element.46), channel_id=1, source_target_pairs={{0,2},{1,3},{2,0},{3,1},{4,6},{5,7},{6,4},{7,5},{8,10},{9,11},{10,... | collective-permute-start | bytes 1966088 | tf_op jit(solution)/shard_map/ppermute | solution.py:457
  18.7 36.6 %collective-permute-start.11 = (bf16[256,1280]{1,0:T(8,128)(2,1)}, bf16[256,1280]{1,0:T(8,128)(2,1)}, u32[]{:S(2)}, u32[]{:S(2)}) collective-permute-start(bf16[256,1280]{1,0:T(8,128)(2,1)} %get-tuple-element.47), channel_id=1, source_target_pairs={{0,1},{1,2},{2,3},{3,0},{4,5},{5,6},{6,7},{7,4},{8,9},{9,10},{10,1... | collective-permute-start | bytes 1966088 | tf_op jit(solution)/shard_map/ppermute | solution.py:457
  20.4 1.2 collective-permute-start
  48.0 7.2 %collective-permute-start.5 = (bf16[4,128,256]{2,1,0:T(8,128)(2,1)}, bf16[4,128,256]{2,1,0:T(8,128)(2,1)S(1)}, u32[]{:S(2)}, u32[]{:S(2)}) collective-permute-start(bf16[4,128,256]{2,1,0:T(8,128)(2,1)} %pick.1), channel_id=1, source_target_pairs={{0,4},{4,0},{1,5},{5,1},{2,6},{6,2},{3,7},{7,3},{8,12},{12,8},{9,1... | collective-permute-start | bytes 786440 | tf_op jit(solution)/shard_map/ppermute | solution.py:465
  50.5 40.7 %collective-permute-start.1 = (bf16[256,1280]{1,0:T(8,128)(2,1)}, bf16[256,1280]{1,0:T(8,128)(2,1)}, u32[]{:S(2)}, u32[]{:S(2)}) collective-permute-start(bf16[256,1280]{1,0:T(8,128)(2,1)} %get-tuple-element.37), channel_id=1, source_target_pairs={{0,3},{1,0},{2,1},{3,2},{4,7},{5,4},{6,5},{7,6},{8,11},{9,8},{10,9... | collective-permute-start | bytes 1966088 | tf_op jit(solution)/shard_map/ppermute | solution.py:457
  53.6 37.6 %collective-permute-start.2 = (bf16[256,1280]{1,0:T(8,128)(2,1)}, bf16[256,1280]{1,0:T(8,128)(2,1)}, u32[]{:S(2)}, u32[]{:S(2)}) collective-permute-start(bf16[256,1280]{1,0:T(8,128)(2,1)} %get-tuple-element.38), channel_id=1, source_target_pairs={{0,2},{1,3},{2,0},{3,1},{4,6},{5,7},{6,4},{7,5},{8,10},{9,11},{10,... | collective-permute-start | bytes 1966088 | tf_op jit(solution)/shard_map/ppermute | solution.py:457
  54.3 37.0 %collective-permute-start.3 = (bf16[256,1280]{1,0:T(8,128)(2,1)}, bf16[256,1280]{1,0:T(8,128)(2,1)}, u32[]{:S(2)}, u32[]{:S(2)}) collective-permute-start(bf16[256,1280]{1,0:T(8,128)(2,1)} %get-tuple-element.39), channel_id=1, source_target_pairs={{0,1},{1,2},{2,3},{3,0},{4,5},{5,6},{6,7},{7,4},{8,9},{9,10},{10,1... | collective-permute-start | bytes 1966088 | tf_op jit(solution)/shard_map/ppermute | solution.py:457
  55.2 0.7 copy-start.5
  80.6 2.5 %collective-permute-start.16 = (bf16[4,128,256]{2,1,0:T(8,128)(2,1)}, bf16[4,128,256]{2,1,0:T(8,128)(2,1)S(1)}, u32[]{:S(2)}, u32[]{:S(2)}) collective-permute-start(bf16[4,128,256]{2,1,0:T(8,128)(2,1)} %get-tuple-element.61.own_ref), channel_id=1, source_target_pairs={{0,4},{4,0},{1,5},{5,1},{2,6},{6,2},{3,7},{7,3},{8,12},{12,8},{9,1... | collective-permute-start | bytes 786440 | tf_op jit(solution)/shard_map/ppermute | solution.py:465
  80.7 54.0 %collective-permute-start.12 = (bf16[256,1280]{1,0:T(8,128)(2,1)}, bf16[256,1280]{1,0:T(8,128)(2,1)}, u32[]{:S(2)}, u32[]{:S(2)}) collective-permute-start(bf16[256,1280]{1,0:T(8,128)(2,1)} %get-tuple-element.49), channel_id=1, source_target_pairs={{0,3},{1,0},{2,1},{3,2},{4,7},{5,4},{6,5},{7,6},{8,11},{9,8},{10,9... | collective-permute-start | bytes 1966088 | tf_op jit(solution)/shard_map/ppermute | solution.py:457
  86.6 34.7 %all-to-all-start.2 = ((bf16[16,128,256]{2,1,0:T(8,128)(2,1)}), bf16[16,128,256]{2,1,0:T(8,128)(2,1)}, u32[]{:S(2)}, u32[]{:S(2)}) async-start(bf16[16,128,256]{2,1,0:T(8,128)(2,1)} %scatter.3), calls=%async_computation.2 | async-start | bytes 2097152 | tf_op jit(solution)/shard_map/all_to_all | solution.py:461
  116.0 1.8 collective-permute-start.15
  121.4 8.9 %copy-start.4 = (bf16[256,1280]{1,0:T(8,128)(2,1)S(1)}, bf16[256,1280]{1,0:T(8,128)(2,1)}, u32[]{:S(2)}) copy-start(bf16[256,1280]{1,0:T(8,128)(2,1)} %get-tuple-element.50) | copy-start | bytes 1966084
  121.4 10.6 %copy-start.3 = (bf16[256,1280]{1,0:T(8,128)(2,1)S(1)}, bf16[256,1280]{1,0:T(8,128)(2,1)}, u32[]{:S(2)}) copy-start(bf16[256,1280]{1,0:T(8,128)(2,1)} %get-tuple-element.51) | copy-start | bytes 1966084
  121.4 73.6 %all-to-all-start.1 = ((bf16[16,128,256]{2,1,0:T(8,128)(2,1)}), bf16[16,128,256]{2,1,0:T(8,128)(2,1)}, u32[]{:S(2)}, u32[]{:S(2)}) async-start(bf16[16,128,256]{2,1,0:T(8,128)(2,1)} %scatter.2), calls=%async_computation.1 | async-start | bytes 2097152 | tf_op jit(solution)/shard_map/all_to_all | solution.py:461
  128.5 37.9 %collective-permute-start.6 = (bf16[256,1280]{1,0:T(8,128)(2,1)}, bf16[256,1280]{1,0:T(8,128)(2,1)}, u32[]{:S(2)}, u32[]{:S(2)}) collective-permute-start(bf16[256,1280]{1,0:T(8,128)(2,1)} %get-tuple-element.42), channel_id=1, source_target_pairs={{0,3},{1,0},{2,1},{3,2},{4,7},{5,4},{6,5},{7,6},{8,11},{9,8},{10,9... | collective-permute-start | bytes 1966088 | tf_op jit(solution)/shard_map/ppermute | solution.py:457
  130.3 19.3 %collective-permute-start.13 = (bf16[256,1280]{1,0:T(8,128)(2,1)S(1)}, bf16[256,1280]{1,0:T(8,128)(2,1)}, u32[]{:S(2)}, u32[]{:S(2)}) collective-permute-start(bf16[256,1280]{1,0:T(8,128)(2,1)S(1)} %copy-done.4), channel_id=1, source_target_pairs={{0,2},{1,3},{2,0},{3,1},{4,6},{5,7},{6,4},{7,5},{8,10},{9,11},{10,... | collective-permute-start | bytes 1966088 | tf_op jit(solution)/shard_map/ppermute | solution.py:457
  131.9 31.7 %collective-permute-start.14 = (bf16[256,1280]{1,0:T(8,128)(2,1)S(1)}, bf16[256,1280]{1,0:T(8,128)(2,1)}, u32[]{:S(2)}, u32[]{:S(2)}) collective-permute-start(bf16[256,1280]{1,0:T(8,128)(2,1)S(1)} %copy-done.3), channel_id=1, source_target_pairs={{0,1},{1,2},{2,3},{3,0},{4,5},{5,6},{6,7},{7,4},{8,9},{9,10},{10,1... | collective-permute-start | bytes 1966088 | tf_op jit(solution)/shard_map/ppermute | solution.py:457
  131.9 45.7 %collective-permute-start.7 = (bf16[256,1280]{1,0:T(8,128)(2,1)}, bf16[256,1280]{1,0:T(8,128)(2,1)}, u32[]{:S(2)}, u32[]{:S(2)}) collective-permute-start(bf16[256,1280]{1,0:T(8,128)(2,1)} %get-tuple-element.43), channel_id=1, source_target_pairs={{0,2},{1,3},{2,0},{3,1},{4,6},{5,7},{6,4},{7,5},{8,10},{9,11},{10,... | collective-permute-start | bytes 1966088 | tf_op jit(solution)/shard_map/ppermute | solution.py:457
  134.7 55.5 %collective-permute-start.8 = (bf16[256,1280]{1,0:T(8,128)(2,1)}, bf16[256,1280]{1,0:T(8,128)(2,1)}, u32[]{:S(2)}, u32[]{:S(2)}) collective-permute-start(bf16[256,1280]{1,0:T(8,128)(2,1)} %get-tuple-element.44), channel_id=1, source_target_pairs={{0,1},{1,2},{2,3},{3,0},{4,5},{5,6},{6,7},{7,4},{8,9},{9,10},{10,1... | collective-permute-start | bytes 1966088 | tf_op jit(solution)/shard_map/ppermute | solution.py:457
  (2 other events, 1.4 us)

commit v5 on v4

--- a/solution.py
+++ b/solution.py
@@ -18,7 +18,7 @@
 BF16 = jnp.bfloat16
 NN = (((1,), (0,)), ((), ()))
 NT = (((1,), (1,)), ((), ()))
-VMEM = 66_500_000
+VMEM = 67_000_000
 TP = 4
 CHUNK = 256
 SLOTS = 4
@@ -144,11 +144,10 @@
 
     @pl.when(head == 0)
     def _():
-        same = sc[S_CORE]
         for t, dst in ((0, keys), (1, vals)):
             for j in range(SLOTS):
                 a, b = near[t * SLOTS + j][0], far[t * SLOTS + j][0]
-                dst[pl.ds(j * BLOCK, BLOCK), :] = jnp.where(same == sc[S_GROUP], a, b)
+                dst[pl.ds(j * BLOCK, BLOCK), :] = jnp.where(lax.rem(sc[S_OWN + j], 2) == sc[S_CORE], a, b)
             for d in range(TP):
                 at = pl.multiple_of(BEAC + lax.rem(me + d, TP) * CHUNK, CHUNK)
                 dst[pl.ds(at, CHUNK), :] = pieces[d][2 + t][...]
@@ -172,7 +171,7 @@
         mid = (scores.at[e], probs.at[e], dscores.at[e])
         chunks = [chunk_steps(i, qs.at[e], gs.at[e], os.at[e], dqs.at[e], *mid, *tables) for i in range(TP)]
         heads.append((chunks, key_steps(qs.at[e], gs.at[e], *mid[1:], dk_acc, dv_acc)))
-    interleave(heads, 0.3, 2.0)
+    interleave(heads, 0.3, 3.0)
     for d in range(TP):
         at = lax.rem(me + d, TP)
         for e in range(STEP):
@@ -216,11 +215,11 @@
     for t in range(2):
         for j in range(SLOTS):
             ops.append(near)
-            in_specs.append(spec((1, BLOCK, HD), lambda h, sc, j=j, t=t: (sc[S_NEAR + j], 0, t)))
+            in_specs.append(spec((1, BLOCK, HD), lambda h, sc, j=j, t=t: (sc[S_NEAR + j], 0, 2 * t + sc[S_GROUP])))
     for t in range(2):
         for j in range(SLOTS):
             ops.append(far)
-            in_specs.append(spec((1, BLOCK, HD), lambda h, sc, j=j, t=t: (j, 0, t)))
+            in_specs.append(spec((1, BLOCK, HD), lambda h, sc, j=j, t=t: (j, 0, 2 * t + sc[S_GROUP])))
     out_specs = [spec((CHUNK, PIECE), lambda h, sc: (0, 0)) for _ in range(TP)]
     out_specs.append(spec((SLOTS, BLOCK, 2 * HD), lambda h, sc: (0, 0, 0)))
     out_shape = [jax.ShapeDtypeStruct((CHUNK, PIECE), BF16) for _ in range(TP)]
@@ -307,16 +306,17 @@
     )(y, *own)
 
 
-def place_body(group, y_ref, *refs):
-    ins, refs = refs[:TP], refs[TP if group == 0 else TP + 4 :]
+def place_body(entries, held, y_ref, *refs):
+    n = len(entries)
+    ins, refs = refs[:n], refs[n + held :]
     outs, bufs, in_sems, out_sems = refs[:4], refs[4], refs[5], refs[6]
     me = y_ref[0]
-    loads = [pltpu.make_async_copy(ins[i], bufs.at[i], in_sems.at[i]) for i in range(TP)]
+    loads = [pltpu.make_async_copy(ins[i], bufs.at[i], in_sems.at[i]) for i in range(n)]
     for copy in loads:
         copy.start()
     stores = []
-    for i in range(TP):
-        src = lax.rem(me + i, TP) * 2 + group
+    for i, (group, d) in enumerate(entries):
+        src = lax.rem(me + d, TP) * 2 + group
         loads[i].wait()
         for t, (at, width) in enumerate(SPANS):
             col = pl.multiple_of(src * width, HD)
@@ -329,24 +329,25 @@
         copy.wait()
 
 
-def place(group, y, pieces, placed):
+def place(entries, y, pieces, placed):
     anyspec = pl.BlockSpec(memory_space=pl.ANY)
     widths = (TP * 2 * QW, TP * 2 * QW, TP * 2 * HD, TP * 2 * HD)
-    return pl.pallas_call(
-        functools.partial(place_body, group),
+    n = len(entries)
+    return pl.pallas_call(
+        functools.partial(place_body, entries, len(placed)),
         grid_spec=pltpu.PrefetchScalarGridSpec(
             num_scalar_prefetch=1,
             grid=(),
-            in_specs=[anyspec] * (TP + len(placed)),
+            in_specs=[anyspec] * (n + len(placed)),
             out_specs=[anyspec] * 4,
             scratch_shapes=[
-                pltpu.VMEM((TP, CHUNK, PIECE), BF16),
-                pltpu.SemaphoreType.DMA((TP,)),
-                pltpu.SemaphoreType.DMA((TP, 4)),
+                pltpu.VMEM((n, CHUNK, PIECE), BF16),
+                pltpu.SemaphoreType.DMA((n,)),
+                pltpu.SemaphoreType.DMA((n, 4)),
             ],
         ),
         out_shape=[jax.ShapeDtypeStruct((CHUNK, w), BF16) for w in widths],
-        input_output_aliases={1 + TP + t: t for t in range(len(placed))},
+        input_output_aliases={1 + n + t: t for t in range(len(placed))},
         compiler_params=pltpu.CompilerParams(vmem_limit_bytes=VMEM),
         cost_estimate=pl.CostEstimate(flops=0, bytes_accessed=5 << 20, transcendentals=0),
         name="place",
@@ -361,10 +362,9 @@
 def pick(tables, gathered):
     def block(j):
         def at(i, tab):
-            b = tab[S_PEER + j]
-            return (b - lax.rem(b, 2) + (lax.rem(b, 2) ^ tab[S_CORE]), 0, 0)
-
-        return pl.BlockSpec((1, BLOCK, 2 * HD), at)
+            return (lax.div(tab[S_PEER + j], 2), 0, 0)
+
+        return pl.BlockSpec((1,) + gathered.shape[1:], at)
 
     return pl.pallas_call(
         pick_body,
@@ -372,11 +372,11 @@
             num_scalar_prefetch=1,
             grid=(1,),
             in_specs=[block(j) for j in range(SLOTS)],
-            out_specs=pl.BlockSpec((SLOTS, BLOCK, 2 * HD), lambda i, tab: (0, 0, 0)),
+            out_specs=pl.BlockSpec((SLOTS,) + gathered.shape[1:], lambda i, tab: (0, 0, 0)),
         ),
-        out_shape=jax.ShapeDtypeStruct((SLOTS, BLOCK, 2 * HD), BF16),
+        out_shape=jax.ShapeDtypeStruct((SLOTS,) + gathered.shape[1:], BF16),
         compiler_params=pltpu.CompilerParams(vmem_limit_bytes=VMEM),
-        cost_estimate=pl.CostEstimate(flops=0, bytes_accessed=1 << 19, transcendentals=0),
+        cost_estimate=pl.CostEstimate(flops=0, bytes_accessed=1 << 20, transcendentals=0),
         name="pick",
     )(tables, *([gathered] * SLOTS))
 
@@ -470,16 +470,8 @@
     core = lax.axis_index("core")
     chips = lax.axis_size("z") * lax.axis_size("x")
 
-    both = [
-        jnp.concatenate(
-            [beacon_keys[:, g * HD : (g + 1) * HD], beacon_values[:, g * HD : (g + 1) * HD]], axis=1
-        )
-        for g in range(2)
-    ]
-    first = core == 0
-    mine = jnp.where(first, both[0], both[1])
-    other = swap(jnp.where(first, both[1], both[0]))
-    chip_blocks = jnp.broadcast_to(jnp.stack([mine, other])[None], (chips, 2, BLOCK, 2 * HD))
+    block = jnp.concatenate([beacon_keys, beacon_values], axis=1)
+    chip_blocks = jnp.broadcast_to(block[None], (chips,) + block.shape)
     row, count = read_blocks[0], read_counts
     table = jnp.concatenate([row, count])
     peer_table = swap(table)
@@ -495,10 +487,7 @@
         recv.append([got[1], got[2], got[3]])
 
     near = to_chips(chip_blocks)
-    near = near.reshape(chips * 2, BLOCK, 2 * HD)
-
-    chip, parity = row // 2, row % 2
-    scalars = [chip * 2 + (parity ^ core), count, y[None], core[None], table, peer_table]
+    scalars = [row // 2, count, y[None], core[None], table, peer_table]
     scalars = group_tables(jnp.concatenate(scalars).astype(jnp.int32))
     far = swap(pick(scalars[0], near))
     back, summed = [], ()
@@ -513,8 +502,8 @@
         parts = to_chips(dense)
         summed = total(g, parts, summed)
     placed = ()
-    for g in range(2):
-        placed = place(g, place_at, back[g], placed)
+    for entries in (((0, 0), (0, 1), (0, 2), (0, 3), (1, 0)), ((1, 1), (1, 3), (1, 2))):
+        placed = place(entries, place_at, [back[g][d] for g, d in entries], placed)
     out, dq, dk, dv = placed
     return out, dq, dk, dv, *summed
 

time: 199 us -> 192 us (0.965)
  waiting for transfers between devices: 77.6 us -> 74.4 us
  local copies, waits for them, and re-layouts: 5.12 us -> 2.14 us
    unnamed x12 -> x6, local copies, waits for them, and re-layouts: 2.12 us -> 0.01 us
    ppermute x5 -> x4, waiting for transfers between devices: 3.97 us -> 1.87 us  [swap(): return lax.ppermute(x, 'core', [(0, 1), (1, 0)])]
  transfers between devices with their start and end apart: 20 -> 19, of which waited for: 8 -> 6; matrix products, arithmetic and copies ran while one was open for 0% -> 0% of each run, Pallas kernels for 36% -> 37%
where the time goes in v5:
time: 192 us
  waiting for transfers between devices  74.4 us (39%)
  Pallas kernels  73.3 us (38%)
  starting transfers between devices  39.3 us (20%)
  local copies, waits for them, and re-layouts  2.14 us (1%)
    ppermute x12, waiting for transfers between devices, shift(): return lax.ppermute(x, 'y', [(s, (s + step) % TP) for s in range(TP)])  50.4 us
    pallas_call x2, Pallas kernels, attn(): pl.pallas_call(attn_body, grid_spec=pltpu.PrefetchScalarGridSpec(num_scal...  49.5 us
    all_to_all x3, waiting for transfers between devices, to_chips(): return lax.all_to_all(x, ('z', 'x'), 0, 0, tiled=True)  22.1 us
    all_to_all x3, starting transfers between devices, to_chips(): return lax.all_to_all(x, ('z', 'x'), 0, 0, tiled=True)  20.5 us
    ppermute x12, starting transfers between devices, shift(): return lax.ppermute(x, 'y', [(s, (s + step) % TP) for s in range(TP)])  18.7 us
    pallas_call x2, Pallas kernels, scatter(): pl.pallas_call(scatter_body, grid_spec=pltpu.PrefetchScalarGridSpec(num_s...  5.65 us
    pallas_call x2, Pallas kernels, place(): pl.pallas_call(functools.partial(place_body, entries, len(placed)), grid_...  5.45 us
    pallas_call x2, Pallas kernels, split(): pl.pallas_call(functools.partial(split_body, group), grid_spec=pltpu.Pref...  4.96 us
  transfers between devices with their start and end apart: 19, of which 6 were waited for; matrix products, arithmetic and copies ran while one was open for 0% of the time, Pallas kernels for 37%

profile of v5, /device:TPU:0, one launch (start us, length us, event | category | flops | bytes accessed | tf_op | source)
XLA Modules:
  0.0 191.6 jit_solution(4181587540812748811)
XLA Ops:
  3.0 8.2 %all-to-all-start = ((bf16[16,128,512]{2,1,0:T(8,128)(2,1)}), bf16[16,128,512]{2,1,0:T(8,128)(2,1)}, u32[]{:S(2)}, u32[]{:S(2)}) async-start(bf16[16,128,512]{2,1,0:T(8,128)(2,1)} %broadcast_in_dim.15), calls=%async_computation | async-start | bytes 4194304 | tf_op jit(solution)/shard_map/all_to_all | solution.py:461
  12.0 2.5 %split.3 = (bf16[256,1280]{1,0:T(8,128)(2,1)}, bf16[256,1280]{1,0:T(8,128)(2,1)}, bf16[256,1280]{1,0:T(8,128)(2,1)}) custom-call(s32[1]{0:T(128)} %bitcast.y_ref, bf16[256,4096]{1,0:T(8,128)(2,1)} %refs_0_.7, bf16[256,4096]{1,0:T(8,128)(2,1)} %refs_1_.7, bf16[256,1024]{1,0:T(8,128)(2,1)} %refs_2_.7, bf16[256,1024]{1,0:T(8,128)(2,1)} %refs_3_.7), custom_call_target="tpu_custom_call" | custom-call | bytes 4194304 | tf_op jit(solution)/shard_map/split/pallas_call | solution.py:289
  14.5 3.1 %collective-permute-start.8 = (bf16[256,1280]{1,0:T(8,128)(2,1)}, bf16[256,1280]{1,0:T(8,128)(2,1)}, u32[]{:S(2)}, u32[]{:S(2)}) collective-permute-start(bf16[256,1280]{1,0:T(8,128)(2,1)} %get-tuple-element.44), channel_id=1, source_target_pairs={{0,3},{1,0},{2,1},{3,2},{4,7},{5,4},{6,5},{7,6},{8,11},{9,8},{10,9... | collective-permute-start | bytes 1966088 | tf_op jit(solution)/shard_map/ppermute | solution.py:457
  21.0 22.1 %all-to-all-done.refs_0_.refs_1_.refs_2_.refs_3_.refs_16_.refs_17_.refs_18_.refs_19_.refs_20_.refs_21_.refs_22_.refs_23_ = bf16[16,128,512]{2,1,0:T(8,128)(2,1)} async-done(((bf16[16,128,512]{2,1,0:T(8,128)(2,1)}), bf16[16,128,512]{2,1,0:T(8,128)(2,1)}, u32[]{:S(2)}, u32[]{:S(2)}) %all-to-all-start) | async-done | bytes 2097184 | tf_op jit(solution)/shard_map/all_to_all | solution.py:461
  43.1 2.6 %pick.1 = bf16[4,128,512]{2,1,0:T(8,128)(2,1)} custom-call(s32[18]{0:T(128)} %get-tuple-element.40.tab_ref.sc, bf16[16,128,512]{2,1,0:T(8,128)(2,1)} %all-to-all-done.refs_0_.refs_1_.refs_2_.refs_3_.refs_16_.refs_17_.refs_18_.refs_19_.refs_20_.refs_21_.refs_22_.refs_23_, ...), custom_call_target="tpu_custom_call" | custom-call | bytes 1048576 | tf_op jit(solution)/shard_map/pick/pallas_call | solution.py:369
  45.7 2.5 %split.2 = (bf16[256,1280]{1,0:T(8,128)(2,1)}, bf16[256,1280]{1,0:T(8,128)(2,1)}, bf16[256,1280]{1,0:T(8,128)(2,1)}) custom-call(s32[1]{0:T(128)} %bitcast.y_ref, bf16[256,4096]{1,0:T(8,128)(2,1)} %refs_0_.7, bf16[256,4096]{1,0:T(8,128)(2,1)} %refs_1_.7, bf16[256,1024]{1,0:T(8,128)(2,1)} %refs_2_.7, bf16[256,1024]{1,0:T(8,128)(2,1)} %refs_3_.7), custom_call_target="tpu_custom_call" | custom-call | bytes 4194304 | tf_op jit(solution)/shard_map/split/pallas_call | solution.py:289
  48.2 3.1 %collective-permute-start.1 = (bf16[256,1280]{1,0:T(8,128)(2,1)}, bf16[256,1280]{1,0:T(8,128)(2,1)}, u32[]{:S(2)}, u32[]{:S(2)}) collective-permute-start(bf16[256,1280]{1,0:T(8,128)(2,1)} %get-tuple-element.37), channel_id=1, source_target_pairs={{0,3},{1,0},{2,1},{3,2},{4,7},{5,4},{6,5},{7,6},{8,11},{9,8},{10,9... | collective-permute-start | bytes 1966088 | tf_op jit(solution)/shard_map/ppermute | solution.py:457
  52.9 24.7 %attn.3 = (bf16[256,1280]{1,0:T(8,128)(2,1)}, bf16[256,1280]{1,0:T(8,128)(2,1)}, bf16[256,1280]{1,0:T(8,128)(2,1)}, bf16[256,1280]{1,0:T(8,128)(2,1)}, bf16[4,128,256]{2,1,0:T(8,128)(2,1)}) custom-call(s32[18]{0:T(128)} %get-tuple-element.40.tab_ref.sc, bf16[256,4096]{1,0:T(8,128)(2,1)} %refs_0_.7, bf16[256,4096]{1,0:T(8,128)(2,1)} %refs_1_.7, ...), custom_call_target="tpu_custom_call" | custom-call | flops 14495514624 | bytes 6291456 | tf_op jit(solution)/shard_map/attn/pallas_call | solution.py:228
  77.7 2.3 %collective-permute-start.11 = (bf16[256,1280]{1,0:T(8,128)(2,1)}, bf16[256,1280]{1,0:T(8,128)(2,1)}, u32[]{:S(2)}, u32[]{:S(2)}) collective-permute-start(bf16[256,1280]{1,0:T(8,128)(2,1)} %get-tuple-element.48), channel_id=1, source_target_pairs={{0,3},{1,0},{2,1},{3,2},{4,7},{5,4},{6,5},{7,6},{8,11},{9,8},{10,9... | collective-permute-start | bytes 1966088 | tf_op jit(solution)/shard_map/ppermute | solution.py:457
  80.1 2.8 %scatter.3 = bf16[16,128,256]{2,1,0:T(8,128)(2,1)} custom-call(s32[18]{0:T(128)} %get-tuple-element.40.tab_ref.sc, bf16[4,128,256]{2,1,0:T(8,128)(2,1)} %get-tuple-element.61.own_ref, bf16[4,128,256]{2,1,0:T(8,128)(2,1)} %collective-permute-done.15.peer_ref), custom_call_target="tpu_custom_call" | custom-call | bytes 2097152 | tf_op jit(solution)/shard_map/scatter/pallas_call | solution.py:398
  82.9 4.9 %all-to-all-start.2 = ((bf16[16,128,256]{2,1,0:T(8,128)(2,1)}), bf16[16,128,256]{2,1,0:T(8,128)(2,1)}, u32[]{:S(2)}, u32[]{:S(2)}) async-start(bf16[16,128,256]{2,1,0:T(8,128)(2,1)} %scatter.3), calls=%async_computation.2 | async-start | bytes 2097152 | tf_op jit(solution)/shard_map/all_to_all | solution.py:461
  87.9 24.8 %attn.2 = (bf16[256,1280]{1,0:T(8,128)(2,1)}, bf16[256,1280]{1,0:T(8,128)(2,1)}, bf16[256,1280]{1,0:T(8,128)(2,1)}, bf16[256,1280]{1,0:T(8,128)(2,1)}, bf16[4,128,256]{2,1,0:T(8,128)(2,1)}) custom-call(s32[18]{0:T(128)} %get-tuple-element.36.sc.tab_ref, bf16[256,4096]{1,0:T(8,128)(2,1)} %refs_0_.7, bf16[256,4096]{1,0:T(8,128)(2,1)} %refs_1_.7, ...), custom_call_target="tpu_custom_call" | custom-call | flops 14495514624 | bytes 6291456 | tf_op jit(solution)/shard_map/attn/pallas_call | solution.py:228
  114.6 2.8 %scatter.2 = bf16[16,128,256]{2,1,0:T(8,128)(2,1)} custom-call(s32[18]{0:T(128)} %get-tuple-element.36.sc.tab_ref, bf16[4,128,256]{2,1,0:T(8,128)(2,1)} %get-tuple-element.60.own_ref, bf16[4,128,256]{2,1,0:T(8,128)(2,1)} %collective-permute-done.14.peer_ref), custom_call_target="tpu_custom_call" | custom-call | bytes 2097152 | tf_op jit(solution)/shard_map/scatter/pallas_call | solution.py:398
  117.4 7.4 %all-to-all-start.1 = ((bf16[16,128,256]{2,1,0:T(8,128)(2,1)}), bf16[16,128,256]{2,1,0:T(8,128)(2,1)}, u32[]{:S(2)}, u32[]{:S(2)}) async-start(bf16[16,128,256]{2,1,0:T(8,128)(2,1)} %scatter.2), calls=%async_computation.1 | async-start | bytes 2097152 | tf_op jit(solution)/shard_map/all_to_all | solution.py:461
  126.9 2.2 %collective-permute-start.5 = (bf16[256,1280]{1,0:T(8,128)(2,1)}, bf16[256,1280]{1,0:T(8,128)(2,1)}, u32[]{:S(2)}, u32[]{:S(2)}) collective-permute-start(bf16[256,1280]{1,0:T(8,128)(2,1)} %get-tuple-element.41), channel_id=1, source_target_pairs={{0,3},{1,0},{2,1},{3,2},{4,7},{5,4},{6,5},{7,6},{8,11},{9,8},{10,9... | collective-permute-start | bytes 1966088 | tf_op jit(solution)/shard_map/ppermute | solution.py:457
  129.1 2.6 %collective-permute-start.7 = (bf16[256,1280]{1,0:T(8,128)(2,1)}, bf16[256,1280]{1,0:T(8,128)(2,1)}, u32[]{:S(2)}, u32[]{:S(2)}) collective-permute-start(bf16[256,1280]{1,0:T(8,128)(2,1)} %get-tuple-element.43), channel_id=1, source_target_pairs={{0,2},{1,3},{2,0},{3,1},{4,6},{5,7},{6,4},{7,5},{8,10},{9,11},{10,... | collective-permute-start | bytes 1966088 | tf_op jit(solution)/shard_map/ppermute | solution.py:457
  131.8 12.4 %collective-permute-done.12.refs_2_ = bf16[256,1280]{1,0:T(8,128)(2,1)} collective-permute-done((bf16[256,1280]{1,0:T(8,128)(2,1)S(1)}, bf16[256,1280]{1,0:T(8,128)(2,1)}, u32[]{:S(2)}, u32[]{:S(2)}) %collective-permute-start.12) | collective-permute-done | bytes 655392 | tf_op jit(solution)/shard_map/ppermute | solution.py:457
  144.1 13.0 %collective-permute-done.13.refs_3_ = bf16[256,1280]{1,0:T(8,128)(2,1)} collective-permute-done((bf16[256,1280]{1,0:T(8,128)(2,1)S(1)}, bf16[256,1280]{1,0:T(8,128)(2,1)}, u32[]{:S(2)}, u32[]{:S(2)}) %collective-permute-start.13) | collective-permute-done | bytes 655392 | tf_op jit(solution)/shard_map/ppermute | solution.py:457
  157.1 3.0 %place.2 = (bf16[256,4096]{1,0:T(8,128)(2,1)}, bf16[256,4096]{1,0:T(8,128)(2,1)}, bf16[256,1024]{1,0:T(8,128)(2,1)}, bf16[256,1024]{1,0:T(8,128)(2,1)}) custom-call(s32[1]{0:T(128)} %bitcast.y_ref, bf16[256,1280]{1,0:T(8,128)(2,1)} %get-tuple-element.47.refs_0_, bf16[256,1280]{1,0:T(8,128)(2,1)} %collective-permute-done.11.refs_1_, ...), custom_call_target="tpu_custom_call" | custom-call | bytes 5242880 | tf_op jit(solution)/shard_map/place/pallas_call | solution.py:336
  160.1 12.0 %collective-permute-done.6.refs_1_ = bf16[256,1280]{1,0:T(8,128)(2,1)} collective-permute-done((bf16[256,1280]{1,0:T(8,128)(2,1)}, bf16[256,1280]{1,0:T(8,128)(2,1)}, u32[]{:S(2)}, u32[]{:S(2)}) %collective-permute-start.6) | collective-permute-done | bytes 655392 | tf_op jit(solution)/shard_map/ppermute | solution.py:457
  172.1 13.0 %collective-permute-done.7.refs_2_ = bf16[256,1280]{1,0:T(8,128)(2,1)} collective-permute-done((bf16[256,1280]{1,0:T(8,128)(2,1)}, bf16[256,1280]{1,0:T(8,128)(2,1)}, u32[]{:S(2)}, u32[]{:S(2)}) %collective-permute-start.7) | collective-permute-done | bytes 655392 | tf_op jit(solution)/shard_map/ppermute | solution.py:457
  185.1 2.5 %place.3 = (bf16[256,4096]{1,0:T(8,128)(2,1)}, bf16[256,4096]{1,0:T(8,128)(2,1)}, bf16[256,1024]{1,0:T(8,128)(2,1)}, bf16[256,1024]{1,0:T(8,128)(2,1)}) custom-call(s32[1]{0:T(128)} %bitcast.y_ref, bf16[256,1280]{1,0:T(8,128)(2,1)} %collective-permute-done.5.refs_0_, ...), custom_call_target="tpu_custom_call", output_to_operand_aliasing={{0}: (4, {}), {1}: (5, {}), {2}: (6, {}), {3}: (7, {})} | custom-call | bytes 5242880 | tf_op jit(solution)/shard_map/place/pallas_call | solution.py:336
  187.6 2.0 %total.2 = (bf16[128,256]{1,0:T(8,128)(2,1)}, bf16[128,256]{1,0:T(8,128)(2,1)}) custom-call(bf16[16,128,256]{2,1,0:T(8,128)(2,1)} %all-to-all-done.2.parts_ref), custom_call_target="tpu_custom_call" | custom-call | bytes 1048576 | tf_op jit(solution)/shard_map/total/pallas_call | solution.py:424
  189.6 2.0 %total.3 = (bf16[128,256]{1,0:T(8,128)(2,1)}, bf16[128,256]{1,0:T(8,128)(2,1)}) custom-call(bf16[16,128,256]{2,1,0:T(8,128)(2,1)} %all-to-all-done.1.parts_ref, bf16[128,256]{1,0:T(8,128)(2,1)} %get-tuple-element.62.refs_0_, bf16[128,256]{1,0:T(8,128)(2,1)} %get-tuple-element.63.refs_1_), custom_call_target="tpu_custom_call", output_to_operand_aliasing={{0}: (1, {}), {1}: (2, {})} | custom-call | bytes 1048576 | tf_op jit(solution)/shard_map/total/pallas_call | solution.py:424
  (37 shorter events, 11.7 us)
Async XLA Ops:
  3.0 8.8 %copy-start = (s32[1,4]{1,0:T(1,128)S(1)}, s32[1,4]{1,0:T(1,128)}, u32[]{:S(2)}) copy-start(s32[1,4]{1,0:T(1,128)} %param.14) | copy-start | bytes 52
  3.0 40.0 %all-to-all-start = ((bf16[16,128,512]{2,1,0:T(8,128)(2,1)}), bf16[16,128,512]{2,1,0:T(8,128)(2,1)}, u32[]{:S(2)}, u32[]{:S(2)}) async-start(bf16[16,128,512]{2,1,0:T(8,128)(2,1)} %broadcast_in_dim.15), calls=%async_computation | async-start | bytes 4194304 | tf_op jit(solution)/shard_map/all_to_all | solution.py:461
  12.0 7.2 %collective-permute-start = (s32[5]{0:T(128)S(1)}, s32[5]{0:T(128)S(1)}, u32[]{:S(2)}, u32[]{:S(2)}) collective-permute-start(s32[5]{0:T(128)S(1)} %pad_add_fusion), channel_id=1, source_target_pairs={{0,4},{4,0},{1,5},{5,1},{2,6},{6,2},{3,7},{7,3},{8,12},{12,8},{9,1... | collective-permute-start | bytes 68 | tf_op jit(solution)/shard_map/ppermute | solution.py:465
  14.5 36.8 %collective-permute-start.8 = (bf16[256,1280]{1,0:T(8,128)(2,1)}, bf16[256,1280]{1,0:T(8,128)(2,1)}, u32[]{:S(2)}, u32[]{:S(2)}) collective-permute-start(bf16[256,1280]{1,0:T(8,128)(2,1)} %get-tuple-element.44), channel_id=1, source_target_pairs={{0,3},{1,0},{2,1},{3,2},{4,7},{5,4},{6,5},{7,6},{8,11},{9,8},{10,9... | collective-permute-start | bytes 1966088 | tf_op jit(solution)/shard_map/ppermute | solution.py:457
  17.5 34.4 %collective-permute-start.9 = (bf16[256,1280]{1,0:T(8,128)(2,1)}, bf16[256,1280]{1,0:T(8,128)(2,1)}, u32[]{:S(2)}, u32[]{:S(2)}) collective-permute-start(bf16[256,1280]{1,0:T(8,128)(2,1)} %get-tuple-element.45), channel_id=1, source_target_pairs={{0,2},{1,3},{2,0},{3,1},{4,6},{5,7},{6,4},{7,5},{8,10},{9,11},{10,... | collective-permute-start | bytes 1966088 | tf_op jit(solution)/shard_map/ppermute | solution.py:457
  18.2 34.7 %collective-permute-start.10 = (bf16[256,1280]{1,0:T(8,128)(2,1)}, bf16[256,1280]{1,0:T(8,128)(2,1)}, u32[]{:S(2)}, u32[]{:S(2)}) collective-permute-start(bf16[256,1280]{1,0:T(8,128)(2,1)} %get-tuple-element.46), channel_id=1, source_target_pairs={{0,1},{1,2},{2,3},{3,0},{4,5},{5,6},{6,7},{7,4},{8,9},{9,10},{10,1... | collective-permute-start | bytes 1966088 | tf_op jit(solution)/shard_map/ppermute | solution.py:457
  45.7 7.2 %collective-permute-start.4 = (bf16[4,128,512]{2,1,0:T(8,128)(2,1)}, bf16[4,128,512]{2,1,0:T(8,128)(2,1)}, u32[]{:S(2)}, u32[]{:S(2)}) collective-permute-start(bf16[4,128,512]{2,1,0:T(8,128)(2,1)} %pick.1), channel_id=1, source_target_pairs={{0,4},{4,0},{1,5},{5,1},{2,6},{6,2},{3,7},{7,3},{8,12},{12,8},{9,1... | collective-permute-start | bytes 1572872 | tf_op jit(solution)/shard_map/ppermute | solution.py:465
  48.2 39.6 %collective-permute-start.1 = (bf16[256,1280]{1,0:T(8,128)(2,1)}, bf16[256,1280]{1,0:T(8,128)(2,1)}, u32[]{:S(2)}, u32[]{:S(2)}) collective-permute-start(bf16[256,1280]{1,0:T(8,128)(2,1)} %get-tuple-element.37), channel_id=1, source_target_pairs={{0,3},{1,0},{2,1},{3,2},{4,7},{5,4},{6,5},{7,6},{8,11},{9,8},{10,9... | collective-permute-start | bytes 1966088 | tf_op jit(solution)/shard_map/ppermute | solution.py:457
  51.3 36.6 %collective-permute-start.2 = (bf16[256,1280]{1,0:T(8,128)(2,1)}, bf16[256,1280]{1,0:T(8,128)(2,1)}, u32[]{:S(2)}, u32[]{:S(2)}) collective-permute-start(bf16[256,1280]{1,0:T(8,128)(2,1)} %get-tuple-element.38), channel_id=1, source_target_pairs={{0,2},{1,3},{2,0},{3,1},{4,6},{5,7},{6,4},{7,5},{8,10},{9,11},{10,... | collective-permute-start | bytes 1966088 | tf_op jit(solution)/shard_map/ppermute | solution.py:457
  51.9 35.9 %collective-permute-start.3 = (bf16[256,1280]{1,0:T(8,128)(2,1)}, bf16[256,1280]{1,0:T(8,128)(2,1)}, u32[]{:S(2)}, u32[]{:S(2)}) collective-permute-start(bf16[256,1280]{1,0:T(8,128)(2,1)} %get-tuple-element.39), channel_id=1, source_target_pairs={{0,1},{1,2},{2,3},{3,0},{4,5},{5,6},{6,7},{7,4},{8,9},{9,10},{10,1... | collective-permute-start | bytes 1966088 | tf_op jit(solution)/shard_map/ppermute | solution.py:457
  77.6 2.4 %collective-permute-start.15 = (bf16[4,128,256]{2,1,0:T(8,128)(2,1)}, bf16[4,128,256]{2,1,0:T(8,128)(2,1)}, u32[]{:S(2)}, u32[]{:S(2)}) collective-permute-start(bf16[4,128,256]{2,1,0:T(8,128)(2,1)} %get-tuple-element.61.own_ref), channel_id=1, source_target_pairs={{0,4},{4,0},{1,5},{5,1},{2,6},{6,2},{3,7},{7,3},{8,12},{12,8},{9,1... | collective-permute-start | bytes 786440 | tf_op jit(solution)/shard_map/ppermute | solution.py:465
  77.7 51.4 %collective-permute-start.11 = (bf16[256,1280]{1,0:T(8,128)(2,1)}, bf16[256,1280]{1,0:T(8,128)(2,1)}, u32[]{:S(2)}, u32[]{:S(2)}) collective-permute-start(bf16[256,1280]{1,0:T(8,128)(2,1)} %get-tuple-element.48), channel_id=1, source_target_pairs={{0,3},{1,0},{2,1},{3,2},{4,7},{5,4},{6,5},{7,6},{8,11},{9,8},{10,9... | collective-permute-start | bytes 1966088 | tf_op jit(solution)/shard_map/ppermute | solution.py:457
  82.9 34.5 %all-to-all-start.2 = ((bf16[16,128,256]{2,1,0:T(8,128)(2,1)}), bf16[16,128,256]{2,1,0:T(8,128)(2,1)}, u32[]{:S(2)}, u32[]{:S(2)}) async-start(bf16[16,128,256]{2,1,0:T(8,128)(2,1)} %scatter.3), calls=%async_computation.2 | async-start | bytes 2097152 | tf_op jit(solution)/shard_map/all_to_all | solution.py:461
  112.6 2.0 %collective-permute-start.14 = (bf16[4,128,256]{2,1,0:T(8,128)(2,1)}, bf16[4,128,256]{2,1,0:T(8,128)(2,1)}, u32[]{:S(2)}, u32[]{:S(2)}) collective-permute-start(bf16[4,128,256]{2,1,0:T(8,128)(2,1)} %get-tuple-element.60.own_ref), channel_id=1, source_target_pairs={{0,4},{4,0},{1,5},{5,1},{2,6},{6,2},{3,7},{7,3},{8,12},{12,8},{9,1... | collective-permute-start | bytes 786440 | tf_op jit(solution)/shard_map/ppermute | solution.py:465
  117.4 7.4 %copy-start.2 = (bf16[256,1280]{1,0:T(8,128)(2,1)S(1)}, bf16[256,1280]{1,0:T(8,128)(2,1)}, u32[]{:S(2)}) copy-start(bf16[256,1280]{1,0:T(8,128)(2,1)} %get-tuple-element.49) | copy-start | bytes 1966084
  117.4 8.5 %copy-start.1 = (bf16[256,1280]{1,0:T(8,128)(2,1)S(1)}, bf16[256,1280]{1,0:T(8,128)(2,1)}, u32[]{:S(2)}) copy-start(bf16[256,1280]{1,0:T(8,128)(2,1)} %get-tuple-element.50) | copy-start | bytes 1966084
  117.4 72.2 %all-to-all-start.1 = ((bf16[16,128,256]{2,1,0:T(8,128)(2,1)}), bf16[16,128,256]{2,1,0:T(8,128)(2,1)}, u32[]{:S(2)}, u32[]{:S(2)}) async-start(bf16[16,128,256]{2,1,0:T(8,128)(2,1)} %scatter.2), calls=%async_computation.1 | async-start | bytes 2097152 | tf_op jit(solution)/shard_map/all_to_all | solution.py:461
  124.8 19.3 %collective-permute-start.12 = (bf16[256,1280]{1,0:T(8,128)(2,1)S(1)}, bf16[256,1280]{1,0:T(8,128)(2,1)}, u32[]{:S(2)}, u32[]{:S(2)}) collective-permute-start(bf16[256,1280]{1,0:T(8,128)(2,1)S(1)} %copy-done.2), channel_id=1, source_target_pairs={{0,2},{1,3},{2,0},{3,1},{4,6},{5,7},{6,4},{7,5},{8,10},{9,11},{10,... | collective-permute-start | bytes 1966088 | tf_op jit(solution)/shard_map/ppermute | solution.py:457
  125.9 31.2 %collective-permute-start.13 = (bf16[256,1280]{1,0:T(8,128)(2,1)S(1)}, bf16[256,1280]{1,0:T(8,128)(2,1)}, u32[]{:S(2)}, u32[]{:S(2)}) collective-permute-start(bf16[256,1280]{1,0:T(8,128)(2,1)S(1)} %copy-done.1), channel_id=1, source_target_pairs={{0,1},{1,2},{2,3},{3,0},{4,5},{5,6},{6,7},{7,4},{8,9},{9,10},{10,1... | collective-permute-start | bytes 1966088 | tf_op jit(solution)/shard_map/ppermute | solution.py:457
  126.9 33.2 %collective-permute-start.5 = (bf16[256,1280]{1,0:T(8,128)(2,1)}, bf16[256,1280]{1,0:T(8,128)(2,1)}, u32[]{:S(2)}, u32[]{:S(2)}) collective-permute-start(bf16[256,1280]{1,0:T(8,128)(2,1)} %get-tuple-element.41), channel_id=1, source_target_pairs={{0,3},{1,0},{2,1},{3,2},{4,7},{5,4},{6,5},{7,6},{8,11},{9,8},{10,9... | collective-permute-start | bytes 1966088 | tf_op jit(solution)/shard_map/ppermute | solution.py:457
  129.1 43.0 %collective-permute-start.6 = (bf16[256,1280]{1,0:T(8,128)(2,1)}, bf16[256,1280]{1,0:T(8,128)(2,1)}, u32[]{:S(2)}, u32[]{:S(2)}) collective-permute-start(bf16[256,1280]{1,0:T(8,128)(2,1)} %get-tuple-element.42), channel_id=1, source_target_pairs={{0,1},{1,2},{2,3},{3,0},{4,5},{5,6},{6,7},{7,4},{8,9},{9,10},{10,1... | collective-permute-start | bytes 1966088 | tf_op jit(solution)/shard_map/ppermute | solution.py:457
  129.1 56.0 %collective-permute-start.7 = (bf16[256,1280]{1,0:T(8,128)(2,1)}, bf16[256,1280]{1,0:T(8,128)(2,1)}, u32[]{:S(2)}, u32[]{:S(2)}) collective-permute-start(bf16[256,1280]{1,0:T(8,128)(2,1)} %get-tuple-element.43), channel_id=1, source_target_pairs={{0,2},{1,3},{2,0},{3,1},{4,6},{5,7},{6,4},{7,5},{8,10},{9,11},{10,... | collective-permute-start | bytes 1966088 | tf_op jit(solution)/shard_map/ppermute | solution.py:457

commit v6 on v5

--- a/solution.py
+++ b/solution.py
@@ -138,7 +138,7 @@
     near, far = refs[: 2 * SLOTS], refs[2 * SLOTS : 4 * SLOTS]
     refs = refs[4 * SLOTS :]
     outs, beac_out = refs[:TP], refs[TP]
-    qs, gs, os, dqs, keys, vals, keys_t, vals_t, bias, scores, probs, dscores, dk_acc, dv_acc = refs[TP + 1 :]
+    qs, gs, os, dqs, keys, vals, keys_t, vals_t, bias, scores, probs, dscores, dk_acc, dv_acc, dkv, sems, kv_sems = refs[TP + 1 :]
     head = pl.program_id(0)
     me = sc[S_Y]
 
@@ -169,27 +169,39 @@
     heads = []
     for e in range(STEP):
         mid = (scores.at[e], probs.at[e], dscores.at[e])
-        chunks = [chunk_steps(i, qs.at[e], gs.at[e], os.at[e], dqs.at[e], *mid, *tables) for i in range(TP)]
+        chunks = [chunk_steps(i, qs.at[e], gs.at[e], os.at[head * STEP + e], dqs.at[head * STEP + e], *mid, *tables) for i in range(TP)]
         heads.append((chunks, key_steps(qs.at[e], gs.at[e], *mid[1:], dk_acc, dv_acc)))
     interleave(heads, 0.3, 3.0)
-    for d in range(TP):
-        at = lax.rem(me + d, TP)
-        for e in range(STEP):
-            at_o = pl.multiple_of((head * STEP + e) * HD, HD)
-            at_q = pl.multiple_of(QW + (head * STEP + e) * HD, HD)
-            outs[d][:, pl.ds(at_o, HD)] = os[e, at]
-            outs[d][:, pl.ds(at_q, HD)] = dqs[e, at]
+
+    def leave(h, d, t):
+        src = (os, dqs)[t].at[h, lax.rem(me + d, TP)]
+        col = pl.multiple_of(t * QW + h * HD, HD)
+        return pltpu.make_async_copy(src, outs[d].at[:, pl.ds(col, HD)], sems.at[h, d, t])
+
+    for e in range(STEP):
+        for d in range(TP):
+            for t in range(2):
+                leave(head * STEP + e, d, t).start()
 
     @pl.when(head == GROUP // STEP - 1)
     def _():
+        tails = []
         for d in range(TP):
             at = pl.multiple_of(BEAC + lax.rem(me + d, TP) * CHUNK, CHUNK)
-            outs[d][:, 2 * QW : 2 * QW + HD] = (dk_acc[pl.ds(at, CHUNK), :] * SCALE).astype(BF16)
-            outs[d][:, 2 * QW + HD :] = dv_acc[pl.ds(at, CHUNK), :].astype(BF16)
+            dkv[d, :, :HD] = (dk_acc[pl.ds(at, CHUNK), :] * SCALE).astype(BF16)
+            dkv[d, :, HD:] = dv_acc[pl.ds(at, CHUNK), :].astype(BF16)
+            tails.append(pltpu.make_async_copy(dkv.at[d], outs[d].at[:, pl.ds(2 * QW, 2 * HD)], kv_sems.at[d]))
+            tails[d].start()
         for j in range(SLOTS):
             rows = pl.ds(j * BLOCK, BLOCK)
             beac_out[j, :, :HD] = (dk_acc[rows, :] * SCALE).astype(BF16)
             beac_out[j, :, HD:] = dv_acc[rows, :].astype(BF16)
+        for h in range(GROUP):
+            for d in range(TP):
+                for t in range(2):
+                    leave(h, d, t).wait()
+        for copy in tails:
+            copy.wait()
 
 
 def attn(scalars, own, pieces, near, far):
@@ -220,7 +232,7 @@
         for j in range(SLOTS):
             ops.append(far)
             in_specs.append(spec((1, BLOCK, HD), lambda h, sc, j=j, t=t: (j, 0, 2 * t + sc[S_GROUP])))
-    out_specs = [spec((CHUNK, PIECE), lambda h, sc: (0, 0)) for _ in range(TP)]
+    out_specs = [spec(memory_space=pl.ANY) for _ in range(TP)]
     out_specs.append(spec((SLOTS, BLOCK, 2 * HD), lambda h, sc: (0, 0, 0)))
     out_shape = [jax.ShapeDtypeStruct((CHUNK, PIECE), BF16) for _ in range(TP)]
     out_shape.append(jax.ShapeDtypeStruct((SLOTS, BLOCK, 2 * HD), BF16))
@@ -235,8 +247,8 @@
             scratch_shapes=[
                 pltpu.VMEM((STEP, TP, CHUNK, HD), BF16),
                 pltpu.VMEM((STEP, TP, CHUNK, HD), BF16),
-                pltpu.VMEM((STEP, TP, CHUNK, HD), BF16),
-                pltpu.VMEM((STEP, TP, CHUNK, HD), BF16),
+                pltpu.VMEM((GROUP, TP, CHUNK, HD), BF16),
+                pltpu.VMEM((GROUP, TP, CHUNK, HD), BF16),
                 pltpu.VMEM((KEYS, HD), BF16),
                 pltpu.VMEM((KEYS, HD), BF16),
                 pltpu.VMEM((HD, KEYS), BF16),
@@ -247,6 +259,9 @@
                 pltpu.VMEM((STEP, KEYS, TP * CHUNK), BF16),
                 pltpu.VMEM((KEYS, HD), F32),
                 pltpu.VMEM((KEYS, HD), F32),
+                pltpu.VMEM((TP, CHUNK, 2 * HD), BF16),
+                pltpu.SemaphoreType.DMA((GROUP, TP, 2)),
+                pltpu.SemaphoreType.DMA((TP,)),
             ],
         ),
         out_shape=out_shape,
@@ -354,6 +369,38 @@
     )(y, *pieces, *placed)
 
 
+def spread_body(k_ref, v_ref, out_ref, buf, in_sems, out_sems):
+    halves = (buf.at[:, : 2 * HD], buf.at[:, 2 * HD :])
+    loads = [pltpu.make_async_copy(r, h, in_sems.at[t]) for t, (r, h) in enumerate(zip((k_ref, v_ref), halves))]
+    for copy in loads:
+        copy.start()
+    for copy in loads:
+        copy.wait()
+    stores = [pltpu.make_async_copy(buf, out_ref.at[n], out_sems.at[n]) for n in range(out_ref.shape[0])]
+    for copy in stores:
+        copy.start()
+    for copy in stores:
+        copy.wait()
+
+
+def spread(beacon_keys, beacon_values, chips):
+    anyspec = pl.BlockSpec(memory_space=pl.ANY)
+    return pl.pallas_call(
+        spread_body,
+        in_specs=[anyspec] * 2,
+        out_specs=anyspec,
+        out_shape=jax.ShapeDtypeStruct((chips, BLOCK, 4 * HD), BF16),
+        scratch_shapes=[
+            pltpu.VMEM((BLOCK, 4 * HD), BF16),
+            pltpu.SemaphoreType.DMA((2,)),
+            pltpu.SemaphoreType.DMA((chips,)),
+        ],
+        compiler_params=pltpu.CompilerParams(vmem_limit_bytes=VMEM),
+        cost_estimate=pl.CostEstimate(flops=0, bytes_accessed=2 << 20, transcendentals=0),
+        name="spread",
+    )(beacon_keys, beacon_values)
+
+
 def pick_body(tab_ref, *refs):
     for j in range(SLOTS):
         refs[SLOTS][j] = refs[j][0]
@@ -470,8 +517,7 @@
     core = lax.axis_index("core")
     chips = lax.axis_size("z") * lax.axis_size("x")
 
-    block = jnp.concatenate([beacon_keys, beacon_values], axis=1)
-    chip_blocks = jnp.broadcast_to(block[None], (chips,) + block.shape)
+    chip_blocks = spread(beacon_keys, beacon_values, chips)
     row, count = read_blocks[0], read_counts
     table = jnp.concatenate([row, count])
     peer_table = swap(table)
@@ -482,7 +528,7 @@
     for g in range(2):
         got = {}
         sent = split(g, place_at, own)
-        for d in (1, 3, 2):
+        for d in (2, 1, 3):
             got[TP - d] = shift(sent[d - 1], d)
         recv.append([got[1], got[2], got[3]])
 
@@ -494,7 +540,7 @@
     for g in range(2):
         res = attn(scalars[g], own, recv[g], near, far)
         got = {0: res[0]}
-        for d in (1, 3, 2):
+        for d in (2, 1, 3):
             got[TP - d] = shift(res[d], d)
         back.append([got[d] for d in range(TP)])
         peer = swap(res[TP])

time: 192 us -> 192 us (level)
  Pallas kernels: 73.3 us -> 75.9 us
    pallas_call x0 -> x1, Pallas kernels: none -> 2.32 us  [spread(): pl.pallas_call(spread_body, in_specs=[anyspec] * 2, out_specs=anyspec, ou...]
where the time goes in v6:
time: 192 us
  Pallas kernels  75.9 us (40%)
  waiting for transfers between devices  74.4 us (39%)
  starting transfers between devices  39.2 us (20%)
    ppermute x12, waiting for transfers between devices, shift(): return lax.ppermute(x, 'y', [(s, (s + step) % TP) for s in range(TP)])  50.4 us
    pallas_call x2, Pallas kernels, attn(): pl.pallas_call(attn_body, grid_spec=pltpu.PrefetchScalarGridSpec(num_scal...  49.8 us
    all_to_all x3, waiting for transfers between devices, to_chips(): return lax.all_to_all(x, ('z', 'x'), 0, 0, tiled=True)  22.1 us
    all_to_all x3, starting transfers between devices, to_chips(): return lax.all_to_all(x, ('z', 'x'), 0, 0, tiled=True)  20.4 us
    ppermute x12, starting transfers between devices, shift(): return lax.ppermute(x, 'y', [(s, (s + step) % TP) for s in range(TP)])  18.6 us
    pallas_call x2, Pallas kernels, scatter(): pl.pallas_call(scatter_body, grid_spec=pltpu.PrefetchScalarGridSpec(num_s...  5.65 us
    pallas_call x2, Pallas kernels, place(): pl.pallas_call(functools.partial(place_body, entries, len(placed)), grid_...  5.45 us
    pallas_call x2, Pallas kernels, split(): pl.pallas_call(functools.partial(split_body, group), grid_spec=pltpu.Pref...  4.96 us
  transfers between devices with their start and end apart: 19, of which 6 were waited for; matrix products, arithmetic and copies ran while one was open for 0% of the time, Pallas kernels for 37%

profile of v6, /device:TPU:0, one launch (start us, length us, event | category | flops | bytes accessed | tf_op | source)
XLA Modules:
  0.0 191.7 jit_solution(4985369651885702842)
XLA Ops:
  0.6 2.3 %spread.1 = bf16[16,128,512]{2,1,0:T(8,128)(2,1)} custom-call(bf16[128,256]{1,0:T(8,128)(2,1)} %k_ref.1, bf16[128,256]{1,0:T(8,128)(2,1)} %v_ref.1), custom_call_target="tpu_custom_call" | custom-call | bytes 2097152 | tf_op jit(solution)/shard_map/spread/pallas_call | solution.py:388
  3.0 8.1 %all-to-all-start = ((bf16[16,128,512]{2,1,0:T(8,128)(2,1)}), bf16[16,128,512]{2,1,0:T(8,128)(2,1)}, u32[]{:S(2)}, u32[]{:S(2)}) async-start(bf16[16,128,512]{2,1,0:T(8,128)(2,1)} %spread.1), calls=%async_computation | async-start | bytes 4194304 | tf_op jit(solution)/shard_map/all_to_all | solution.py:508
  11.8 2.5 %split.3 = (bf16[256,1280]{1,0:T(8,128)(2,1)}, bf16[256,1280]{1,0:T(8,128)(2,1)}, bf16[256,1280]{1,0:T(8,128)(2,1)}) custom-call(s32[1]{0:T(128)} %bitcast.y_ref, bf16[256,4096]{1,0:T(8,128)(2,1)} %refs_0_.7, bf16[256,4096]{1,0:T(8,128)(2,1)} %refs_1_.7, bf16[256,1024]{1,0:T(8,128)(2,1)} %refs_2_.7, bf16[256,1024]{1,0:T(8,128)(2,1)} %refs_3_.7), custom_call_target="tpu_custom_call" | custom-call | bytes 4194304 | tf_op jit(solution)/shard_map/split/pallas_call | solution.py:304
  14.3 3.1 %collective-permute-start.8 = (bf16[256,1280]{1,0:T(8,128)(2,1)}, bf16[256,1280]{1,0:T(8,128)(2,1)}, u32[]{:S(2)}, u32[]{:S(2)}) collective-permute-start(bf16[256,1280]{1,0:T(8,128)(2,1)} %get-tuple-element.44), channel_id=1, source_target_pairs={{0,3},{1,0},{2,1},{3,2},{4,7},{5,4},{6,5},{7,6},{8,11},{9,8},{10,9... | collective-permute-start | bytes 1966088 | tf_op jit(solution)/shard_map/ppermute | solution.py:504
  20.8 22.1 %all-to-all-done.refs_0_.refs_1_.refs_2_.refs_3_.refs_16_.refs_17_.refs_18_.refs_19_.refs_20_.refs_21_.refs_22_.refs_23_ = bf16[16,128,512]{2,1,0:T(8,128)(2,1)} async-done(((bf16[16,128,512]{2,1,0:T(8,128)(2,1)}), bf16[16,128,512]{2,1,0:T(8,128)(2,1)}, u32[]{:S(2)}, u32[]{:S(2)}) %all-to-all-start) | async-done | bytes 2097184 | tf_op jit(solution)/shard_map/all_to_all | solution.py:508
  42.9 2.6 %pick.1 = bf16[4,128,512]{2,1,0:T(8,128)(2,1)} custom-call(s32[18]{0:T(128)} %get-tuple-element.40.tab_ref.sc, bf16[16,128,512]{2,1,0:T(8,128)(2,1)} %all-to-all-done.refs_0_.refs_1_.refs_2_.refs_3_.refs_16_.refs_17_.refs_18_.refs_19_.refs_20_.refs_21_.refs_22_.refs_23_, ...), custom_call_target="tpu_custom_call" | custom-call | bytes 1048576 | tf_op jit(solution)/shard_map/pick/pallas_call | solution.py:416
  45.5 2.5 %split.2 = (bf16[256,1280]{1,0:T(8,128)(2,1)}, bf16[256,1280]{1,0:T(8,128)(2,1)}, bf16[256,1280]{1,0:T(8,128)(2,1)}) custom-call(s32[1]{0:T(128)} %bitcast.y_ref, bf16[256,4096]{1,0:T(8,128)(2,1)} %refs_0_.7, bf16[256,4096]{1,0:T(8,128)(2,1)} %refs_1_.7, bf16[256,1024]{1,0:T(8,128)(2,1)} %refs_2_.7, bf16[256,1024]{1,0:T(8,128)(2,1)} %refs_3_.7), custom_call_target="tpu_custom_call" | custom-call | bytes 4194304 | tf_op jit(solution)/shard_map/split/pallas_call | solution.py:304
  48.0 3.1 %collective-permute-start.1 = (bf16[256,1280]{1,0:T(8,128)(2,1)}, bf16[256,1280]{1,0:T(8,128)(2,1)}, u32[]{:S(2)}, u32[]{:S(2)}) collective-permute-start(bf16[256,1280]{1,0:T(8,128)(2,1)} %get-tuple-element.37), channel_id=1, source_target_pairs={{0,3},{1,0},{2,1},{3,2},{4,7},{5,4},{6,5},{7,6},{8,11},{9,8},{10,9... | collective-permute-start | bytes 1966088 | tf_op jit(solution)/shard_map/ppermute | solution.py:504
  52.7 24.9 %attn.3 = (bf16[256,1280]{1,0:T(8,128)(2,1)}, bf16[256,1280]{1,0:T(8,128)(2,1)}, bf16[256,1280]{1,0:T(8,128)(2,1)}, bf16[256,1280]{1,0:T(8,128)(2,1)}, bf16[4,128,256]{2,1,0:T(8,128)(2,1)}) custom-call(s32[18]{0:T(128)} %get-tuple-element.40.tab_ref.sc, bf16[256,4096]{1,0:T(8,128)(2,1)} %refs_0_.7, bf16[256,4096]{1,0:T(8,128)(2,1)} %refs_1_.7, ...), custom_call_target="tpu_custom_call" | custom-call | flops 14495514624 | bytes 6291456 | tf_op jit(solution)/shard_map/attn/pallas_call | solution.py:240
  77.7 2.3 %collective-permute-start.11 = (bf16[256,1280]{1,0:T(8,128)(2,1)}, bf16[256,1280]{1,0:T(8,128)(2,1)}, u32[]{:S(2)}, u32[]{:S(2)}) collective-permute-start(bf16[256,1280]{1,0:T(8,128)(2,1)} %get-tuple-element.48), channel_id=1, source_target_pairs={{0,3},{1,0},{2,1},{3,2},{4,7},{5,4},{6,5},{7,6},{8,11},{9,8},{10,9... | collective-permute-start | bytes 1966088 | tf_op jit(solution)/shard_map/ppermute | solution.py:504
  80.0 2.8 %scatter.3 = bf16[16,128,256]{2,1,0:T(8,128)(2,1)} custom-call(s32[18]{0:T(128)} %get-tuple-element.40.tab_ref.sc, bf16[4,128,256]{2,1,0:T(8,128)(2,1)} %get-tuple-element.61.own_ref, bf16[4,128,256]{2,1,0:T(8,128)(2,1)} %collective-permute-done.15.peer_ref), custom_call_target="tpu_custom_call" | custom-call | bytes 2097152 | tf_op jit(solution)/shard_map/scatter/pallas_call | solution.py:445
  82.8 5.0 %all-to-all-start.2 = ((bf16[16,128,256]{2,1,0:T(8,128)(2,1)}), bf16[16,128,256]{2,1,0:T(8,128)(2,1)}, u32[]{:S(2)}, u32[]{:S(2)}) async-start(bf16[16,128,256]{2,1,0:T(8,128)(2,1)} %scatter.3), calls=%async_computation.2 | async-start | bytes 2097152 | tf_op jit(solution)/shard_map/all_to_all | solution.py:508
  87.8 24.9 %attn.2 = (bf16[256,1280]{1,0:T(8,128)(2,1)}, bf16[256,1280]{1,0:T(8,128)(2,1)}, bf16[256,1280]{1,0:T(8,128)(2,1)}, bf16[256,1280]{1,0:T(8,128)(2,1)}, bf16[4,128,256]{2,1,0:T(8,128)(2,1)}) custom-call(s32[18]{0:T(128)} %get-tuple-element.36.sc.tab_ref, bf16[256,4096]{1,0:T(8,128)(2,1)} %refs_0_.7, bf16[256,4096]{1,0:T(8,128)(2,1)} %refs_1_.7, ...), custom_call_target="tpu_custom_call" | custom-call | flops 14495514624 | bytes 6291456 | tf_op jit(solution)/shard_map/attn/pallas_call | solution.py:240
  114.7 2.8 %scatter.2 = bf16[16,128,256]{2,1,0:T(8,128)(2,1)} custom-call(s32[18]{0:T(128)} %get-tuple-element.36.sc.tab_ref, bf16[4,128,256]{2,1,0:T(8,128)(2,1)} %get-tuple-element.60.own_ref, bf16[4,128,256]{2,1,0:T(8,128)(2,1)} %collective-permute-done.14.peer_ref), custom_call_target="tpu_custom_call" | custom-call | bytes 2097152 | tf_op jit(solution)/shard_map/scatter/pallas_call | solution.py:445
  117.5 7.4 %all-to-all-start.1 = ((bf16[16,128,256]{2,1,0:T(8,128)(2,1)}), bf16[16,128,256]{2,1,0:T(8,128)(2,1)}, u32[]{:S(2)}, u32[]{:S(2)}) async-start(bf16[16,128,256]{2,1,0:T(8,128)(2,1)} %scatter.2), calls=%async_computation.1 | async-start | bytes 2097152 | tf_op jit(solution)/shard_map/all_to_all | solution.py:508
  126.9 2.3 %collective-permute-start.5 = (bf16[256,1280]{1,0:T(8,128)(2,1)}, bf16[256,1280]{1,0:T(8,128)(2,1)}, u32[]{:S(2)}, u32[]{:S(2)}) collective-permute-start(bf16[256,1280]{1,0:T(8,128)(2,1)} %get-tuple-element.41), channel_id=1, source_target_pairs={{0,3},{1,0},{2,1},{3,2},{4,7},{5,4},{6,5},{7,6},{8,11},{9,8},{10,9... | collective-permute-start | bytes 1966088 | tf_op jit(solution)/shard_map/ppermute | solution.py:504
  129.2 2.7 %collective-permute-start.7 = (bf16[256,1280]{1,0:T(8,128)(2,1)}, bf16[256,1280]{1,0:T(8,128)(2,1)}, u32[]{:S(2)}, u32[]{:S(2)}) collective-permute-start(bf16[256,1280]{1,0:T(8,128)(2,1)} %get-tuple-element.43), channel_id=1, source_target_pairs={{0,2},{1,3},{2,0},{3,1},{4,6},{5,7},{6,4},{7,5},{8,10},{9,11},{10,... | collective-permute-start | bytes 1966088 | tf_op jit(solution)/shard_map/ppermute | solution.py:504
  131.8 12.4 %collective-permute-done.12.refs_2_ = bf16[256,1280]{1,0:T(8,128)(2,1)} collective-permute-done((bf16[256,1280]{1,0:T(8,128)(2,1)S(1)}, bf16[256,1280]{1,0:T(8,128)(2,1)}, u32[]{:S(2)}, u32[]{:S(2)}) %collective-permute-start.12) | collective-permute-done | bytes 655392 | tf_op jit(solution)/shard_map/ppermute | solution.py:504
  144.2 13.0 %collective-permute-done.13.refs_3_ = bf16[256,1280]{1,0:T(8,128)(2,1)} collective-permute-done((bf16[256,1280]{1,0:T(8,128)(2,1)S(1)}, bf16[256,1280]{1,0:T(8,128)(2,1)}, u32[]{:S(2)}, u32[]{:S(2)}) %collective-permute-start.13) | collective-permute-done | bytes 655392 | tf_op jit(solution)/shard_map/ppermute | solution.py:504
  157.2 3.0 %place.2 = (bf16[256,4096]{1,0:T(8,128)(2,1)}, bf16[256,4096]{1,0:T(8,128)(2,1)}, bf16[256,1024]{1,0:T(8,128)(2,1)}, bf16[256,1024]{1,0:T(8,128)(2,1)}) custom-call(s32[1]{0:T(128)} %bitcast.y_ref, bf16[256,1280]{1,0:T(8,128)(2,1)} %get-tuple-element.47.refs_0_, bf16[256,1280]{1,0:T(8,128)(2,1)} %collective-permute-done.11.refs_1_, ...), custom_call_target="tpu_custom_call" | custom-call | bytes 5242880 | tf_op jit(solution)/shard_map/place/pallas_call | solution.py:351
  160.2 12.0 %collective-permute-done.6.refs_1_ = bf16[256,1280]{1,0:T(8,128)(2,1)} collective-permute-done((bf16[256,1280]{1,0:T(8,128)(2,1)}, bf16[256,1280]{1,0:T(8,128)(2,1)}, u32[]{:S(2)}, u32[]{:S(2)}) %collective-permute-start.6) | collective-permute-done | bytes 655392 | tf_op jit(solution)/shard_map/ppermute | solution.py:504
  172.2 13.0 %collective-permute-done.7.refs_2_ = bf16[256,1280]{1,0:T(8,128)(2,1)} collective-permute-done((bf16[256,1280]{1,0:T(8,128)(2,1)}, bf16[256,1280]{1,0:T(8,128)(2,1)}, u32[]{:S(2)}, u32[]{:S(2)}) %collective-permute-start.7) | collective-permute-done | bytes 655392 | tf_op jit(solution)/shard_map/ppermute | solution.py:504
  185.2 2.5 %place.3 = (bf16[256,4096]{1,0:T(8,128)(2,1)}, bf16[256,4096]{1,0:T(8,128)(2,1)}, bf16[256,1024]{1,0:T(8,128)(2,1)}, bf16[256,1024]{1,0:T(8,128)(2,1)}) custom-call(s32[1]{0:T(128)} %bitcast.y_ref, bf16[256,1280]{1,0:T(8,128)(2,1)} %collective-permute-done.5.refs_0_, ...), custom_call_target="tpu_custom_call", output_to_operand_aliasing={{0}: (4, {}), {1}: (5, {}), {2}: (6, {}), {3}: (7, {})} | custom-call | bytes 5242880 | tf_op jit(solution)/shard_map/place/pallas_call | solution.py:351
  187.7 2.0 %total.2 = (bf16[128,256]{1,0:T(8,128)(2,1)}, bf16[128,256]{1,0:T(8,128)(2,1)}) custom-call(bf16[16,128,256]{2,1,0:T(8,128)(2,1)} %all-to-all-done.2.parts_ref), custom_call_target="tpu_custom_call" | custom-call | bytes 1048576 | tf_op jit(solution)/shard_map/total/pallas_call | solution.py:471
  (36 shorter events, 11.2 us)
Async XLA Ops:
  3.0 8.7 %copy-start = (s32[1,4]{1,0:T(1,128)S(1)}, s32[1,4]{1,0:T(1,128)}, u32[]{:S(2)}) copy-start(s32[1,4]{1,0:T(1,128)} %param.14) | copy-start | bytes 52
  3.0 39.9 %all-to-all-start = ((bf16[16,128,512]{2,1,0:T(8,128)(2,1)}), bf16[16,128,512]{2,1,0:T(8,128)(2,1)}, u32[]{:S(2)}, u32[]{:S(2)}) async-start(bf16[16,128,512]{2,1,0:T(8,128)(2,1)} %spread.1), calls=%async_computation | async-start | bytes 4194304 | tf_op jit(solution)/shard_map/all_to_all | solution.py:508
  11.8 7.2 %collective-permute-start = (s32[5]{0:T(128)S(1)}, s32[5]{0:T(128)S(1)}, u32[]{:S(2)}, u32[]{:S(2)}) collective-permute-start(s32[5]{0:T(128)S(1)} %pad_add_fusion), channel_id=1, source_target_pairs={{0,4},{4,0},{1,5},{5,1},{2,6},{6,2},{3,7},{7,3},{8,12},{12,8},{9,1... | collective-permute-start | bytes 68 | tf_op jit(solution)/shard_map/ppermute | solution.py:512
  14.3 36.8 %collective-permute-start.8 = (bf16[256,1280]{1,0:T(8,128)(2,1)}, bf16[256,1280]{1,0:T(8,128)(2,1)}, u32[]{:S(2)}, u32[]{:S(2)}) collective-permute-start(bf16[256,1280]{1,0:T(8,128)(2,1)} %get-tuple-element.44), channel_id=1, source_target_pairs={{0,3},{1,0},{2,1},{3,2},{4,7},{5,4},{6,5},{7,6},{8,11},{9,8},{10,9... | collective-permute-start | bytes 1966088 | tf_op jit(solution)/shard_map/ppermute | solution.py:504
  17.4 34.4 %collective-permute-start.9 = (bf16[256,1280]{1,0:T(8,128)(2,1)}, bf16[256,1280]{1,0:T(8,128)(2,1)}, u32[]{:S(2)}, u32[]{:S(2)}) collective-permute-start(bf16[256,1280]{1,0:T(8,128)(2,1)} %get-tuple-element.45), channel_id=1, source_target_pairs={{0,2},{1,3},{2,0},{3,1},{4,6},{5,7},{6,4},{7,5},{8,10},{9,11},{10,... | collective-permute-start | bytes 1966088 | tf_op jit(solution)/shard_map/ppermute | solution.py:504
  18.0 34.7 %collective-permute-start.10 = (bf16[256,1280]{1,0:T(8,128)(2,1)}, bf16[256,1280]{1,0:T(8,128)(2,1)}, u32[]{:S(2)}, u32[]{:S(2)}) collective-permute-start(bf16[256,1280]{1,0:T(8,128)(2,1)} %get-tuple-element.46), channel_id=1, source_target_pairs={{0,1},{1,2},{2,3},{3,0},{4,5},{5,6},{6,7},{7,4},{8,9},{9,10},{10,1... | collective-permute-start | bytes 1966088 | tf_op jit(solution)/shard_map/ppermute | solution.py:504
  45.5 7.2 %collective-permute-start.4 = (bf16[4,128,512]{2,1,0:T(8,128)(2,1)}, bf16[4,128,512]{2,1,0:T(8,128)(2,1)}, u32[]{:S(2)}, u32[]{:S(2)}) collective-permute-start(bf16[4,128,512]{2,1,0:T(8,128)(2,1)} %pick.1), channel_id=1, source_target_pairs={{0,4},{4,0},{1,5},{5,1},{2,6},{6,2},{3,7},{7,3},{8,12},{12,8},{9,1... | collective-permute-start | bytes 1572872 | tf_op jit(solution)/shard_map/ppermute | solution.py:512
  48.0 39.8 %collective-permute-start.1 = (bf16[256,1280]{1,0:T(8,128)(2,1)}, bf16[256,1280]{1,0:T(8,128)(2,1)}, u32[]{:S(2)}, u32[]{:S(2)}) collective-permute-start(bf16[256,1280]{1,0:T(8,128)(2,1)} %get-tuple-element.37), channel_id=1, source_target_pairs={{0,3},{1,0},{2,1},{3,2},{4,7},{5,4},{6,5},{7,6},{8,11},{9,8},{10,9... | collective-permute-start | bytes 1966088 | tf_op jit(solution)/shard_map/ppermute | solution.py:504
  51.1 36.7 %collective-permute-start.2 = (bf16[256,1280]{1,0:T(8,128)(2,1)}, bf16[256,1280]{1,0:T(8,128)(2,1)}, u32[]{:S(2)}, u32[]{:S(2)}) collective-permute-start(bf16[256,1280]{1,0:T(8,128)(2,1)} %get-tuple-element.38), channel_id=1, source_target_pairs={{0,2},{1,3},{2,0},{3,1},{4,6},{5,7},{6,4},{7,5},{8,10},{9,11},{10,... | collective-permute-start | bytes 1966088 | tf_op jit(solution)/shard_map/ppermute | solution.py:504
  51.7 36.1 %collective-permute-start.3 = (bf16[256,1280]{1,0:T(8,128)(2,1)}, bf16[256,1280]{1,0:T(8,128)(2,1)}, u32[]{:S(2)}, u32[]{:S(2)}) collective-permute-start(bf16[256,1280]{1,0:T(8,128)(2,1)} %get-tuple-element.39), channel_id=1, source_target_pairs={{0,1},{1,2},{2,3},{3,0},{4,5},{5,6},{6,7},{7,4},{8,9},{9,10},{10,1... | collective-permute-start | bytes 1966088 | tf_op jit(solution)/shard_map/ppermute | solution.py:504
  77.6 2.4 %collective-permute-start.15 = (bf16[4,128,256]{2,1,0:T(8,128)(2,1)}, bf16[4,128,256]{2,1,0:T(8,128)(2,1)}, u32[]{:S(2)}, u32[]{:S(2)}) collective-permute-start(bf16[4,128,256]{2,1,0:T(8,128)(2,1)} %get-tuple-element.61.own_ref), channel_id=1, source_target_pairs={{0,4},{4,0},{1,5},{5,1},{2,6},{6,2},{3,7},{7,3},{8,12},{12,8},{9,1... | collective-permute-start | bytes 786440 | tf_op jit(solution)/shard_map/ppermute | solution.py:512
  77.7 51.5 %collective-permute-start.11 = (bf16[256,1280]{1,0:T(8,128)(2,1)}, bf16[256,1280]{1,0:T(8,128)(2,1)}, u32[]{:S(2)}, u32[]{:S(2)}) collective-permute-start(bf16[256,1280]{1,0:T(8,128)(2,1)} %get-tuple-element.48), channel_id=1, source_target_pairs={{0,3},{1,0},{2,1},{3,2},{4,7},{5,4},{6,5},{7,6},{8,11},{9,8},{10,9... | collective-permute-start | bytes 1966088 | tf_op jit(solution)/shard_map/ppermute | solution.py:504
  82.8 34.7 %all-to-all-start.2 = ((bf16[16,128,256]{2,1,0:T(8,128)(2,1)}), bf16[16,128,256]{2,1,0:T(8,128)(2,1)}, u32[]{:S(2)}, u32[]{:S(2)}) async-start(bf16[16,128,256]{2,1,0:T(8,128)(2,1)} %scatter.3), calls=%async_computation.2 | async-start | bytes 2097152 | tf_op jit(solution)/shard_map/all_to_all | solution.py:508
  112.7 2.0 %collective-permute-start.14 = (bf16[4,128,256]{2,1,0:T(8,128)(2,1)}, bf16[4,128,256]{2,1,0:T(8,128)(2,1)}, u32[]{:S(2)}, u32[]{:S(2)}) collective-permute-start(bf16[4,128,256]{2,1,0:T(8,128)(2,1)} %get-tuple-element.60.own_ref), channel_id=1, source_target_pairs={{0,4},{4,0},{1,5},{5,1},{2,6},{6,2},{3,7},{7,3},{8,12},{12,8},{9,1... | collective-permute-start | bytes 786440 | tf_op jit(solution)/shard_map/ppermute | solution.py:512
  117.5 7.4 %copy-start.2 = (bf16[256,1280]{1,0:T(8,128)(2,1)S(1)}, bf16[256,1280]{1,0:T(8,128)(2,1)}, u32[]{:S(2)}) copy-start(bf16[256,1280]{1,0:T(8,128)(2,1)} %get-tuple-element.49) | copy-start | bytes 1966084
  117.5 8.4 %copy-start.1 = (bf16[256,1280]{1,0:T(8,128)(2,1)S(1)}, bf16[256,1280]{1,0:T(8,128)(2,1)}, u32[]{:S(2)}) copy-start(bf16[256,1280]{1,0:T(8,128)(2,1)} %get-tuple-element.50) | copy-start | bytes 1966084
  117.5 72.2 %all-to-all-start.1 = ((bf16[16,128,256]{2,1,0:T(8,128)(2,1)}), bf16[16,128,256]{2,1,0:T(8,128)(2,1)}, u32[]{:S(2)}, u32[]{:S(2)}) async-start(bf16[16,128,256]{2,1,0:T(8,128)(2,1)} %scatter.2), calls=%async_computation.1 | async-start | bytes 2097152 | tf_op jit(solution)/shard_map/all_to_all | solution.py:508
  124.9 19.3 %collective-permute-start.12 = (bf16[256,1280]{1,0:T(8,128)(2,1)S(1)}, bf16[256,1280]{1,0:T(8,128)(2,1)}, u32[]{:S(2)}, u32[]{:S(2)}) collective-permute-start(bf16[256,1280]{1,0:T(8,128)(2,1)S(1)} %copy-done.2), channel_id=1, source_target_pairs={{0,2},{1,3},{2,0},{3,1},{4,6},{5,7},{6,4},{7,5},{8,10},{9,11},{10,... | collective-permute-start | bytes 1966088 | tf_op jit(solution)/shard_map/ppermute | solution.py:504
  125.9 31.3 %collective-permute-start.13 = (bf16[256,1280]{1,0:T(8,128)(2,1)S(1)}, bf16[256,1280]{1,0:T(8,128)(2,1)}, u32[]{:S(2)}, u32[]{:S(2)}) collective-permute-start(bf16[256,1280]{1,0:T(8,128)(2,1)S(1)} %copy-done.1), channel_id=1, source_target_pairs={{0,1},{1,2},{2,3},{3,0},{4,5},{5,6},{6,7},{7,4},{8,9},{9,10},{10,1... | collective-permute-start | bytes 1966088 | tf_op jit(solution)/shard_map/ppermute | solution.py:504
  126.9 33.3 %collective-permute-start.5 = (bf16[256,1280]{1,0:T(8,128)(2,1)}, bf16[256,1280]{1,0:T(8,128)(2,1)}, u32[]{:S(2)}, u32[]{:S(2)}) collective-permute-start(bf16[256,1280]{1,0:T(8,128)(2,1)} %get-tuple-element.41), channel_id=1, source_target_pairs={{0,3},{1,0},{2,1},{3,2},{4,7},{5,4},{6,5},{7,6},{8,11},{9,8},{10,9... | collective-permute-start | bytes 1966088 | tf_op jit(solution)/shard_map/ppermute | solution.py:504
  129.2 43.1 %collective-permute-start.6 = (bf16[256,1280]{1,0:T(8,128)(2,1)}, bf16[256,1280]{1,0:T(8,128)(2,1)}, u32[]{:S(2)}, u32[]{:S(2)}) collective-permute-start(bf16[256,1280]{1,0:T(8,128)(2,1)} %get-tuple-element.42), channel_id=1, source_target_pairs={{0,1},{1,2},{2,3},{3,0},{4,5},{5,6},{6,7},{7,4},{8,9},{9,10},{10,1... | collective-permute-start | bytes 1966088 | tf_op jit(solution)/shard_map/ppermute | solution.py:504
  129.2 56.1 %collective-permute-start.7 = (bf16[256,1280]{1,0:T(8,128)(2,1)}, bf16[256,1280]{1,0:T(8,128)(2,1)}, u32[]{:S(2)}, u32[]{:S(2)}) collective-permute-start(bf16[256,1280]{1,0:T(8,128)(2,1)} %get-tuple-element.43), channel_id=1, source_target_pairs={{0,2},{1,3},{2,0},{3,1},{4,6},{5,7},{6,4},{7,5},{8,10},{9,11},{10,... | collective-permute-start | bytes 1966088 | tf_op jit(solution)/shard_map/ppermute | solution.py:504

commit v7 on v5

--- a/solution.py
+++ b/solution.py
@@ -133,10 +133,13 @@
 
 
 def attn_body(sc, *refs):
-    pieces = [refs[4 * d : 4 * d + 4] for d in range(TP)]
-    refs = refs[4 * TP :]
-    near, far = refs[: 2 * SLOTS], refs[2 * SLOTS : 4 * SLOTS]
-    refs = refs[4 * SLOTS :]
+    pieces = [refs[:2]] + [refs[4 + 3 * d : 6 + 3 * d] for d in range(TP - 1)]
+    pairs = [refs[6 + 3 * d] for d in range(TP - 1)]
+    token_keys = [refs[2]] + [p.at[:, :HD] for p in pairs]
+    token_vals = [refs[3]] + [p.at[:, HD:] for p in pairs]
+    refs = refs[4 + 3 * (TP - 1) :]
+    near, far = refs[:SLOTS], refs[SLOTS : 2 * SLOTS]
+    refs = refs[2 * SLOTS :]
     outs, beac_out = refs[:TP], refs[TP]
     qs, gs, os, dqs, keys, vals, keys_t, vals_t, bias, scores, probs, dscores, dk_acc, dv_acc = refs[TP + 1 :]
     head = pl.program_id(0)
@@ -144,13 +147,14 @@
 
     @pl.when(head == 0)
     def _():
-        for t, dst in ((0, keys), (1, vals)):
+        for t, dst, token in ((0, keys, token_keys), (1, vals, token_vals)):
+            cols = slice(t * HD, (t + 1) * HD)
             for j in range(SLOTS):
-                a, b = near[t * SLOTS + j][0], far[t * SLOTS + j][0]
+                a, b = near[j][0, :, cols], far[j][0, :, cols]
                 dst[pl.ds(j * BLOCK, BLOCK), :] = jnp.where(lax.rem(sc[S_OWN + j], 2) == sc[S_CORE], a, b)
             for d in range(TP):
                 at = pl.multiple_of(BEAC + lax.rem(me + d, TP) * CHUNK, CHUNK)
-                dst[pl.ds(at, CHUNK), :] = pieces[d][2 + t][...]
+                dst[pl.ds(at, CHUNK), :] = token[d][...]
         for j in range(SLOTS):
             row = jnp.where(j < sc[S_COUNT], 0.0, NEG)
             bias[pl.ds(j * BLOCK, BLOCK), :] = jnp.full((BLOCK, HD), row, F32)
@@ -205,21 +209,18 @@
         ops.append(own[2 + t])
         in_specs.append(spec((CHUNK, HD), lambda h, sc: (0, sc[S_Y] * kv_heads + sc[S_GROUP])))
     for piece in pieces:
-        ops += [piece] * 4
+        ops += [piece] * 3
         in_specs += [
             spec((CHUNK, STEP * HD), lambda h, sc: (0, h)),
             spec((CHUNK, STEP * HD), lambda h, sc: (0, GROUP // STEP + h)),
-            spec((CHUNK, HD), lambda h, sc: (0, 2 * GROUP)),
-            spec((CHUNK, HD), lambda h, sc: (0, 2 * GROUP + 1)),
+            spec((CHUNK, 2 * HD), lambda h, sc: (0, GROUP)),
         ]
-    for t in range(2):
-        for j in range(SLOTS):
-            ops.append(near)
-            in_specs.append(spec((1, BLOCK, HD), lambda h, sc, j=j, t=t: (sc[S_NEAR + j], 0, 2 * t + sc[S_GROUP])))
-    for t in range(2):
-        for j in range(SLOTS):
-            ops.append(far)
-            in_specs.append(spec((1, BLOCK, HD), lambda h, sc, j=j, t=t: (j, 0, 2 * t + sc[S_GROUP])))
+    for j in range(SLOTS):
+        ops.append(near)
+        in_specs.append(spec((1, BLOCK, 2 * HD), lambda h, sc, j=j: (sc[S_NEAR + j], 0, sc[S_GROUP])))
+    for j in range(SLOTS):
+        ops.append(far)
+        in_specs.append(spec((1, BLOCK, 2 * HD), lambda h, sc, j=j: (j, 0, sc[S_GROUP])))
     out_specs = [spec((CHUNK, PIECE), lambda h, sc: (0, 0)) for _ in range(TP)]
     out_specs.append(spec((SLOTS, BLOCK, 2 * HD), lambda h, sc: (0, 0, 0)))
     out_shape = [jax.ShapeDtypeStruct((CHUNK, PIECE), BF16) for _ in range(TP)]
@@ -354,6 +355,41 @@
     )(y, *pieces, *placed)
 
 
+def spread_body(k_ref, v_ref, out_ref, buf, in_sems, out_sems):
+    loads = []
+    for t, ref in enumerate((k_ref, v_ref)):
+        for g in range(2):
+            dst = buf.at[:, pl.ds((2 * g + t) * HD, HD)]
+            loads.append(pltpu.make_async_copy(ref.at[:, pl.ds(g * HD, HD)], dst, in_sems.at[2 * g + t]))
+    for copy in loads:
+        copy.start()
+    for copy in loads:
+        copy.wait()
+    stores = [pltpu.make_async_copy(buf, out_ref.at[n], out_sems.at[n]) for n in range(out_ref.shape[0])]
+    for copy in stores:
+        copy.start()
+    for copy in stores:
+        copy.wait()
+
+
+def spread(beacon_keys, beacon_values, chips):
+    anyspec = pl.BlockSpec(memory_space=pl.ANY)
+    return pl.pallas_call(
+        spread_body,
+        in_specs=[anyspec] * 2,
+        out_specs=anyspec,
+        out_shape=jax.ShapeDtypeStruct((chips, BLOCK, 4 * HD), BF16),
+        scratch_shapes=[
+            pltpu.VMEM((BLOCK, 4 * HD), BF16),
+            pltpu.SemaphoreType.DMA((4,)),
+            pltpu.SemaphoreType.DMA((chips,)),
+        ],
+        compiler_params=pltpu.CompilerParams(vmem_limit_bytes=VMEM),
+        cost_estimate=pl.CostEstimate(flops=0, bytes_accessed=2 << 20, transcendentals=0),
+        name="spread",
+    )(beacon_keys, beacon_values)
+
+
 def pick_body(tab_ref, *refs):
     for j in range(SLOTS):
         refs[SLOTS][j] = refs[j][0]
@@ -470,8 +506,7 @@
     core = lax.axis_index("core")
     chips = lax.axis_size("z") * lax.axis_size("x")
 
-    block = jnp.concatenate([beacon_keys, beacon_values], axis=1)
-    chip_blocks = jnp.broadcast_to(block[None], (chips,) + block.shape)
+    chip_blocks = spread(beacon_keys, beacon_values, chips)
     row, count = read_blocks[0], read_counts
     table = jnp.concatenate([row, count])
     peer_table = swap(table)
@@ -482,7 +517,7 @@
     for g in range(2):
         got = {}
         sent = split(g, place_at, own)
-        for d in (1, 3, 2):
+        for d in (2, 1, 3):
             got[TP - d] = shift(sent[d - 1], d)
         recv.append([got[1], got[2], got[3]])
 

time: 192 us -> 192 us (level)
  Pallas kernels: 73.3 us -> 75.6 us
    pallas_call x0 -> x1, Pallas kernels: none -> 2.28 us  [spread(): pl.pallas_call(spread_body, in_specs=[anyspec] * 2, out_specs=anyspec, ou...]
where the time goes in v7:
time: 192 us; the launch traced here: 191 us
  Pallas kernels  75.6 us (39%)
  waiting for transfers between devices  74.3 us (39%)
  starting transfers between devices  39.4 us (21%)
    ppermute x12, waiting for transfers between devices, shift(): return lax.ppermute(x, 'y', [(s, (s + step) % TP) for s in range(TP)])  50.3 us
    pallas_call x2, Pallas kernels, attn(): pl.pallas_call(attn_body, grid_spec=pltpu.PrefetchScalarGridSpec(num_scal...  49.5 us
    all_to_all x3, waiting for transfers between devices, to_chips(): return lax.all_to_all(x, ('z', 'x'), 0, 0, tiled=True)  22.1 us
    all_to_all x3, starting transfers between devices, to_chips(): return lax.all_to_all(x, ('z', 'x'), 0, 0, tiled=True)  20.4 us
    ppermute x12, starting transfers between devices, shift(): return lax.ppermute(x, 'y', [(s, (s + step) % TP) for s in range(TP)])  18.8 us
    pallas_call x2, Pallas kernels, scatter(): pl.pallas_call(scatter_body, grid_spec=pltpu.PrefetchScalarGridSpec(num_s...  5.65 us
    pallas_call x2, Pallas kernels, place(): pl.pallas_call(functools.partial(place_body, entries, len(placed)), grid_...  5.45 us
    pallas_call x2, Pallas kernels, split(): pl.pallas_call(functools.partial(split_body, group), grid_spec=pltpu.Pref...  4.96 us
  transfers between devices with their start and end apart: 19, of which 6 were waited for; matrix products, arithmetic and copies ran while one was open for 0% of the time, Pallas kernels for 37%

profile of v7, /device:TPU:0, one launch (start us, length us, event | category | flops | bytes accessed | tf_op | source)
XLA Modules:
  0.0 191.4 jit_solution(17622636738624972772)
XLA Ops:
  0.6 2.3 %spread.1 = bf16[16,128,512]{2,1,0:T(8,128)(2,1)} custom-call(bf16[128,256]{1,0:T(8,128)(2,1)} %k_ref.1, bf16[128,256]{1,0:T(8,128)(2,1)} %v_ref.1), custom_call_target="tpu_custom_call" | custom-call | bytes 2097152 | tf_op jit(solution)/shard_map/spread/pallas_call | solution.py:377
  2.9 8.1 %all-to-all-start = ((bf16[16,128,512]{2,1,0:T(8,128)(2,1)}), bf16[16,128,512]{2,1,0:T(8,128)(2,1)}, u32[]{:S(2)}, u32[]{:S(2)}) async-start(bf16[16,128,512]{2,1,0:T(8,128)(2,1)} %spread.1), calls=%async_computation | async-start | bytes 4194304 | tf_op jit(solution)/shard_map/all_to_all | solution.py:497
  11.8 2.5 %split.3 = (bf16[256,1280]{1,0:T(8,128)(2,1)}, bf16[256,1280]{1,0:T(8,128)(2,1)}, bf16[256,1280]{1,0:T(8,128)(2,1)}) custom-call(s32[1]{0:T(128)} %bitcast.y_ref, bf16[256,4096]{1,0:T(8,128)(2,1)} %refs_0_.7, bf16[256,4096]{1,0:T(8,128)(2,1)} %refs_1_.7, bf16[256,1024]{1,0:T(8,128)(2,1)} %refs_2_.7, bf16[256,1024]{1,0:T(8,128)(2,1)} %refs_3_.7), custom_call_target="tpu_custom_call" | custom-call | bytes 4194304 | tf_op jit(solution)/shard_map/split/pallas_call | solution.py:290
  14.2 3.1 %collective-permute-start.8 = (bf16[256,1280]{1,0:T(8,128)(2,1)}, bf16[256,1280]{1,0:T(8,128)(2,1)}, u32[]{:S(2)}, u32[]{:S(2)}) collective-permute-start(bf16[256,1280]{1,0:T(8,128)(2,1)} %get-tuple-element.44), channel_id=1, source_target_pairs={{0,3},{1,0},{2,1},{3,2},{4,7},{5,4},{6,5},{7,6},{8,11},{9,8},{10,9... | collective-permute-start | bytes 1966088 | tf_op jit(solution)/shard_map/ppermute | solution.py:493
  20.7 22.1 %all-to-all-done.refs_0_.refs_1_.refs_2_.refs_3_.refs_13_.refs_14_.refs_15_.refs_16_ = bf16[16,128,512]{2,1,0:T(8,128)(2,1)} async-done(((bf16[16,128,512]{2,1,0:T(8,128)(2,1)}), bf16[16,128,512]{2,1,0:T(8,128)(2,1)}, u32[]{:S(2)}, u32[]{:S(2)}) %all-to-all-start) | async-done | bytes 2097184 | tf_op jit(solution)/shard_map/all_to_all | solution.py:497
  42.8 2.6 %pick.1 = bf16[4,128,512]{2,1,0:T(8,128)(2,1)} custom-call(s32[18]{0:T(128)} %get-tuple-element.40.tab_ref.sc, bf16[16,128,512]{2,1,0:T(8,128)(2,1)} %all-to-all-done.refs_0_.refs_1_.refs_2_.refs_3_.refs_13_.refs_14_.refs_15_.refs_16_, bf16[16,128,512]{2,1,0:T(8,128)(2,1)} %all-to-all-done.refs_0_.refs_1_.refs_2_.refs_3_.refs_13_.refs_14_.refs_15_.refs_16_, ...), custom_call_target="tpu_custom_call" | custom-call | bytes 1048576 | tf_op jit(solution)/shard_map/pick/pallas_call | solution.py:405
  45.4 2.5 %split.2 = (bf16[256,1280]{1,0:T(8,128)(2,1)}, bf16[256,1280]{1,0:T(8,128)(2,1)}, bf16[256,1280]{1,0:T(8,128)(2,1)}) custom-call(s32[1]{0:T(128)} %bitcast.y_ref, bf16[256,4096]{1,0:T(8,128)(2,1)} %refs_0_.7, bf16[256,4096]{1,0:T(8,128)(2,1)} %refs_1_.7, bf16[256,1024]{1,0:T(8,128)(2,1)} %refs_2_.7, bf16[256,1024]{1,0:T(8,128)(2,1)} %refs_3_.7), custom_call_target="tpu_custom_call" | custom-call | bytes 4194304 | tf_op jit(solution)/shard_map/split/pallas_call | solution.py:290
  48.0 3.1 %collective-permute-start.1 = (bf16[256,1280]{1,0:T(8,128)(2,1)}, bf16[256,1280]{1,0:T(8,128)(2,1)}, u32[]{:S(2)}, u32[]{:S(2)}) collective-permute-start(bf16[256,1280]{1,0:T(8,128)(2,1)} %get-tuple-element.37), channel_id=1, source_target_pairs={{0,3},{1,0},{2,1},{3,2},{4,7},{5,4},{6,5},{7,6},{8,11},{9,8},{10,9... | collective-permute-start | bytes 1966088 | tf_op jit(solution)/shard_map/ppermute | solution.py:493
  52.7 24.7 %attn.3 = (bf16[256,1280]{1,0:T(8,128)(2,1)}, bf16[256,1280]{1,0:T(8,128)(2,1)}, bf16[256,1280]{1,0:T(8,128)(2,1)}, bf16[256,1280]{1,0:T(8,128)(2,1)}, bf16[4,128,256]{2,1,0:T(8,128)(2,1)}) custom-call(s32[18]{0:T(128)} %get-tuple-element.40.tab_ref.sc, bf16[256,4096]{1,0:T(8,128)(2,1)} %refs_0_.7, bf16[256,4096]{1,0:T(8,128)(2,1)} %refs_1_.7, ...), custom_call_target="tpu_custom_call" | custom-call | flops 14495514624 | bytes 6291456 | tf_op jit(solution)/shard_map/attn/pallas_call | solution.py:229
  77.5 2.4 %collective-permute-start.11 = (bf16[256,1280]{1,0:T(8,128)(2,1)}, bf16[256,1280]{1,0:T(8,128)(2,1)}, u32[]{:S(2)}, u32[]{:S(2)}) collective-permute-start(bf16[256,1280]{1,0:T(8,128)(2,1)} %get-tuple-element.48), channel_id=1, source_target_pairs={{0,3},{1,0},{2,1},{3,2},{4,7},{5,4},{6,5},{7,6},{8,11},{9,8},{10,9... | collective-permute-start | bytes 1966088 | tf_op jit(solution)/shard_map/ppermute | solution.py:493
  79.9 2.8 %scatter.3 = bf16[16,128,256]{2,1,0:T(8,128)(2,1)} custom-call(s32[18]{0:T(128)} %get-tuple-element.40.tab_ref.sc, bf16[4,128,256]{2,1,0:T(8,128)(2,1)} %get-tuple-element.61.own_ref, bf16[4,128,256]{2,1,0:T(8,128)(2,1)} %collective-permute-done.15.peer_ref), custom_call_target="tpu_custom_call" | custom-call | bytes 2097152 | tf_op jit(solution)/shard_map/scatter/pallas_call | solution.py:434
  82.7 4.9 %all-to-all-start.2 = ((bf16[16,128,256]{2,1,0:T(8,128)(2,1)}), bf16[16,128,256]{2,1,0:T(8,128)(2,1)}, u32[]{:S(2)}, u32[]{:S(2)}) async-start(bf16[16,128,256]{2,1,0:T(8,128)(2,1)} %scatter.3), calls=%async_computation.2 | async-start | bytes 2097152 | tf_op jit(solution)/shard_map/all_to_all | solution.py:497
  87.7 24.8 %attn.2 = (bf16[256,1280]{1,0:T(8,128)(2,1)}, bf16[256,1280]{1,0:T(8,128)(2,1)}, bf16[256,1280]{1,0:T(8,128)(2,1)}, bf16[256,1280]{1,0:T(8,128)(2,1)}, bf16[4,128,256]{2,1,0:T(8,128)(2,1)}) custom-call(s32[18]{0:T(128)} %get-tuple-element.36.sc.tab_ref, bf16[256,4096]{1,0:T(8,128)(2,1)} %refs_0_.7, bf16[256,4096]{1,0:T(8,128)(2,1)} %refs_1_.7, ...), custom_call_target="tpu_custom_call" | custom-call | flops 14495514624 | bytes 6291456 | tf_op jit(solution)/shard_map/attn/pallas_call | solution.py:229
  114.4 2.8 %scatter.2 = bf16[16,128,256]{2,1,0:T(8,128)(2,1)} custom-call(s32[18]{0:T(128)} %get-tuple-element.36.sc.tab_ref, bf16[4,128,256]{2,1,0:T(8,128)(2,1)} %get-tuple-element.60.own_ref, bf16[4,128,256]{2,1,0:T(8,128)(2,1)} %collective-permute-done.14.peer_ref), custom_call_target="tpu_custom_call" | custom-call | bytes 2097152 | tf_op jit(solution)/shard_map/scatter/pallas_call | solution.py:434
  117.3 7.4 %all-to-all-start.1 = ((bf16[16,128,256]{2,1,0:T(8,128)(2,1)}), bf16[16,128,256]{2,1,0:T(8,128)(2,1)}, u32[]{:S(2)}, u32[]{:S(2)}) async-start(bf16[16,128,256]{2,1,0:T(8,128)(2,1)} %scatter.2), calls=%async_computation.1 | async-start | bytes 2097152 | tf_op jit(solution)/shard_map/all_to_all | solution.py:497
  126.8 2.2 %collective-permute-start.5 = (bf16[256,1280]{1,0:T(8,128)(2,1)}, bf16[256,1280]{1,0:T(8,128)(2,1)}, u32[]{:S(2)}, u32[]{:S(2)}) collective-permute-start(bf16[256,1280]{1,0:T(8,128)(2,1)} %get-tuple-element.41), channel_id=1, source_target_pairs={{0,3},{1,0},{2,1},{3,2},{4,7},{5,4},{6,5},{7,6},{8,11},{9,8},{10,9... | collective-permute-start | bytes 1966088 | tf_op jit(solution)/shard_map/ppermute | solution.py:493
  129.0 2.7 %collective-permute-start.7 = (bf16[256,1280]{1,0:T(8,128)(2,1)}, bf16[256,1280]{1,0:T(8,128)(2,1)}, u32[]{:S(2)}, u32[]{:S(2)}) collective-permute-start(bf16[256,1280]{1,0:T(8,128)(2,1)} %get-tuple-element.43), channel_id=1, source_target_pairs={{0,2},{1,3},{2,0},{3,1},{4,6},{5,7},{6,4},{7,5},{8,10},{9,11},{10,... | collective-permute-start | bytes 1966088 | tf_op jit(solution)/shard_map/ppermute | solution.py:493
  131.7 12.3 %collective-permute-done.12.refs_2_ = bf16[256,1280]{1,0:T(8,128)(2,1)} collective-permute-done((bf16[256,1280]{1,0:T(8,128)(2,1)S(1)}, bf16[256,1280]{1,0:T(8,128)(2,1)}, u32[]{:S(2)}, u32[]{:S(2)}) %collective-permute-start.12) | collective-permute-done | bytes 655392 | tf_op jit(solution)/shard_map/ppermute | solution.py:493
  144.0 13.0 %collective-permute-done.13.refs_3_ = bf16[256,1280]{1,0:T(8,128)(2,1)} collective-permute-done((bf16[256,1280]{1,0:T(8,128)(2,1)S(1)}, bf16[256,1280]{1,0:T(8,128)(2,1)}, u32[]{:S(2)}, u32[]{:S(2)}) %collective-permute-start.13) | collective-permute-done | bytes 655392 | tf_op jit(solution)/shard_map/ppermute | solution.py:493
  157.0 3.0 %place.2 = (bf16[256,4096]{1,0:T(8,128)(2,1)}, bf16[256,4096]{1,0:T(8,128)(2,1)}, bf16[256,1024]{1,0:T(8,128)(2,1)}, bf16[256,1024]{1,0:T(8,128)(2,1)}) custom-call(s32[1]{0:T(128)} %bitcast.y_ref, bf16[256,1280]{1,0:T(8,128)(2,1)} %get-tuple-element.47.refs_0_, bf16[256,1280]{1,0:T(8,128)(2,1)} %collective-permute-done.11.refs_1_, ...), custom_call_target="tpu_custom_call" | custom-call | bytes 5242880 | tf_op jit(solution)/shard_map/place/pallas_call | solution.py:337
  160.0 12.0 %collective-permute-done.6.refs_1_ = bf16[256,1280]{1,0:T(8,128)(2,1)} collective-permute-done((bf16[256,1280]{1,0:T(8,128)(2,1)}, bf16[256,1280]{1,0:T(8,128)(2,1)}, u32[]{:S(2)}, u32[]{:S(2)}) %collective-permute-start.6) | collective-permute-done | bytes 655392 | tf_op jit(solution)/shard_map/ppermute | solution.py:493
  172.0 13.0 %collective-permute-done.7.refs_2_ = bf16[256,1280]{1,0:T(8,128)(2,1)} collective-permute-done((bf16[256,1280]{1,0:T(8,128)(2,1)}, bf16[256,1280]{1,0:T(8,128)(2,1)}, u32[]{:S(2)}, u32[]{:S(2)}) %collective-permute-start.7) | collective-permute-done | bytes 655392 | tf_op jit(solution)/shard_map/ppermute | solution.py:493
  185.0 2.5 %place.3 = (bf16[256,4096]{1,0:T(8,128)(2,1)}, bf16[256,4096]{1,0:T(8,128)(2,1)}, bf16[256,1024]{1,0:T(8,128)(2,1)}, bf16[256,1024]{1,0:T(8,128)(2,1)}) custom-call(s32[1]{0:T(128)} %bitcast.y_ref, bf16[256,1280]{1,0:T(8,128)(2,1)} %collective-permute-done.5.refs_0_, ...), custom_call_target="tpu_custom_call", output_to_operand_aliasing={{0}: (4, {}), {1}: (5, {}), {2}: (6, {}), {3}: (7, {})} | custom-call | bytes 5242880 | tf_op jit(solution)/shard_map/place/pallas_call | solution.py:337
  187.5 2.0 %total.2 = (bf16[128,256]{1,0:T(8,128)(2,1)}, bf16[128,256]{1,0:T(8,128)(2,1)}) custom-call(bf16[16,128,256]{2,1,0:T(8,128)(2,1)} %all-to-all-done.2.parts_ref), custom_call_target="tpu_custom_call" | custom-call | bytes 1048576 | tf_op jit(solution)/shard_map/total/pallas_call | solution.py:460
  (36 shorter events, 11.3 us)
Async XLA Ops:
  2.9 8.7 %copy-start = (s32[1,4]{1,0:T(1,128)S(1)}, s32[1,4]{1,0:T(1,128)}, u32[]{:S(2)}) copy-start(s32[1,4]{1,0:T(1,128)} %param.14) | copy-start | bytes 52
  2.9 39.9 %all-to-all-start = ((bf16[16,128,512]{2,1,0:T(8,128)(2,1)}), bf16[16,128,512]{2,1,0:T(8,128)(2,1)}, u32[]{:S(2)}, u32[]{:S(2)}) async-start(bf16[16,128,512]{2,1,0:T(8,128)(2,1)} %spread.1), calls=%async_computation | async-start | bytes 4194304 | tf_op jit(solution)/shard_map/all_to_all | solution.py:497
  11.7 7.2 %collective-permute-start = (s32[5]{0:T(128)S(1)}, s32[5]{0:T(128)S(1)}, u32[]{:S(2)}, u32[]{:S(2)}) collective-permute-start(s32[5]{0:T(128)S(1)} %pad_add_fusion), channel_id=1, source_target_pairs={{0,4},{4,0},{1,5},{5,1},{2,6},{6,2},{3,7},{7,3},{8,12},{12,8},{9,1... | collective-permute-start | bytes 68 | tf_op jit(solution)/shard_map/ppermute | solution.py:501
  14.2 36.8 %collective-permute-start.8 = (bf16[256,1280]{1,0:T(8,128)(2,1)}, bf16[256,1280]{1,0:T(8,128)(2,1)}, u32[]{:S(2)}, u32[]{:S(2)}) collective-permute-start(bf16[256,1280]{1,0:T(8,128)(2,1)} %get-tuple-element.44), channel_id=1, source_target_pairs={{0,3},{1,0},{2,1},{3,2},{4,7},{5,4},{6,5},{7,6},{8,11},{9,8},{10,9... | collective-permute-start | bytes 1966088 | tf_op jit(solution)/shard_map/ppermute | solution.py:493
  17.3 34.4 %collective-permute-start.9 = (bf16[256,1280]{1,0:T(8,128)(2,1)}, bf16[256,1280]{1,0:T(8,128)(2,1)}, u32[]{:S(2)}, u32[]{:S(2)}) collective-permute-start(bf16[256,1280]{1,0:T(8,128)(2,1)} %get-tuple-element.45), channel_id=1, source_target_pairs={{0,2},{1,3},{2,0},{3,1},{4,6},{5,7},{6,4},{7,5},{8,10},{9,11},{10,... | collective-permute-start | bytes 1966088 | tf_op jit(solution)/shard_map/ppermute | solution.py:493
  17.9 34.7 %collective-permute-start.10 = (bf16[256,1280]{1,0:T(8,128)(2,1)}, bf16[256,1280]{1,0:T(8,128)(2,1)}, u32[]{:S(2)}, u32[]{:S(2)}) collective-permute-start(bf16[256,1280]{1,0:T(8,128)(2,1)} %get-tuple-element.46), channel_id=1, source_target_pairs={{0,1},{1,2},{2,3},{3,0},{4,5},{5,6},{6,7},{7,4},{8,9},{9,10},{10,1... | collective-permute-start | bytes 1966088 | tf_op jit(solution)/shard_map/ppermute | solution.py:493
  45.4 7.2 %collective-permute-start.4 = (bf16[4,128,512]{2,1,0:T(8,128)(2,1)}, bf16[4,128,512]{2,1,0:T(8,128)(2,1)}, u32[]{:S(2)}, u32[]{:S(2)}) collective-permute-start(bf16[4,128,512]{2,1,0:T(8,128)(2,1)} %pick.1), channel_id=1, source_target_pairs={{0,4},{4,0},{1,5},{5,1},{2,6},{6,2},{3,7},{7,3},{8,12},{12,8},{9,1... | collective-permute-start | bytes 1572872 | tf_op jit(solution)/shard_map/ppermute | solution.py:501
  48.0 39.7 %collective-permute-start.1 = (bf16[256,1280]{1,0:T(8,128)(2,1)}, bf16[256,1280]{1,0:T(8,128)(2,1)}, u32[]{:S(2)}, u32[]{:S(2)}) collective-permute-start(bf16[256,1280]{1,0:T(8,128)(2,1)} %get-tuple-element.37), channel_id=1, source_target_pairs={{0,3},{1,0},{2,1},{3,2},{4,7},{5,4},{6,5},{7,6},{8,11},{9,8},{10,9... | collective-permute-start | bytes 1966088 | tf_op jit(solution)/shard_map/ppermute | solution.py:493
  51.0 36.6 %collective-permute-start.2 = (bf16[256,1280]{1,0:T(8,128)(2,1)}, bf16[256,1280]{1,0:T(8,128)(2,1)}, u32[]{:S(2)}, u32[]{:S(2)}) collective-permute-start(bf16[256,1280]{1,0:T(8,128)(2,1)} %get-tuple-element.38), channel_id=1, source_target_pairs={{0,2},{1,3},{2,0},{3,1},{4,6},{5,7},{6,4},{7,5},{8,10},{9,11},{10,... | collective-permute-start | bytes 1966088 | tf_op jit(solution)/shard_map/ppermute | solution.py:493
  51.7 36.0 %collective-permute-start.3 = (bf16[256,1280]{1,0:T(8,128)(2,1)}, bf16[256,1280]{1,0:T(8,128)(2,1)}, u32[]{:S(2)}, u32[]{:S(2)}) collective-permute-start(bf16[256,1280]{1,0:T(8,128)(2,1)} %get-tuple-element.39), channel_id=1, source_target_pairs={{0,1},{1,2},{2,3},{3,0},{4,5},{5,6},{6,7},{7,4},{8,9},{9,10},{10,1... | collective-permute-start | bytes 1966088 | tf_op jit(solution)/shard_map/ppermute | solution.py:493
  77.4 2.5 %collective-permute-start.15 = (bf16[4,128,256]{2,1,0:T(8,128)(2,1)}, bf16[4,128,256]{2,1,0:T(8,128)(2,1)}, u32[]{:S(2)}, u32[]{:S(2)}) collective-permute-start(bf16[4,128,256]{2,1,0:T(8,128)(2,1)} %get-tuple-element.61.own_ref), channel_id=1, source_target_pairs={{0,4},{4,0},{1,5},{5,1},{2,6},{6,2},{3,7},{7,3},{8,12},{12,8},{9,1... | collective-permute-start | bytes 786440 | tf_op jit(solution)/shard_map/ppermute | solution.py:501
  77.5 51.5 %collective-permute-start.11 = (bf16[256,1280]{1,0:T(8,128)(2,1)}, bf16[256,1280]{1,0:T(8,128)(2,1)}, u32[]{:S(2)}, u32[]{:S(2)}) collective-permute-start(bf16[256,1280]{1,0:T(8,128)(2,1)} %get-tuple-element.48), channel_id=1, source_target_pairs={{0,3},{1,0},{2,1},{3,2},{4,7},{5,4},{6,5},{7,6},{8,11},{9,8},{10,9... | collective-permute-start | bytes 1966088 | tf_op jit(solution)/shard_map/ppermute | solution.py:493
  82.7 34.5 %all-to-all-start.2 = ((bf16[16,128,256]{2,1,0:T(8,128)(2,1)}), bf16[16,128,256]{2,1,0:T(8,128)(2,1)}, u32[]{:S(2)}, u32[]{:S(2)}) async-start(bf16[16,128,256]{2,1,0:T(8,128)(2,1)} %scatter.3), calls=%async_computation.2 | async-start | bytes 2097152 | tf_op jit(solution)/shard_map/all_to_all | solution.py:497
  112.5 2.0 %collective-permute-start.14 = (bf16[4,128,256]{2,1,0:T(8,128)(2,1)}, bf16[4,128,256]{2,1,0:T(8,128)(2,1)}, u32[]{:S(2)}, u32[]{:S(2)}) collective-permute-start(bf16[4,128,256]{2,1,0:T(8,128)(2,1)} %get-tuple-element.60.own_ref), channel_id=1, source_target_pairs={{0,4},{4,0},{1,5},{5,1},{2,6},{6,2},{3,7},{7,3},{8,12},{12,8},{9,1... | collective-permute-start | bytes 786440 | tf_op jit(solution)/shard_map/ppermute | solution.py:501
  117.2 7.4 %copy-start.2 = (bf16[256,1280]{1,0:T(8,128)(2,1)S(1)}, bf16[256,1280]{1,0:T(8,128)(2,1)}, u32[]{:S(2)}) copy-start(bf16[256,1280]{1,0:T(8,128)(2,1)} %get-tuple-element.49) | copy-start | bytes 1966084
  117.2 8.5 %copy-start.1 = (bf16[256,1280]{1,0:T(8,128)(2,1)S(1)}, bf16[256,1280]{1,0:T(8,128)(2,1)}, u32[]{:S(2)}) copy-start(bf16[256,1280]{1,0:T(8,128)(2,1)} %get-tuple-element.50) | copy-start | bytes 1966084
  117.3 72.2 %all-to-all-start.1 = ((bf16[16,128,256]{2,1,0:T(8,128)(2,1)}), bf16[16,128,256]{2,1,0:T(8,128)(2,1)}, u32[]{:S(2)}, u32[]{:S(2)}) async-start(bf16[16,128,256]{2,1,0:T(8,128)(2,1)} %scatter.2), calls=%async_computation.1 | async-start | bytes 2097152 | tf_op jit(solution)/shard_map/all_to_all | solution.py:497
  124.6 19.3 %collective-permute-start.12 = (bf16[256,1280]{1,0:T(8,128)(2,1)S(1)}, bf16[256,1280]{1,0:T(8,128)(2,1)}, u32[]{:S(2)}, u32[]{:S(2)}) collective-permute-start(bf16[256,1280]{1,0:T(8,128)(2,1)S(1)} %copy-done.2), channel_id=1, source_target_pairs={{0,2},{1,3},{2,0},{3,1},{4,6},{5,7},{6,4},{7,5},{8,10},{9,11},{10,... | collective-permute-start | bytes 1966088 | tf_op jit(solution)/shard_map/ppermute | solution.py:493
  125.8 31.2 %collective-permute-start.13 = (bf16[256,1280]{1,0:T(8,128)(2,1)S(1)}, bf16[256,1280]{1,0:T(8,128)(2,1)}, u32[]{:S(2)}, u32[]{:S(2)}) collective-permute-start(bf16[256,1280]{1,0:T(8,128)(2,1)S(1)} %copy-done.1), channel_id=1, source_target_pairs={{0,1},{1,2},{2,3},{3,0},{4,5},{5,6},{6,7},{7,4},{8,9},{9,10},{10,1... | collective-permute-start | bytes 1966088 | tf_op jit(solution)/shard_map/ppermute | solution.py:493
  126.8 33.2 %collective-permute-start.5 = (bf16[256,1280]{1,0:T(8,128)(2,1)}, bf16[256,1280]{1,0:T(8,128)(2,1)}, u32[]{:S(2)}, u32[]{:S(2)}) collective-permute-start(bf16[256,1280]{1,0:T(8,128)(2,1)} %get-tuple-element.41), channel_id=1, source_target_pairs={{0,3},{1,0},{2,1},{3,2},{4,7},{5,4},{6,5},{7,6},{8,11},{9,8},{10,9... | collective-permute-start | bytes 1966088 | tf_op jit(solution)/shard_map/ppermute | solution.py:493
  129.0 43.0 %collective-permute-start.6 = (bf16[256,1280]{1,0:T(8,128)(2,1)}, bf16[256,1280]{1,0:T(8,128)(2,1)}, u32[]{:S(2)}, u32[]{:S(2)}) collective-permute-start(bf16[256,1280]{1,0:T(8,128)(2,1)} %get-tuple-element.42), channel_id=1, source_target_pairs={{0,1},{1,2},{2,3},{3,0},{4,5},{5,6},{6,7},{7,4},{8,9},{9,10},{10,1... | collective-permute-start | bytes 1966088 | tf_op jit(solution)/shard_map/ppermute | solution.py:493
  129.0 56.0 %collective-permute-start.7 = (bf16[256,1280]{1,0:T(8,128)(2,1)}, bf16[256,1280]{1,0:T(8,128)(2,1)}, u32[]{:S(2)}, u32[]{:S(2)}) collective-permute-start(bf16[256,1280]{1,0:T(8,128)(2,1)} %get-tuple-element.43), channel_id=1, source_target_pairs={{0,2},{1,3},{2,0},{3,1},{4,6},{5,7},{6,4},{7,5},{8,10},{9,11},{10,... | collective-permute-start | bytes 1966088 | tf_op jit(solution)/shard_map/ppermute | solution.py:493

commit v8 on v7

--- a/solution.py
+++ b/solution.py
@@ -417,9 +417,14 @@
     )(tables, *([gathered] * SLOTS))
 
 
-def scatter_body(tab_ref, own_ref, peer_ref, out_ref):
+def scatter_body(tab_ref, own_ref, peer_ref, out_ref, held, sems):
+    loads = [pltpu.make_async_copy(ref, held.at[t], sems.at[t]) for t, ref in enumerate((own_ref, peer_ref))]
+    for copy in loads:
+        copy.start()
     out_ref[...] = jnp.zeros_like(out_ref)
-    for terms, base in ((own_ref, S_OWN), (peer_ref, S_PEER)):
+    for copy in loads:
+        copy.wait()
+    for terms, base in ((held.at[0], S_OWN), (held.at[1], S_PEER)):
         for j in range(SLOTS):
             block = tab_ref[base + j]
 
@@ -430,7 +435,7 @@
 
 
 def scatter(tables, own, peer, chips):
-    whole = pl.BlockSpec((SLOTS, BLOCK, 2 * HD), lambda i, tab: (0, 0, 0))
+    whole = pl.BlockSpec(memory_space=pl.ANY)
     return pl.pallas_call(
         scatter_body,
         grid_spec=pltpu.PrefetchScalarGridSpec(
@@ -438,6 +443,7 @@
             grid=(1,),
             in_specs=[whole, whole],
             out_specs=pl.BlockSpec((chips, BLOCK, 2 * HD), lambda i, tab: (0, 0, 0)),
+            scratch_shapes=[pltpu.VMEM((2, SLOTS, BLOCK, 2 * HD), BF16), pltpu.SemaphoreType.DMA((2,))],
         ),
         out_shape=jax.ShapeDtypeStruct((chips, BLOCK, 2 * HD), BF16),
         compiler_params=pltpu.CompilerParams(vmem_limit_bytes=VMEM),

time: 192 us -> 192 us (level)
  no operation moved by 1% of the time
where the time goes in v8:
time: 192 us; the launch traced here: 191 us
  Pallas kernels  75.4 us (39%)
  waiting for transfers between devices  74.3 us (39%)
  starting transfers between devices  39.4 us (21%)
    ppermute x12, waiting for transfers between devices, shift(): return lax.ppermute(x, 'y', [(s, (s + step) % TP) for s in range(TP)])  50.3 us
    pallas_call x2, Pallas kernels, attn(): pl.pallas_call(attn_body, grid_spec=pltpu.PrefetchScalarGridSpec(num_scal...  49.5 us
    all_to_all x3, waiting for transfers between devices, to_chips(): return lax.all_to_all(x, ('z', 'x'), 0, 0, tiled=True)  22.1 us
    all_to_all x3, starting transfers between devices, to_chips(): return lax.all_to_all(x, ('z', 'x'), 0, 0, tiled=True)  20.4 us
    ppermute x12, starting transfers between devices, shift(): return lax.ppermute(x, 'y', [(s, (s + step) % TP) for s in range(TP)])  18.8 us
    pallas_call x2, Pallas kernels, place(): pl.pallas_call(functools.partial(place_body, entries, len(placed)), grid_...  5.45 us
    pallas_call x2, Pallas kernels, scatter(): pl.pallas_call(scatter_body, grid_spec=pltpu.PrefetchScalarGridSpec(num_s...  5.45 us
    pallas_call x2, Pallas kernels, split(): pl.pallas_call(functools.partial(split_body, group), grid_spec=pltpu.Pref...  4.96 us
  transfers between devices with their start and end apart: 19, of which 6 were waited for; matrix products, arithmetic and copies ran while one was open for 0% of the time, Pallas kernels for 37%

profile of v8, /device:TPU:0, one launch (start us, length us, event | category | flops | bytes accessed | tf_op | source)
XLA Modules:
  0.0 191.3 jit_solution(14628918565296938500)
XLA Ops:
  0.6 2.3 %spread.1 = bf16[16,128,512]{2,1,0:T(8,128)(2,1)} custom-call(bf16[128,256]{1,0:T(8,128)(2,1)} %k_ref.1, bf16[128,256]{1,0:T(8,128)(2,1)} %v_ref.1), custom_call_target="tpu_custom_call" | custom-call | bytes 2097152 | tf_op jit(solution)/shard_map/spread/pallas_call | solution.py:377
  2.9 8.1 %all-to-all-start = ((bf16[16,128,512]{2,1,0:T(8,128)(2,1)}), bf16[16,128,512]{2,1,0:T(8,128)(2,1)}, u32[]{:S(2)}, u32[]{:S(2)}) async-start(bf16[16,128,512]{2,1,0:T(8,128)(2,1)} %spread.1), calls=%async_computation | async-start | bytes 4194304 | tf_op jit(solution)/shard_map/all_to_all | solution.py:503
  11.8 2.5 %split.3 = (bf16[256,1280]{1,0:T(8,128)(2,1)}, bf16[256,1280]{1,0:T(8,128)(2,1)}, bf16[256,1280]{1,0:T(8,128)(2,1)}) custom-call(s32[1]{0:T(128)} %bitcast.y_ref, bf16[256,4096]{1,0:T(8,128)(2,1)} %refs_0_.7, bf16[256,4096]{1,0:T(8,128)(2,1)} %refs_1_.7, bf16[256,1024]{1,0:T(8,128)(2,1)} %refs_2_.7, bf16[256,1024]{1,0:T(8,128)(2,1)} %refs_3_.7), custom_call_target="tpu_custom_call" | custom-call | bytes 4194304 | tf_op jit(solution)/shard_map/split/pallas_call | solution.py:290
  14.2 3.1 %collective-permute-start.8 = (bf16[256,1280]{1,0:T(8,128)(2,1)}, bf16[256,1280]{1,0:T(8,128)(2,1)}, u32[]{:S(2)}, u32[]{:S(2)}) collective-permute-start(bf16[256,1280]{1,0:T(8,128)(2,1)} %get-tuple-element.44), channel_id=1, source_target_pairs={{0,3},{1,0},{2,1},{3,2},{4,7},{5,4},{6,5},{7,6},{8,11},{9,8},{10,9... | collective-permute-start | bytes 1966088 | tf_op jit(solution)/shard_map/ppermute | solution.py:499
  20.7 22.1 %all-to-all-done.refs_0_.refs_1_.refs_2_.refs_3_.refs_13_.refs_14_.refs_15_.refs_16_ = bf16[16,128,512]{2,1,0:T(8,128)(2,1)} async-done(((bf16[16,128,512]{2,1,0:T(8,128)(2,1)}), bf16[16,128,512]{2,1,0:T(8,128)(2,1)}, u32[]{:S(2)}, u32[]{:S(2)}) %all-to-all-start) | async-done | bytes 2097184 | tf_op jit(solution)/shard_map/all_to_all | solution.py:503
  42.8 2.6 %pick.1 = bf16[4,128,512]{2,1,0:T(8,128)(2,1)} custom-call(s32[18]{0:T(128)} %get-tuple-element.40.tab_ref.sc, bf16[16,128,512]{2,1,0:T(8,128)(2,1)} %all-to-all-done.refs_0_.refs_1_.refs_2_.refs_3_.refs_13_.refs_14_.refs_15_.refs_16_, bf16[16,128,512]{2,1,0:T(8,128)(2,1)} %all-to-all-done.refs_0_.refs_1_.refs_2_.refs_3_.refs_13_.refs_14_.refs_15_.refs_16_, ...), custom_call_target="tpu_custom_call" | custom-call | bytes 1048576 | tf_op jit(solution)/shard_map/pick/pallas_call | solution.py:405
  45.4 2.5 %split.2 = (bf16[256,1280]{1,0:T(8,128)(2,1)}, bf16[256,1280]{1,0:T(8,128)(2,1)}, bf16[256,1280]{1,0:T(8,128)(2,1)}) custom-call(s32[1]{0:T(128)} %bitcast.y_ref, bf16[256,4096]{1,0:T(8,128)(2,1)} %refs_0_.7, bf16[256,4096]{1,0:T(8,128)(2,1)} %refs_1_.7, bf16[256,1024]{1,0:T(8,128)(2,1)} %refs_2_.7, bf16[256,1024]{1,0:T(8,128)(2,1)} %refs_3_.7), custom_call_target="tpu_custom_call" | custom-call | bytes 4194304 | tf_op jit(solution)/shard_map/split/pallas_call | solution.py:290
  48.0 3.1 %collective-permute-start.1 = (bf16[256,1280]{1,0:T(8,128)(2,1)}, bf16[256,1280]{1,0:T(8,128)(2,1)}, u32[]{:S(2)}, u32[]{:S(2)}) collective-permute-start(bf16[256,1280]{1,0:T(8,128)(2,1)} %get-tuple-element.37), channel_id=1, source_target_pairs={{0,3},{1,0},{2,1},{3,2},{4,7},{5,4},{6,5},{7,6},{8,11},{9,8},{10,9... | collective-permute-start | bytes 1966088 | tf_op jit(solution)/shard_map/ppermute | solution.py:499
  52.7 24.7 %attn.3 = (bf16[256,1280]{1,0:T(8,128)(2,1)}, bf16[256,1280]{1,0:T(8,128)(2,1)}, bf16[256,1280]{1,0:T(8,128)(2,1)}, bf16[256,1280]{1,0:T(8,128)(2,1)}, bf16[4,128,256]{2,1,0:T(8,128)(2,1)}) custom-call(s32[18]{0:T(128)} %get-tuple-element.40.tab_ref.sc, bf16[256,4096]{1,0:T(8,128)(2,1)} %refs_0_.7, bf16[256,4096]{1,0:T(8,128)(2,1)} %refs_1_.7, ...), custom_call_target="tpu_custom_call" | custom-call | flops 14495514624 | bytes 6291456 | tf_op jit(solution)/shard_map/attn/pallas_call | solution.py:229
  77.5 2.4 %collective-permute-start.11 = (bf16[256,1280]{1,0:T(8,128)(2,1)}, bf16[256,1280]{1,0:T(8,128)(2,1)}, u32[]{:S(2)}, u32[]{:S(2)}) collective-permute-start(bf16[256,1280]{1,0:T(8,128)(2,1)} %get-tuple-element.48), channel_id=1, source_target_pairs={{0,3},{1,0},{2,1},{3,2},{4,7},{5,4},{6,5},{7,6},{8,11},{9,8},{10,9... | collective-permute-start | bytes 1966088 | tf_op jit(solution)/shard_map/ppermute | solution.py:499
  79.9 2.7 %scatter.3 = bf16[16,128,256]{2,1,0:T(8,128)(2,1)} custom-call(s32[18]{0:T(128)} %get-tuple-element.40.tab_ref.sc, bf16[4,128,256]{2,1,0:T(8,128)(2,1)} %get-tuple-element.61.own_ref, bf16[4,128,256]{2,1,0:T(8,128)(2,1)} %collective-permute-done.15.peer_ref), custom_call_target="tpu_custom_call" | custom-call | bytes 2097152 | tf_op jit(solution)/shard_map/scatter/pallas_call | solution.py:439
  82.6 5.0 %all-to-all-start.2 = ((bf16[16,128,256]{2,1,0:T(8,128)(2,1)}), bf16[16,128,256]{2,1,0:T(8,128)(2,1)}, u32[]{:S(2)}, u32[]{:S(2)}) async-start(bf16[16,128,256]{2,1,0:T(8,128)(2,1)} %scatter.3), calls=%async_computation.2 | async-start | bytes 2097152 | tf_op jit(solution)/shard_map/all_to_all | solution.py:503
  87.7 24.8 %attn.2 = (bf16[256,1280]{1,0:T(8,128)(2,1)}, bf16[256,1280]{1,0:T(8,128)(2,1)}, bf16[256,1280]{1,0:T(8,128)(2,1)}, bf16[256,1280]{1,0:T(8,128)(2,1)}, bf16[4,128,256]{2,1,0:T(8,128)(2,1)}) custom-call(s32[18]{0:T(128)} %get-tuple-element.36.sc.tab_ref, bf16[256,4096]{1,0:T(8,128)(2,1)} %refs_0_.7, bf16[256,4096]{1,0:T(8,128)(2,1)} %refs_1_.7, ...), custom_call_target="tpu_custom_call" | custom-call | flops 14495514624 | bytes 6291456 | tf_op jit(solution)/shard_map/attn/pallas_call | solution.py:229
  114.4 2.7 %scatter.2 = bf16[16,128,256]{2,1,0:T(8,128)(2,1)} custom-call(s32[18]{0:T(128)} %get-tuple-element.36.sc.tab_ref, bf16[4,128,256]{2,1,0:T(8,128)(2,1)} %get-tuple-element.60.own_ref, bf16[4,128,256]{2,1,0:T(8,128)(2,1)} %collective-permute-done.14.peer_ref), custom_call_target="tpu_custom_call" | custom-call | bytes 2097152 | tf_op jit(solution)/shard_map/scatter/pallas_call | solution.py:439
  117.1 7.4 %all-to-all-start.1 = ((bf16[16,128,256]{2,1,0:T(8,128)(2,1)}), bf16[16,128,256]{2,1,0:T(8,128)(2,1)}, u32[]{:S(2)}, u32[]{:S(2)}) async-start(bf16[16,128,256]{2,1,0:T(8,128)(2,1)} %scatter.2), calls=%async_computation.1 | async-start | bytes 2097152 | tf_op jit(solution)/shard_map/all_to_all | solution.py:503
  126.7 2.2 %collective-permute-start.5 = (bf16[256,1280]{1,0:T(8,128)(2,1)}, bf16[256,1280]{1,0:T(8,128)(2,1)}, u32[]{:S(2)}, u32[]{:S(2)}) collective-permute-start(bf16[256,1280]{1,0:T(8,128)(2,1)} %get-tuple-element.41), channel_id=1, source_target_pairs={{0,3},{1,0},{2,1},{3,2},{4,7},{5,4},{6,5},{7,6},{8,11},{9,8},{10,9... | collective-permute-start | bytes 1966088 | tf_op jit(solution)/shard_map/ppermute | solution.py:499
  128.9 2.7 %collective-permute-start.7 = (bf16[256,1280]{1,0:T(8,128)(2,1)}, bf16[256,1280]{1,0:T(8,128)(2,1)}, u32[]{:S(2)}, u32[]{:S(2)}) collective-permute-start(bf16[256,1280]{1,0:T(8,128)(2,1)} %get-tuple-element.43), channel_id=1, source_target_pairs={{0,2},{1,3},{2,0},{3,1},{4,6},{5,7},{6,4},{7,5},{8,10},{9,11},{10,... | collective-permute-start | bytes 1966088 | tf_op jit(solution)/shard_map/ppermute | solution.py:499
  131.6 12.4 %collective-permute-done.12.refs_2_ = bf16[256,1280]{1,0:T(8,128)(2,1)} collective-permute-done((bf16[256,1280]{1,0:T(8,128)(2,1)S(1)}, bf16[256,1280]{1,0:T(8,128)(2,1)}, u32[]{:S(2)}, u32[]{:S(2)}) %collective-permute-start.12) | collective-permute-done | bytes 655392 | tf_op jit(solution)/shard_map/ppermute | solution.py:499
  143.9 12.9 %collective-permute-done.13.refs_3_ = bf16[256,1280]{1,0:T(8,128)(2,1)} collective-permute-done((bf16[256,1280]{1,0:T(8,128)(2,1)S(1)}, bf16[256,1280]{1,0:T(8,128)(2,1)}, u32[]{:S(2)}, u32[]{:S(2)}) %collective-permute-start.13) | collective-permute-done | bytes 655392 | tf_op jit(solution)/shard_map/ppermute | solution.py:499
  156.8 3.0 %place.2 = (bf16[256,4096]{1,0:T(8,128)(2,1)}, bf16[256,4096]{1,0:T(8,128)(2,1)}, bf16[256,1024]{1,0:T(8,128)(2,1)}, bf16[256,1024]{1,0:T(8,128)(2,1)}) custom-call(s32[1]{0:T(128)} %bitcast.y_ref, bf16[256,1280]{1,0:T(8,128)(2,1)} %get-tuple-element.47.refs_0_, bf16[256,1280]{1,0:T(8,128)(2,1)} %collective-permute-done.11.refs_1_, ...), custom_call_target="tpu_custom_call" | custom-call | bytes 5242880 | tf_op jit(solution)/shard_map/place/pallas_call | solution.py:337
  159.8 12.1 %collective-permute-done.6.refs_1_ = bf16[256,1280]{1,0:T(8,128)(2,1)} collective-permute-done((bf16[256,1280]{1,0:T(8,128)(2,1)}, bf16[256,1280]{1,0:T(8,128)(2,1)}, u32[]{:S(2)}, u32[]{:S(2)}) %collective-permute-start.6) | collective-permute-done | bytes 655392 | tf_op jit(solution)/shard_map/ppermute | solution.py:499
  171.9 13.0 %collective-permute-done.7.refs_2_ = bf16[256,1280]{1,0:T(8,128)(2,1)} collective-permute-done((bf16[256,1280]{1,0:T(8,128)(2,1)}, bf16[256,1280]{1,0:T(8,128)(2,1)}, u32[]{:S(2)}, u32[]{:S(2)}) %collective-permute-start.7) | collective-permute-done | bytes 655392 | tf_op jit(solution)/shard_map/ppermute | solution.py:499
  184.9 2.5 %place.3 = (bf16[256,4096]{1,0:T(8,128)(2,1)}, bf16[256,4096]{1,0:T(8,128)(2,1)}, bf16[256,1024]{1,0:T(8,128)(2,1)}, bf16[256,1024]{1,0:T(8,128)(2,1)}) custom-call(s32[1]{0:T(128)} %bitcast.y_ref, bf16[256,1280]{1,0:T(8,128)(2,1)} %collective-permute-done.5.refs_0_, ...), custom_call_target="tpu_custom_call", output_to_operand_aliasing={{0}: (4, {}), {1}: (5, {}), {2}: (6, {}), {3}: (7, {})} | custom-call | bytes 5242880 | tf_op jit(solution)/shard_map/place/pallas_call | solution.py:337
  187.4 2.0 %total.2 = (bf16[128,256]{1,0:T(8,128)(2,1)}, bf16[128,256]{1,0:T(8,128)(2,1)}) custom-call(bf16[16,128,256]{2,1,0:T(8,128)(2,1)} %all-to-all-done.2.parts_ref), custom_call_target="tpu_custom_call" | custom-call | bytes 1048576 | tf_op jit(solution)/shard_map/total/pallas_call | solution.py:466
  (36 shorter events, 11.3 us)
Async XLA Ops:
  2.9 8.7 %copy-start = (s32[1,4]{1,0:T(1,128)S(1)}, s32[1,4]{1,0:T(1,128)}, u32[]{:S(2)}) copy-start(s32[1,4]{1,0:T(1,128)} %param.14) | copy-start | bytes 52
  2.9 39.9 %all-to-all-start = ((bf16[16,128,512]{2,1,0:T(8,128)(2,1)}), bf16[16,128,512]{2,1,0:T(8,128)(2,1)}, u32[]{:S(2)}, u32[]{:S(2)}) async-start(bf16[16,128,512]{2,1,0:T(8,128)(2,1)} %spread.1), calls=%async_computation | async-start | bytes 4194304 | tf_op jit(solution)/shard_map/all_to_all | solution.py:503
  11.7 7.2 %collective-permute-start = (s32[5]{0:T(128)S(1)}, s32[5]{0:T(128)S(1)}, u32[]{:S(2)}, u32[]{:S(2)}) collective-permute-start(s32[5]{0:T(128)S(1)} %pad_add_fusion), channel_id=1, source_target_pairs={{0,4},{4,0},{1,5},{5,1},{2,6},{6,2},{3,7},{7,3},{8,12},{12,8},{9,1... | collective-permute-start | bytes 68 | tf_op jit(solution)/shard_map/ppermute | solution.py:507
  14.2 36.8 %collective-permute-start.8 = (bf16[256,1280]{1,0:T(8,128)(2,1)}, bf16[256,1280]{1,0:T(8,128)(2,1)}, u32[]{:S(2)}, u32[]{:S(2)}) collective-permute-start(bf16[256,1280]{1,0:T(8,128)(2,1)} %get-tuple-element.44), channel_id=1, source_target_pairs={{0,3},{1,0},{2,1},{3,2},{4,7},{5,4},{6,5},{7,6},{8,11},{9,8},{10,9... | collective-permute-start | bytes 1966088 | tf_op jit(solution)/shard_map/ppermute | solution.py:499
  17.3 34.4 %collective-permute-start.9 = (bf16[256,1280]{1,0:T(8,128)(2,1)}, bf16[256,1280]{1,0:T(8,128)(2,1)}, u32[]{:S(2)}, u32[]{:S(2)}) collective-permute-start(bf16[256,1280]{1,0:T(8,128)(2,1)} %get-tuple-element.45), channel_id=1, source_target_pairs={{0,2},{1,3},{2,0},{3,1},{4,6},{5,7},{6,4},{7,5},{8,10},{9,11},{10,... | collective-permute-start | bytes 1966088 | tf_op jit(solution)/shard_map/ppermute | solution.py:499
  17.9 34.7 %collective-permute-start.10 = (bf16[256,1280]{1,0:T(8,128)(2,1)}, bf16[256,1280]{1,0:T(8,128)(2,1)}, u32[]{:S(2)}, u32[]{:S(2)}) collective-permute-start(bf16[256,1280]{1,0:T(8,128)(2,1)} %get-tuple-element.46), channel_id=1, source_target_pairs={{0,1},{1,2},{2,3},{3,0},{4,5},{5,6},{6,7},{7,4},{8,9},{9,10},{10,1... | collective-permute-start | bytes 1966088 | tf_op jit(solution)/shard_map/ppermute | solution.py:499
  45.4 7.2 %collective-permute-start.4 = (bf16[4,128,512]{2,1,0:T(8,128)(2,1)}, bf16[4,128,512]{2,1,0:T(8,128)(2,1)}, u32[]{:S(2)}, u32[]{:S(2)}) collective-permute-start(bf16[4,128,512]{2,1,0:T(8,128)(2,1)} %pick.1), channel_id=1, source_target_pairs={{0,4},{4,0},{1,5},{5,1},{2,6},{6,2},{3,7},{7,3},{8,12},{12,8},{9,1... | collective-permute-start | bytes 1572872 | tf_op jit(solution)/shard_map/ppermute | solution.py:507
  48.0 39.7 %collective-permute-start.1 = (bf16[256,1280]{1,0:T(8,128)(2,1)}, bf16[256,1280]{1,0:T(8,128)(2,1)}, u32[]{:S(2)}, u32[]{:S(2)}) collective-permute-start(bf16[256,1280]{1,0:T(8,128)(2,1)} %get-tuple-element.37), channel_id=1, source_target_pairs={{0,3},{1,0},{2,1},{3,2},{4,7},{5,4},{6,5},{7,6},{8,11},{9,8},{10,9... | collective-permute-start | bytes 1966088 | tf_op jit(solution)/shard_map/ppermute | solution.py:499
  51.0 36.6 %collective-permute-start.2 = (bf16[256,1280]{1,0:T(8,128)(2,1)}, bf16[256,1280]{1,0:T(8,128)(2,1)}, u32[]{:S(2)}, u32[]{:S(2)}) collective-permute-start(bf16[256,1280]{1,0:T(8,128)(2,1)} %get-tuple-element.38), channel_id=1, source_target_pairs={{0,2},{1,3},{2,0},{3,1},{4,6},{5,7},{6,4},{7,5},{8,10},{9,11},{10,... | collective-permute-start | bytes 1966088 | tf_op jit(solution)/shard_map/ppermute | solution.py:499
  51.7 36.0 %collective-permute-start.3 = (bf16[256,1280]{1,0:T(8,128)(2,1)}, bf16[256,1280]{1,0:T(8,128)(2,1)}, u32[]{:S(2)}, u32[]{:S(2)}) collective-permute-start(bf16[256,1280]{1,0:T(8,128)(2,1)} %get-tuple-element.39), channel_id=1, source_target_pairs={{0,1},{1,2},{2,3},{3,0},{4,5},{5,6},{6,7},{7,4},{8,9},{9,10},{10,1... | collective-permute-start | bytes 1966088 | tf_op jit(solution)/shard_map/ppermute | solution.py:499
  77.4 2.5 %collective-permute-start.15 = (bf16[4,128,256]{2,1,0:T(8,128)(2,1)}, bf16[4,128,256]{2,1,0:T(8,128)(2,1)}, u32[]{:S(2)}, u32[]{:S(2)}) collective-permute-start(bf16[4,128,256]{2,1,0:T(8,128)(2,1)} %get-tuple-element.61.own_ref), channel_id=1, source_target_pairs={{0,4},{4,0},{1,5},{5,1},{2,6},{6,2},{3,7},{7,3},{8,12},{12,8},{9,1... | collective-permute-start | bytes 786440 | tf_op jit(solution)/shard_map/ppermute | solution.py:507
  77.5 51.4 %collective-permute-start.11 = (bf16[256,1280]{1,0:T(8,128)(2,1)}, bf16[256,1280]{1,0:T(8,128)(2,1)}, u32[]{:S(2)}, u32[]{:S(2)}) collective-permute-start(bf16[256,1280]{1,0:T(8,128)(2,1)} %get-tuple-element.48), channel_id=1, source_target_pairs={{0,3},{1,0},{2,1},{3,2},{4,7},{5,4},{6,5},{7,6},{8,11},{9,8},{10,9... | collective-permute-start | bytes 1966088 | tf_op jit(solution)/shard_map/ppermute | solution.py:499
  82.6 34.5 %all-to-all-start.2 = ((bf16[16,128,256]{2,1,0:T(8,128)(2,1)}), bf16[16,128,256]{2,1,0:T(8,128)(2,1)}, u32[]{:S(2)}, u32[]{:S(2)}) async-start(bf16[16,128,256]{2,1,0:T(8,128)(2,1)} %scatter.3), calls=%async_computation.2 | async-start | bytes 2097152 | tf_op jit(solution)/shard_map/all_to_all | solution.py:503
  112.4 2.0 %collective-permute-start.14 = (bf16[4,128,256]{2,1,0:T(8,128)(2,1)}, bf16[4,128,256]{2,1,0:T(8,128)(2,1)}, u32[]{:S(2)}, u32[]{:S(2)}) collective-permute-start(bf16[4,128,256]{2,1,0:T(8,128)(2,1)} %get-tuple-element.60.own_ref), channel_id=1, source_target_pairs={{0,4},{4,0},{1,5},{5,1},{2,6},{6,2},{3,7},{7,3},{8,12},{12,8},{9,1... | collective-permute-start | bytes 786440 | tf_op jit(solution)/shard_map/ppermute | solution.py:507
  117.1 7.5 %copy-start.2 = (bf16[256,1280]{1,0:T(8,128)(2,1)S(1)}, bf16[256,1280]{1,0:T(8,128)(2,1)}, u32[]{:S(2)}) copy-start(bf16[256,1280]{1,0:T(8,128)(2,1)} %get-tuple-element.49) | copy-start | bytes 1966084
  117.1 8.5 %copy-start.1 = (bf16[256,1280]{1,0:T(8,128)(2,1)S(1)}, bf16[256,1280]{1,0:T(8,128)(2,1)}, u32[]{:S(2)}) copy-start(bf16[256,1280]{1,0:T(8,128)(2,1)} %get-tuple-element.50) | copy-start | bytes 1966084
  117.1 72.2 %all-to-all-start.1 = ((bf16[16,128,256]{2,1,0:T(8,128)(2,1)}), bf16[16,128,256]{2,1,0:T(8,128)(2,1)}, u32[]{:S(2)}, u32[]{:S(2)}) async-start(bf16[16,128,256]{2,1,0:T(8,128)(2,1)} %scatter.2), calls=%async_computation.1 | async-start | bytes 2097152 | tf_op jit(solution)/shard_map/all_to_all | solution.py:503
  124.6 19.3 %collective-permute-start.12 = (bf16[256,1280]{1,0:T(8,128)(2,1)S(1)}, bf16[256,1280]{1,0:T(8,128)(2,1)}, u32[]{:S(2)}, u32[]{:S(2)}) collective-permute-start(bf16[256,1280]{1,0:T(8,128)(2,1)S(1)} %copy-done.2), channel_id=1, source_target_pairs={{0,2},{1,3},{2,0},{3,1},{4,6},{5,7},{6,4},{7,5},{8,10},{9,11},{10,... | collective-permute-start | bytes 1966088 | tf_op jit(solution)/shard_map/ppermute | solution.py:499
  125.7 31.2 %collective-permute-start.13 = (bf16[256,1280]{1,0:T(8,128)(2,1)S(1)}, bf16[256,1280]{1,0:T(8,128)(2,1)}, u32[]{:S(2)}, u32[]{:S(2)}) collective-permute-start(bf16[256,1280]{1,0:T(8,128)(2,1)S(1)} %copy-done.1), channel_id=1, source_target_pairs={{0,1},{1,2},{2,3},{3,0},{4,5},{5,6},{6,7},{7,4},{8,9},{9,10},{10,1... | collective-permute-start | bytes 1966088 | tf_op jit(solution)/shard_map/ppermute | solution.py:499
  126.7 33.2 %collective-permute-start.5 = (bf16[256,1280]{1,0:T(8,128)(2,1)}, bf16[256,1280]{1,0:T(8,128)(2,1)}, u32[]{:S(2)}, u32[]{:S(2)}) collective-permute-start(bf16[256,1280]{1,0:T(8,128)(2,1)} %get-tuple-element.41), channel_id=1, source_target_pairs={{0,3},{1,0},{2,1},{3,2},{4,7},{5,4},{6,5},{7,6},{8,11},{9,8},{10,9... | collective-permute-start | bytes 1966088 | tf_op jit(solution)/shard_map/ppermute | solution.py:499
  128.9 43.0 %collective-permute-start.6 = (bf16[256,1280]{1,0:T(8,128)(2,1)}, bf16[256,1280]{1,0:T(8,128)(2,1)}, u32[]{:S(2)}, u32[]{:S(2)}) collective-permute-start(bf16[256,1280]{1,0:T(8,128)(2,1)} %get-tuple-element.42), channel_id=1, source_target_pairs={{0,1},{1,2},{2,3},{3,0},{4,5},{5,6},{6,7},{7,4},{8,9},{9,10},{10,1... | collective-permute-start | bytes 1966088 | tf_op jit(solution)/shard_map/ppermute | solution.py:499
  128.9 56.0 %collective-permute-start.7 = (bf16[256,1280]{1,0:T(8,128)(2,1)}, bf16[256,1280]{1,0:T(8,128)(2,1)}, u32[]{:S(2)}, u32[]{:S(2)}) collective-permute-start(bf16[256,1280]{1,0:T(8,128)(2,1)} %get-tuple-element.43), channel_id=1, source_target_pairs={{0,2},{1,3},{2,0},{3,1},{4,6},{5,7},{6,4},{7,5},{8,10},{9,11},{10,... | collective-permute-start | bytes 1966088 | tf_op jit(solution)/shard_map/ppermute | solution.py:499
